TPU v7x, 256 devices: a whole 4x4x8 slice. The times are simulated.
256 devices in a mesh: grp: 4 (over z_hi), gx: 16 (over z_lo, y, core), gy: 4 (over x).
Axes of the slice: x: 4, y: 4, z: 8 (z_hi: 4, z_lo: 2; z = z_hi * 2 + z_lo), core: 2. Of those that a mesh axis runs over, the one named last changes fastest.
Arguments:
- states: bfloat16 [12, 256, 64, 512], P(None, 'gx', 'gy', 'grp'), may hold values from 0 to 1
- membrane: float32 [256, 64, 512], P('gx', 'gy', 'grp'), may hold values from -3 to 3
- phi_heart: float32 [256, 64, 512], P('gx', 'gy', 'grp'), may hold values from -3 to 3
- ion_params: float32 [5, 12], replicated, may hold values from -1.5 to 20, as said below
- torso_phi: float32 [256, 128, 512], P('gx', 'gy', 'grp'), may hold values from -3 to 3
- tissue_scale: float32 [256, 128, 512], P('gx', 'gy', 'grp'), may hold values from 0.5 to 2
- labels: int32 [256, 128, 512], P('gx', 'gy', 'grp'), may hold values from 0 to 3
- cond_table: float32 [4], replicated, may hold values from 0.1 to 2
- send_node: int32 [4, 16, 4, 64, 512], P('grp', 'gx', 'gy'), may hold values from 0 to 8191
- send_count: int32 [4, 16, 4, 64], P('grp', 'gx', 'gy'), may hold values from 64 to 512, as said below
- recv_voxel: int32 [4, 16, 4, 64, 512], P('grp', 'gx', 'gy'), may hold values from 0 to 16383
- recv_count: int32 [4, 16, 4, 64], P('grp', 'gx', 'gy'), may hold values from 64 to 512, as said below
Outputs:
- new_membrane: float32 [256, 64, 512], P('gx', 'gy', 'grp')
- heart_phi: float32 [256, 64, 512], P('gx', 'gy', 'grp')
- torso_out: float32 [256, 128, 512], P('gx', 'gy', 'grp')
Inputs may be any that keep to these rules, and one draw needn't show every extreme that they name: `ion_params`: rows are midpoints in -1 to 1, slopes in 0.1 to 0.5, relaxation rates in 0.5 to 20, conductances in 0.1 to 0.6 and reversal potentials in -1.5 to 1.5, one column per state. send_count[g, i, j, p] is the number of live slots, from the first on, of the patch that device (g, i, j) sends to peer p of its slab; every device sends exactly 512 to one peer. recv_count[g, i, j, s] equals send_count of peer s of slab g for peer i * 4 + j; every device receives exactly 512 from one peer.
All inputs are finite; a program needn't handle non-finite values.
Results may differ from a plain program's by a relative error of at most 0.0003.
Values sent between devices are 32-bit elements; how exact they have to be, the bound alone decides.
No kernel may reach another device: no remote copies, remote signals or barrier semaphores. Data moves between devices by JAX's collectives and lax.ppermute only.
A program may use at most 128 MiB of HBM per device.

v0:
```python
import functools

import jax
import jax.numpy as jnp
from jax import lax
from jax.experimental import pallas as pl
from jax.experimental.pallas import tpu as pltpu
from jax.sharding import PartitionSpec as P


LABELS = 4
SWEEPS_H = 3
SWEEPS_T = 4
W = 4
LANES = 128

time_step = 0.1
intra_cond = 0.25
extra_cond = 0.5
penalty = 2.0
cheb_low = 0.1
cheb_high = 2.0
VMEM_LIMIT = 24 << 20
VMEM_WHOLE = 60 * 1024 * 1024


def cheb_coeffs(sweeps):
    centre = 0.5 * (cheb_high + cheb_low)
    half_width = 0.5 * (cheb_high - cheb_low)
    scaled = centre / half_width
    coeffs = [(0.0, 1.0 / centre)]
    rho_old = 1.0 / scaled
    for _ in range(1, sweeps):
        rho_new = 1.0 / (2.0 * scaled - rho_old)
        coeffs.append((rho_new * rho_old, 2.0 * rho_new / half_width))
        rho_old = rho_new
    return coeffs


def f32(*shape):
    return jax.ShapeDtypeStruct(shape, jnp.float32)


def call(body, outs, n_in, scratch=(), smem=(), after=(), whole=False):
    spaces = [pltpu.SMEM if i in smem else pltpu.VMEM for i in range(n_in)] + [pl.ANY] * len(after)

    def run(*refs):
        body(*refs[:n_in], *refs[n_in + len(after) :])

    made = pl.pallas_call(
        run,
        out_shape=outs,
        in_specs=[pl.BlockSpec(memory_space=space) for space in spaces],
        out_specs=jax.tree.map(lambda _: pl.BlockSpec(memory_space=pltpu.VMEM), outs),
        scratch_shapes=list(scratch),
        compiler_params=pltpu.CompilerParams(vmem_limit_bytes=VMEM_WHOLE if whole else VMEM_LIMIT),
    )

    def placed(*args):
        return made(*args, *after)

    return placed


def loop(first, last, body, unroll=2):
    def step(i, carry):
        for u in range(unroll):
            body(i * unroll + u + first)
        return carry

    lax.fori_loop(0, (last - first + 1) // unroll, step, 0)


def lane_iota(rows):
    return lax.broadcasted_iota(jnp.int32, (rows, LANES), 1)


def z_faces(values, zlo, zhi):
    for number, value in enumerate(values):
        turned = value.T
        zlo[W * number : W * (number + 1), :] = turned[:W]
        zhi[W * number : W * (number + 1), :] = turned[LANES - W :]


def lane_pack(slices):
    rows = slices[0].shape[0]
    lane = lane_iota(rows)
    packed = jnp.zeros((rows, LANES), jnp.float32)
    for x, item in enumerate(slices):
        spot = (lane >= 2 * W * x) & (lane < 2 * W * (x + 1))
        packed = jnp.where(spot, pltpu.roll(item, (2 * W * x + W) % LANES, 1), packed)
    return packed


def lane_unpack(packed, x):
    lane = lane_iota(packed.shape[0])
    moved = pltpu.roll(packed, (2 * LANES - (2 * W * x + W)) % LANES, 1)
    return jnp.where((lane < W) | (lane >= LANES - W), moved, 0.0)


def edges(place):
    j, g, ny, nz, rows = place[0], place[1], place[2], place[3], place[4]
    return (j > 0, (j + 1) * rows < ny), (g > 0, (g + 1) * LANES < nz)


def y_part(f0, f1, rl, rr, h0, h1, ylo, yhi, near):
    X, Y, _ = f0.shape
    for number, h in enumerate((h0, h1)):
        part = slice(W * number, W * (number + 1))
        left = jnp.where(near[0], rl[part, :], 0.0)
        right = jnp.where(near[1], rr[part, :], 0.0)
        rows = jnp.concatenate([left, right], 0).T
        wide = jnp.concatenate([rows, jnp.zeros((X * Y, LANES - 2 * W), jnp.float32)], 1)
        h[...] = pltpu.roll(wide, LANES - W, 1).reshape(X, Y, LANES)
    for out, part in ((ylo, slice(0, W)), (yhi, slice(Y - W, Y))):
        out[0:X] = jnp.concatenate([f0[:, part, :], f1[:, part, :]], 1)
        out[X] = lane_pack([jnp.concatenate([h0[x, part], h1[x, part]], 0) for x in range(X)])


def fill(E, f0, f1, h0, h1, ryl, ryr, near):
    X, Y, _ = f0.shape
    for number, (f, h) in enumerate(((f0, h0), (f1, h1))):
        part = slice(W * number, W * (number + 1))
        right = jnp.where(near[1], ryr[:, part], 0.0)
        left = jnp.where(near[0], ryl[:, part], 0.0)
        both = jnp.concatenate([right, left], 1)
        E[2 * number, :, 0:Y] = f[...]
        E[2 * number, :, Y:] = both[0:X]
        E[2 * number + 1, :, 0:Y] = h[...]
        for x in range(X):
            E[2 * number + 1, x, Y:] = lane_unpack(both[X], x)


def x_face(E, start, out):
    for number in range(2):
        base = (W + 1) * number
        out[base : base + W] = E[2 * number, start : start + W]
        out[base + W] = lane_pack([E[2 * number + 1, start + x] for x in range(W)])


def y_body(groups, place, *refs):
    fields, rest = refs[: 2 * groups], refs[2 * groups :]
    rl, rr, halos, ylo, yhi = rest[0], rest[1], rest[2:-2], rest[-2], rest[-1]
    near = edges(place)[1]
    col = row = 0
    for k in range(groups):
        f0, f1 = fields[2 * k : 2 * k + 2]
        X, Y, _ = f0.shape
        cols, rows = pl.ds(col, X * Y), pl.ds(row, X + 1)
        y_part(
            f0, f1, rl.at[:, cols], rr.at[:, cols], halos[2 * k], halos[2 * k + 1],
            ylo.at[rows], yhi.at[rows], near,
        )
        col, row = col + X * Y, row + X + 1


def heart_x_body(place, f0, f1, h0, h1, ryl, ryr, E, high):
    X = f0.shape[0]
    rows = pl.ds(0, X + 1)
    fill(E, f0, f1, h0, h1, ryl.at[rows], ryr.at[rows], edges(place)[0])
    x_face(E, X - W, high)


def torso_x_body(place, heart, f0, f1, h0, h1, ryl, ryr, E, high, low):
    X = f0.shape[0]
    rows = pl.ds(heart.shape[1] + 1, X + 1)
    fill(E, f0, f1, h0, h1, ryl.at[rows], ryr.at[rows], edges(place)[0])
    x_face(E, X - W, high)
    x_face(heart, 0, low.at[:, pl.ds(0, heart.shape[2])])
    x_face(E, 0, low.at[:, pl.ds(heart.shape[2], E.shape[2])])


def right_x_body(place, f0, f1, h0, h1, ryl, ryr, E, low):
    fill(E, f0, f1, h0, h1, ryl, ryr, edges(place)[0])
    x_face(E, 0, low)


def from_next(value, axis):
    count = lax.axis_size(axis)
    return lax.ppermute(value, axis, [((i + 1) % count, i) for i in range(count)])


def from_last(value, axis):
    count = lax.axis_size(axis)
    return lax.ppermute(value, axis, [(i, (i + 1) % count) for i in range(count)])


def swap(value):
    return lax.all_to_all(value, ("gx", "gy"), split_axis=0, concat_axis=0, tiled=True)


def two_stages(place, groups, zlo, zhi):
    count = len(groups)
    fields = [f for group in groups for f in group]
    rr, rl = from_next(zlo, "grp"), from_last(zhi, "grp")
    tall = f32(sum(group[0].shape[0] + 1 for group in groups), 2 * W, LANES)
    *halos, ylo, yhi = call(
        functools.partial(y_body, count),
        tuple(f32(*f.shape) for f in fields) + (tall, tall),
        3 + len(fields), smem=(0,),
    )(place, *fields, rl, rr)
    return halos, from_last(yhi, "gy"), from_next(ylo, "gy")


def wide_of(X, Y):
    return f32(4, X, Y + 2 * W, LANES)


def face_of(rows):
    return f32(2 * (W + 1), rows + 2 * W, LANES)


def assemble(M, H, number, E, rxl, rxr):
    X = E.shape[1]
    base = (W + 1) * number
    M[0:X] = E[2 * number]
    H[0:X] = E[2 * number + 1]
    top = M.shape[0] - 2 * W
    for start, source in ((top, rxr), (top + W, rxl)):
        if source is None:
            continue
        M[start : start + W] = source[base : base + W]
        for x in range(W):
            H[start + x] = lane_unpack(source[base + W], x)


def y_next(v):
    return pltpu.roll(v, v.shape[0] - 1, 0)


def y_last(v):
    return pltpu.roll(v, 1, 0)


def z_next(m, h):
    end = lane_iota(m.shape[0]) == LANES - 1
    rm, rh = pltpu.roll(m, LANES - 1, 1), pltpu.roll(h, LANES - 1, 1)
    return jnp.where(end, rh, rm), jnp.where(end, rm, rh)


def z_last(m, h):
    end = lane_iota(m.shape[0]) == 0
    rm, rh = pltpu.roll(m, 1, 1), pltpu.roll(h, 1, 1)
    return jnp.where(end, rh, rm), jnp.where(end, rm, rh)


def wrapped(x, count):
    return jnp.where(x >= count, x - count, jnp.where(x < 0, x + count, x))


def around(M, H, x, count):
    xn, xl = wrapped(x + 1, count), wrapped(x - 1, count)
    m, h = M[x], H[x]
    zn, zl = z_next(m, h), z_last(m, h)
    sm = M[xn] + M[xl] + y_next(m) + y_last(m) + zn[0] + zl[0]
    sh = H[xn] + H[xl] + y_next(h) + y_last(h) + zn[1] + zl[1]
    return m, h, sm, sh


def gather_rows(table, index, store):
    rows_n = table.shape[0]

    def tile(i, carry):
        top = pl.multiple_of(i * 8, 8)
        for j in range(index.shape[1] // LANES):
            spot = (pl.ds(top, 8), slice(j * LANES, (j + 1) * LANES))
            where = index[spot[0], spot[1]]
            cols, rows = where & (LANES - 1), where >> 7
            total = jnp.zeros((8, LANES), jnp.float32)
            for r in range(rows_n):
                line = jnp.broadcast_to(table[r : r + 1, :], (8, LANES))
                got = jnp.take_along_axis(line, cols, axis=1, mode="promise_in_bounds")
                total = jnp.where(rows == r, got, total)
            store(spot, where, total)
        return carry

    lax.fori_loop(0, index.shape[0] // 8, tile, 0)


def scatter_rows(values, index, rows_n, total, unroll):
    cap = index.shape[1]
    total[...] = jnp.zeros_like(total)

    def hot(count, key, weight):
        same = lax.broadcasted_iota(jnp.int32, (count, cap), 0) == key
        return jnp.where(same, weight, 0.0).astype(jnp.bfloat16)

    def one(s):
        where = index[pl.ds(s, 1), :]
        rows, cols = where >> 7, where & (LANES - 1)
        if values is None:
            left = hot(rows_n, rows, 1.0)
        else:
            value = values[pl.ds(s, 1), :]
            high = value.astype(jnp.bfloat16).astype(jnp.float32)
            left = jnp.concatenate([hot(rows_n, rows, high), hot(rows_n, rows, value - high)], 0)
        return lax.dot_general(
            left, hot(LANES, cols, 1.0), (((1,), (1,)), ((), ())), preferred_element_type=jnp.float32
        )

    def step(i, carry):
        part = one(i * unroll)
        for u in range(1, unroll):
            part = part + one(i * unroll + u)
        total[...] += part
        return carry

    lax.fori_loop(0, index.shape[0] // unroll, step, 0)


def start_body(table, m, p, phi, scale, labels, cond, zlo, zhi):
    X, Y, _ = m.shape
    TX, TY, _ = phi.shape
    cols, more = pl.ds(0, X * Y), pl.ds(X * Y, TX * TY)
    z_faces(
        [m[...].reshape(X * Y, LANES), p[...].reshape(X * Y, LANES)], zlo.at[:, cols], zhi.at[:, cols]
    )
    picked = jnp.zeros(labels.shape, jnp.float32)
    for number in range(LABELS):
        picked = jnp.where(labels[...] == number, table[number], picked)
    value = scale[...] * picked
    cond[...] = value
    z_faces(
        [phi[...].reshape(TX * TY, LANES), value.reshape(TX * TY, LANES)], zlo.at[:, more], zhi.at[:, more]
    )


def weight_body(index, weight, total):
    scatter_rows(None, index, total.shape[0], total, 8)
    weight[...] = (penalty * total[...]).reshape(weight.shape)


def heart_tiles(place, Y):
    j, g = place[0], place[1]
    row = lax.broadcasted_iota(jnp.int32, (Y + 2 * W, LANES), 0)
    lane = lane_iota(Y + 2 * W)
    yg = j * Y + jnp.where(row >= Y + W, row - Y - 2 * W, row)
    tiles = []
    for zl in (lane, jnp.where(lane >= LANES // 2, lane - LANES, lane + LANES)):
        zg = g * LANES + zl
        ny, nz = place[2], place[3]
        one = lambda cond: cond.astype(jnp.float32)
        inside = one((yg >= 0) & (yg < ny) & (zg >= 0) & (zg < nz))
        diag = 2.0 + one(yg + 1 < ny) + one(yg - 1 >= 0) + one(zg + 1 < nz) + one(zg - 1 >= 0)
        tiles.append((diag, inside / diag, inside))
    return tiles


def heart_surface_body(place, E, rxl, index, sent, table, mM, mH, uM, uH, wM, wH, vM, vH, fM, fH):
    S, Y = E.shape[1] // 4, E.shape[2] - 2 * W
    for number, (M, H) in enumerate(((mM, mH), (uM, uH))):
        base = (W + 1) * number
        M[0:W] = rxl[base : base + W]
        for x in range(W):
            H[x] = lane_unpack(rxl[base + W], x)
        M[W:] = E[2 * number, 0 : 2 * W]
        H[W:] = E[2 * number + 1, 0 : 2 * W]
    count = 3 * W
    (_, qm, im), (_, qh, ih) = heart_tiles(place, Y)
    ratio = intra_cond / (intra_cond + extra_cond)
    old, new = (uM, uH), (wM, wH)
    for number, (carry_coef, resid_coef) in enumerate(cheb_coeffs(SWEEPS_H)):
        reach = SWEEPS_H - 1 - number
        for x in range(W - reach, W + S + reach):
            a, b, sa, sb = around(old[0], old[1], x, count)
            if number == 0:
                c, d, sc, sd = around(mM, mH, x, count)
                fa, fb = -ratio * (c * im - sc * qm), -ratio * (d * ih - sd * qh)
                fM[x], fH[x] = fa, fb
            else:
                fa, fb = fM[x], fH[x]
            va = resid_coef * (fa + sa * qm - a)
            vb = resid_coef * (fb + sb * qh - b)
            if number > 0:
                va, vb = carry_coef * vM[x] + va, carry_coef * vH[x] + vb
            if number < SWEEPS_H - 1:
                vM[x], vH[x] = va, vb
                new[0][x], new[1][x] = a + va, b + vb
            else:
                table[(x - W) * Y : (x - W + 1) * Y, :] = (a + va)[0:Y]
        old, new = new, old

    def store(spot, where, value):
        sent[spot[0], spot[1]] = value

    gather_rows(table, index, store)


def heart_body(
    place, current, E, rxl, rxr, phi_out, new_out, mM, mH, uM, uH, wM, wH, vM, vH, fM, fH
):
    X, Y, _ = phi_out.shape
    count = X + 2 * W
    near = pl.ds(0, Y + 2 * W)
    assemble(mM, mH, 0, E, rxl, rxr.at[:, near])
    assemble(uM, uH, 1, E, rxl, rxr.at[:, near])
    (dm, qm, im), (_, qh, ih) = heart_tiles(place, Y)
    ratio = intra_cond / (intra_cond + extra_cond)
    old, new = (uM, uH), (wM, wH)
    for number, (carry_coef, resid_coef) in enumerate(cheb_coeffs(SWEEPS_H)):

        def sweep(x, old=old, new=new, cc=carry_coef, rc=resid_coef, number=number):
            x = wrapped(x, count)
            a, b, sa, sb = around(old[0], old[1], x, count)
            if number == 0:
                c, d, sc, sd = around(mM, mH, x, count)
                fa, fb = -ratio * (c * im - sc * qm), -ratio * (d * ih - sd * qh)
                fM[x], fH[x] = fa, fb
            else:
                fa, fb = fM[x], fH[x]
            va = rc * (fa + sa * qm - a)
            vb = rc * (fb + sb * qh - b)
            if number > 0:
                va, vb = cc * vM[x] + va, cc * vH[x] + vb
            vM[x], vH[x] = va, vb
            new[0][x], new[1][x] = a + va, b + vb

        reach = SWEEPS_H - number
        loop(-reach, X - 1 + reach, sweep)
        old, new = new, old
    phi_out[...] = old[0][0:X, 0:Y]

    def finish(x):
        a, _, sa, _ = around(mM, mH, x, count)
        c, _, sc, _ = around(old[0], old[1], x, count)
        lap = dm * (a + c) - (sa + sc)
        new_out[x] = (a - time_step * intra_cond * lap)[0:Y] - time_step * current[x]

    loop(0, X - 1, finish)


def right_body(arrived, index, weight, right, zlo, zhi, total):
    rows = index_rows = weight.shape[0] * weight.shape[1]
    scatter_rows(arrived, index, rows, total, 8)
    value = penalty * (total[0:rows] + total[rows : 2 * rows])
    right[...] = value.reshape(right.shape)
    z_faces([value, weight[...].reshape(index_rows, LANES)], zlo, zhi)


def faces_body(E, rxl, rxr, F, cM, cH):
    uM, uH, fxM, fxH, fyM, fyH, fzM, fzH, dM, dH = (F.at[k] for k in range(10))
    X, rows = E.shape[1], E.shape[2]
    count = X + 2 * W
    far = pl.ds(rxr.shape[1] - rows, rows)
    assemble(uM, uH, 0, E, rxl, rxr.at[:, far])
    assemble(cM, cH, 1, E, rxl, rxr.at[:, far])

    def harmonic(a, b):
        total = a + b
        return jnp.where(total > 0.0, 2.0 * a * b / jnp.where(total > 0.0, total, 1.0), 0.0)

    def prepare(x):
        xn = wrapped(x + 1, count)
        a, b = cM[x], cH[x]
        za, zb = z_next(a, b)
        fxM[x], fxH[x] = harmonic(a, cM[xn]), harmonic(b, cH[xn])
        fyM[x], fyH[x] = harmonic(a, y_next(a)), harmonic(b, y_next(b))
        fzM[x], fzH[x] = harmonic(a, za), harmonic(b, zb)

    loop(0, count - 1, prepare)

    def total(x):
        xl = wrapped(x - 1, count)
        za, zb = z_last(fzM[x], fzH[x])
        dM[x] = fxM[x] + fxM[xl] + fyM[x] + y_last(fyM[x]) + fzM[x] + za
        dH[x] = fxH[x] + fxH[xl] + fyH[x] + y_last(fyH[x]) + fzH[x] + zb

    loop(0, count - 1, total)


def reciprocal(value):
    return jnp.where(value > 0.0, 1.0 / jnp.where(value > 0.0, value, 1.0), 0.0)


def flow(m, h, nM, nH, lM, lH, fxM, fxH, gxM, gxH, fy, gy, fz, gz):
    zn = z_next(m, h)
    zl = z_last(fz * m, gz * h)
    sm = fxM * nM + gxM * lM + fy * y_next(m) + y_last(fy * m)
    sh = fxH * nH + gxH * lH + gy * y_next(h) + y_last(gy * h)
    return sm + fz * zn[0] + zl[0], sh + gz * zn[1] + zl[1]


def torso_surface_body(
    R, arrived, index, F, surface, returned, aM, aH, bM, bH, vM, vH, iM, iH
):
    uM, uH, fxM, fxH, fyM, fyH, fzM, fzH, dM, dH = (F.at[k] for k in range(10))
    S, Y, _ = surface.shape
    count = F.shape[1]
    old, new = None, (aM, aH)
    for number, (carry_coef, resid_coef) in enumerate(cheb_coeffs(SWEEPS_T)):
        reach = SWEEPS_T - 1 - number

        def value(x, tile, old=old):
            return (uM, uH)[tile][x % count] if old is None else old[tile][x + W]

        for x in range(-reach, S + reach):
            at, last = x % count, (x - 1) % count
            m, h = value(x, 0), value(x, 1)
            sm, sh = flow(
                m, h, value(x + 1, 0), value(x + 1, 1), value(x - 1, 0), value(x - 1, 1),
                fxM[at], fxH[at], fxM[last], fxH[last], fyM[at], fyH[at], fzM[at], fzH[at],
            )
            inside = 0 <= x < S
            if number == 0:
                wm, wh = dM[at], dH[at]
                if inside:
                    wm, wh = wm + R[2, x], wh + R[3, x]
                wm, wh = reciprocal(wm), reciprocal(wh)
                iM[x + W], iH[x + W] = wm, wh
            else:
                wm, wh = iM[x + W], iH[x + W]
            if inside:
                sm, sh = sm + R[0, x], sh + R[1, x]
            va, vb = resid_coef * (sm * wm - m), resid_coef * (sh * wh - h)
            if number > 0:
                va, vb = carry_coef * vM[x + W] + va, carry_coef * vH[x + W] + vb
            if number < SWEEPS_T - 1:
                vM[x + W], vH[x + W] = va, vb
                new[0][x + W], new[1][x + W] = m + va, h + vb
            else:
                surface[x] = (m + va)[0:Y]
        old, new = new, ((bM, bH) if number == 0 else old)
    table = surface[...].reshape(S * Y, LANES)

    def store(spot, where, value):
        returned[spot[0], spot[1]] = jnp.where(
            where >= 0, penalty * (arrived[spot[0], spot[1]] - value), 0.0
        )

    gather_rows(table, index, store)


def torso_body(
    surface, R, rxr, F, torso_out, aM, aH, bM, bH, vM, vH, rM, rH, iM, iH
):
    uM, uH, fxM, fxH, fyM, fyH, fzM, fzH, dM, dH = (F.at[k] for k in range(10))
    X, Y = torso_out.shape[0], torso_out.shape[1]
    S = surface.shape[0]
    for ref in (rM, rH, iM, iH):
        ref[S:X] = jnp.zeros((X - S,) + ref.shape[1:], jnp.float32)
    assemble(rM, rH, 0, R, None, rxr)
    assemble(iM, iH, 1, R, None, rxr)

    old, new = (uM, uH), (aM, aH)
    for number, (carry_coef, resid_coef) in enumerate(cheb_coeffs(SWEEPS_T)):

        def sweep(x, old=old, new=new, cc=carry_coef, rc=resid_coef, number=number):
            xn, xl = x + 1, x - 1
            m, h = old[0][x], old[1][x]
            if number == 0:
                iM[x], iH[x] = reciprocal(dM[x] + iM[x]), reciprocal(dH[x] + iH[x])
            sm, sh = flow(
                m, h, old[0][xn], old[1][xn], old[0][xl], old[1][xl],
                fxM[x], fxH[x], fxM[xl], fxH[xl], fyM[x], fyH[x], fzM[x], fzH[x],
            )
            va = rc * ((rM[x] + sm) * iM[x] - m)
            vb = rc * ((rH[x] + sh) * iH[x] - h)
            if number > 0:
                va, vb = cc * vM[x] + va, cc * vH[x] + vb
            vM[x], vH[x] = va, vb
            new[0][x], new[1][x] = m + va, h + vb

        reach = SWEEPS_T - 1 - number
        loop(S - reach, X - 1 + reach, sweep)
        old, new = new, ((bM, bH) if number == 0 else old)
    torso_out[0:S] = surface[...]
    torso_out[S:X] = old[0][S:X, 0:Y]


def final_body(place, back, index, phi, out, total):
    X, Y, _ = phi.shape
    rows = X // 4 * Y
    scatter_rows(back, index, rows, total, 8)
    flux = (total[0:rows] + total[rows : 2 * rows]).reshape(X // 4, Y, LANES)
    (dm, _, _), _ = heart_tiles(place, Y)
    out[X // 4 :] = phi[X // 4 :]
    scale = (1.0 / ((intra_cond + extra_cond) * dm))[0:Y]
    for x in range(X // 4):
        out[x] = phi[x] - flux[x] * scale


def ionic_current(states, membrane, ion_params):
    params_col = ion_params[:, :, None, None, None]
    gate_vals = states.astype(jnp.float32)
    voltage = membrane[None]
    steady = jax.nn.sigmoid((voltage - params_col[0]) / params_col[1])
    gate_vals = steady + (gate_vals - steady) * jnp.exp(-time_step * params_col[2])
    return jnp.sum(params_col[3] * gate_vals * (voltage - params_col[4]), axis=0)


def per_device(
    states, membrane, phi_heart, ion_params, torso_phi, tissue_scale, labels, cond_table,
    send_node, send_count, recv_voxel, recv_count,
):
    X, Y, _ = membrane.shape
    TX, TY, _ = torso_phi.shape
    peers = lax.axis_size("gx") * lax.axis_size("gy")
    cap = send_node.shape[-1]
    place = jnp.stack([
        lax.axis_index("gy"), lax.axis_index("grp"),
        jnp.int32(Y * lax.axis_size("gy")), jnp.int32(LANES * lax.axis_size("grp")), jnp.int32(Y),
    ])
    slots = jnp.arange(cap, dtype=jnp.int32)[None, :]
    send_index = jnp.where(slots < send_count.reshape(peers, 1), send_node.reshape(peers, cap), -1)
    recv_index = jnp.where(slots < recv_count.reshape(peers, 1), recv_voxel.reshape(peers, cap), -1)

    S = TX // 4
    wide = f32(2 * W, X * Y + TX * TY)
    cond, zlo, zhi = call(
        start_body, (f32(TX, TY, LANES), wide, wide), 6, smem=(0,), whole=True,
    )(cond_table, membrane, phi_heart, torso_phi, tissue_scale, labels)
    weight = call(
        weight_body, f32(S, TY, LANES), 1, scratch=[pltpu.VMEM((S * TY, LANES), jnp.float32)]
    )(recv_index)
    current = ionic_current(states, membrane, ion_params)

    heart, torso = (membrane, phi_heart), (torso_phi, cond)
    halos, ryl, ryr = two_stages(place, (heart, torso), zlo, zhi)
    heart_wide, high = call(
        heart_x_body, (wide_of(X, Y), face_of(Y)), 7, smem=(0,)
    )(place, *heart, *halos[:2], ryl, ryr)
    hxl = from_last(high, "gx")
    torso_wide, high, low = call(
        torso_x_body, (wide_of(TX, TY), face_of(TY), face_of(Y + 2 * W + TY)), 8,
        smem=(0,), after=(hxl,),
    )(place, heart_wide, *torso, *halos[2:], ryl, ryr)
    txl, xr = from_last(high, "gx"), from_next(low, "gx")

    thin = pltpu.VMEM((3 * W, Y + 2 * W, LANES), jnp.float32)
    sent = call(
        heart_surface_body, f32(peers, cap), 4,
        scratch=[pltpu.VMEM((X // 4 * Y, LANES), jnp.float32)] + [thin] * 10, smem=(0,),
    )(place, heart_wide, hxl, send_index)
    arrived = swap(sent)

    ext = pltpu.VMEM((X + 2 * W, Y + 2 * W, LANES), jnp.float32)
    phi_new, new_membrane = call(
        heart_body, (f32(X, Y, LANES), f32(X, Y, LANES)), 5,
        scratch=[ext] * 10, smem=(0,), whole=True,
    )(place, current, heart_wide, hxl, xr)
    right, rzlo, rzhi = call(
        right_body,
        (f32(S, TY, LANES), f32(2 * W, S * TY), f32(2 * W, S * TY)),
        3, scratch=[pltpu.VMEM((2 * S * TY, LANES), jnp.float32)],
    )(arrived, recv_index, weight)
    text = (TX + 2 * W, TY + 2 * W, LANES)
    big = pltpu.VMEM(text, jnp.float32)
    faces = call(faces_body, f32(10, *text), 3, scratch=[big] * 2)(torso_wide, txl, xr)
    halos, ryl, ryr = two_stages(place, ((right, weight),), rzlo, rzhi)
    right_wide, low = call(
        right_x_body, (wide_of(S, TY), face_of(TY)), 7, smem=(0,)
    )(place, right, weight, *halos, ryl, ryr)
    rxr = from_next(low, "gx")
    flat = pltpu.VMEM((3 * W, TY + 2 * W, LANES), jnp.float32)
    surface, returned = call(
        torso_surface_body, (f32(S, TY, LANES), f32(peers, cap)), 4,
        scratch=[flat] * 8,
    )(right_wide, arrived, recv_index, faces)
    back = swap(returned)
    torso_out = call(
        torso_body, f32(TX, TY, LANES), 4, scratch=[big] * 10, whole=True,
    )(surface, right_wide, rxr, faces)
    heart_phi = call(
        final_body, f32(X, Y, LANES), 4,
        scratch=[pltpu.VMEM((2 * X // 4 * Y, LANES), jnp.float32)], smem=(0,),
    )(place, back, send_index, phi_new)
    return (new_membrane, heart_phi, torso_out)


def solution(mesh):
    placed = (
        P(None, "gx", "gy", "grp"),
        P("gx", "gy", "grp"),
        P("gx", "gy", "grp"),
        P(),
        P("gx", "gy", "grp"),
        P("gx", "gy", "grp"),
        P("gx", "gy", "grp"),
        P(),
        P("grp", "gx", "gy", None, None),
        P("grp", "gx", "gy", None),
        P("grp", "gx", "gy", None, None),
        P("grp", "gx", "gy", None),
    )
    return jax.shard_map(
        per_device,
        mesh=mesh,
        in_specs=placed,
        out_specs=(P("gx", "gy", "grp"), P("gx", "gy", "grp"), P("gx", "gy", "grp")),
        check_vma=False,
    )
```

profile of v0, /device:TPU:1, one launch (start us, length us, event | category | flops | bytes accessed | tf_op | source)
XLA Modules:
  0.0 114.3 jit_solution(4323879867081023547)
XLA Ops:
  0.7 2.2 %shard_map.139 = (f32[16,32,128]{2,1,0:T(8,128)}, f32[8,768]{1,0:T(8,128)}, f32[8,768]{1,0:T(8,128)}) custom-call(f32[4]{0:T(128)} %refs_0_.1, f32[16,16,128]{2,1,0:T(8,128)} %refs_1_.5, f32[16,16,128]{2,1,0:T(8,128)} %refs_2_.6, f32[16,32,128]{2,1,0:T(8,128)} %refs_2_.7, f32[16,32,128]{2,1,0:T(8,128)} %refs_4_.1, s32[16,32,128]{2,1,0:T(8,128)} %refs_5_.1), custom_call_target="tpu_custom_call" | custom-call | tf_op jit(solution)/shard_map/pallas_call | solution.py:60
  2.8 3.8 %collective-permute-start = (f32[8,768]{1,0:T(8,128)}, f32[8,768]{1,0:T(8,128)S(1)}, u32[]{:S(2)}, u32[]{:S(2)}) collective-permute-start(f32[8,768]{1,0:T(8,128)} %get-tuple-element.31), channel_id=1, source_target_pairs={{0,64},{64,128},{128,192},{192,0},{1,65},{65,129},{129,193},{193,1... | collective-permute-start | bytes 73736 | tf_op jit(solution)/shard_map/ppermute | solution.py:185
  6.6 3.0 %collective-permute-start.1 = (f32[8,768]{1,0:T(8,128)}, f32[8,768]{1,0:T(8,128)S(1)}, u32[]{:S(2)}, u32[]{:S(2)}) collective-permute-start(f32[8,768]{1,0:T(8,128)} %get-tuple-element.32), channel_id=1, source_target_pairs={{64,0},{128,64},{192,128},{0,192},{65,1},{129,65},{193,129},{1,193... | collective-permute-start | bytes 73736 | tf_op jit(solution)/shard_map/ppermute | solution.py:180
  9.7 0.1 stack.11.refs_0_
  9.7 1.3 %collective-permute-done.refs_5_ = f32[8,768]{1,0:T(8,128)S(1)} collective-permute-done((f32[8,768]{1,0:T(8,128)}, f32[8,768]{1,0:T(8,128)S(1)}, u32[]{:S(2)}, u32[]{:S(2)}) %collective-permute-start) | collective-permute-done | bytes 24608 | tf_op jit(solution)/shard_map/ppermute | solution.py:185
  11.1 1.2 %collective-permute-done.1.refs_6_ = f32[8,768]{1,0:T(8,128)S(1)} collective-permute-done((f32[8,768]{1,0:T(8,128)}, f32[8,768]{1,0:T(8,128)S(1)}, u32[]{:S(2)}, u32[]{:S(2)}) %collective-permute-start.1) | collective-permute-done | bytes 24608 | tf_op jit(solution)/shard_map/ppermute | solution.py:180
  12.2 0.9 copy-done.2
  13.2 0.9 copy-done.4
  14.1 0.9 copy-done.8
  15.0 0.9 copy-done.10
  16.0 1.2 %shard_map.140 = (f32[16,16,128]{2,1,0:T(8,128)S(1)}, f32[16,16,128]{2,1,0:T(8,128)S(1)}, f32[16,32,128]{2,1,0:T(8,128)S(1)}, f32[16,32,128]{2,1,0:T(8,128)S(1)}...) custom-call(s32[5]{0:T(128)S(1)} %stack.11.refs_0_, f32[16,16,128]{2,1,0:T(8,128)S(1)} %copy-done.4, ...), custom_call_target="tpu_custom_call" | custom-call | tf_op jit(solution)/shard_map/pallas_call | solution.py:60
  17.2 1.3 %collective-permute-start.2 = (f32[34,8,128]{2,1,0:T(8,128)S(1)}, f32[34,8,128]{2,1,0:T(8,128)S(1)}, u32[]{:S(2)}, u32[]{:S(2)}) collective-permute-start(f32[34,8,128]{2,1,0:T(8,128)S(1)} %get-tuple-element.35), channel_id=1, source_target_pairs={{0,1},{1,2},{2,3},{3,0},{4,5},{5,6},{6,7},{7,4},{8,9},{9,10},{10,1... | collective-permute-start | bytes 417800 | tf_op jit(solution)/shard_map/ppermute | solution.py:185
  18.5 1.5 %collective-permute-start.3 = (f32[34,8,128]{2,1,0:T(8,128)S(1)}, f32[34,8,128]{2,1,0:T(8,128)S(1)}, u32[]{:S(2)}, u32[]{:S(2)}) collective-permute-start(f32[34,8,128]{2,1,0:T(8,128)S(1)} %get-tuple-element.36), channel_id=1, source_target_pairs={{1,0},{2,1},{3,2},{0,3},{5,4},{6,5},{7,6},{4,7},{9,8},{10,9},{11,1... | collective-permute-start | bytes 417800 | tf_op jit(solution)/shard_map/ppermute | solution.py:180
  20.0 2.4 %collective-permute-done.2.refs_5_.refs_6_ = f32[34,8,128]{2,1,0:T(8,128)S(1)} collective-permute-done((f32[34,8,128]{2,1,0:T(8,128)S(1)}, f32[34,8,128]{2,1,0:T(8,128)S(1)}, u32[]{:S(2)}, u32[]{:S(2)}) %collective-permute-start.2) | collective-permute-done | bytes 139296 | tf_op jit(solution)/shard_map/ppermute | solution.py:185
  22.4 0.7 shard_map.141
  23.1 4.5 %collective-permute-start.4 = (f32[10,24,128]{2,1,0:T(8,128)S(1)}, f32[10,24,128]{2,1,0:T(8,128)S(1)}, u32[]{:S(2)}, u32[]{:S(2)}) collective-permute-start(f32[10,24,128]{2,1,0:T(8,128)S(1)} %get-tuple-element.38), channel_id=1, source_target_pairs={{0,4},{4,8},{8,12},{12,16},{16,20},{20,24},{24,28},{28,32},{32,36}... | collective-permute-start | bytes 368648 | tf_op jit(solution)/shard_map/ppermute | solution.py:185
  27.6 0.1 bitcast_select_fusion.1.refs_3_.refs_2_
  27.7 1.8 %collective-permute-done.4.refs_8_.refs_3_.refs_2_ = f32[10,24,128]{2,1,0:T(8,128)S(1)} collective-permute-done((f32[10,24,128]{2,1,0:T(8,128)S(1)}, f32[10,24,128]{2,1,0:T(8,128)S(1)}, u32[]{:S(2)}, u32[]{:S(2)}) %collective-permute-start.4) | collective-permute-done | bytes 122912 | tf_op jit(solution)/shard_map/ppermute | solution.py:185
  29.5 3.8 %shard_map.144 = f32[64,512]{1,0:T(8,128)S(1)} custom-call(s32[5]{0:T(128)S(1)} %stack.11.refs_0_, f32[4,16,24,128]{3,2,1,0:T(8,128)S(1)} %get-tuple-element.37.refs_1_.refs_2_, f32[10,24,128]{2,1,0:T(8,128)S(1)} %collective-permute-done.4.refs_8_.refs_3_.refs_2_, s32[64,512]{1,0:T(8,128)S(1)} %bitcast_select_fusion.1.refs_3_.refs_2_), custom_call_target="tpu_custom_call" | custom-call | tf_op jit(solution)/shard_map/pallas_call | solution.py:60
  33.3 0.8 copy.15
  34.1 9.1 %all-to-all-start = ((f32[64,1,512]{2,1,0:T(1,128)}), f32[64,1,512]{2,1,0:T(1,128)S(1)}, u32[]{:S(2)}, u32[]{:S(2)}) async-start(f32[64,1,512]{2,1,0:T(1,128)} %copy.15), calls=%async_computation | async-start | bytes 262144 | tf_op jit(solution)/shard_map/all_to_all | solution.py:189
  43.3 0.9 copy-done.13
  44.2 1.5 %shard_map.142 = (f32[4,16,40,128]{3,2,1,0:T(8,128)S(1)}, f32[10,40,128]{2,1,0:T(8,128)S(1)}, f32[10,64,128]{2,1,0:T(8,128)}) custom-call(s32[5]{0:T(128)S(1)} %stack.11.refs_0_, f32[4,16,24,128]{3,2,1,0:T(8,128)S(1)} %get-tuple-element.37.refs_1_.refs_2_, f32[16,32,128]{2,1,0:T(8,128)S(1)} %copy-done.3, f32[16,32,128]{2,1,0:T(8,128)S(1)} %copy-done.11, ...), custom_call_target="tpu_custom_call" | custom-call | tf_op jit(solution)/shard_map/pallas_call | solution.py:60
  45.7 0.7 copy-done.18
  46.4 0.5 collective-permute-start.5
  46.9 1.0 bitcast_select_fusion.refs_0_.refs_1_.refs_2_
  47.9 3.9 %shard_map.145.refs_2_ = f32[4,32,128]{2,1,0:T(8,128)S(1)} custom-call(s32[64,512]{1,0:T(8,128)S(1)} %bitcast_select_fusion.refs_0_.refs_1_.refs_2_), custom_call_target="tpu_custom_call" | custom-call | tf_op jit(solution)/shard_map/pallas_call | solution.py:60
  51.8 0.0 all-to-all-done
  51.8 7.0 %shard_map.146 = (f32[4,32,128]{2,1,0:T(8,128)S(1)}, f32[8,128]{1,0:T(8,128)S(1)}, f32[8,128]{1,0:T(8,128)S(1)}) custom-call(f32[64,512]{1,0:T(8,128)S(1)} %bitcast.26, s32[64,512]{1,0:T(8,128)S(1)} %bitcast_select_fusion.refs_0_.refs_1_.refs_2_, f32[4,32,128]{2,1,0:T(8,128)S(1)} %shard_map.145.refs_2_), custom_call_target="tpu_custom_call" | custom-call | tf_op jit(solution)/shard_map/pallas_call | solution.py:60
  58.9 3.9 %collective-permute-start.6 = (f32[8,128]{1,0:T(8,128)S(1)}, f32[8,128]{1,0:T(8,128)S(1)}, u32[]{:S(2)}, u32[]{:S(2)}) collective-permute-start(f32[8,128]{1,0:T(8,128)S(1)} %get-tuple-element.44), channel_id=1, source_target_pairs={{0,64},{64,128},{128,192},{192,0},{1,65},{65,129},{129,193},{193,1... | collective-permute-start | bytes 12296 | tf_op jit(solution)/shard_map/ppermute | solution.py:185
  62.8 1.6 %collective-permute-start.10 = (f32[10,40,128]{2,1,0:T(8,128)}, f32[10,40,128]{2,1,0:T(8,128)S(1)}, u32[]{:S(2)}, u32[]{:S(2)}) collective-permute-start(f32[10,40,128]{2,1,0:T(8,128)} %copy-done.18), channel_id=1, source_target_pairs={{0,4},{4,8},{8,12},{12,16},{16,20},{20,24},{24,28},{28,32},{32,36}... | collective-permute-start | bytes 614408 | tf_op jit(solution)/shard_map/ppermute | solution.py:185
  64.4 1.8 %collective-permute-done.7.refs_4_ = f32[8,128]{1,0:T(8,128)S(1)} collective-permute-done((f32[8,128]{1,0:T(8,128)S(1)}, f32[8,128]{1,0:T(8,128)S(1)}, u32[]{:S(2)}, u32[]{:S(2)}) %collective-permute-start.7) | collective-permute-done | bytes 4128 | tf_op jit(solution)/shard_map/ppermute | solution.py:180
  66.1 0.8 shard_map.147
  67.0 1.5 %collective-permute-start.8 = (f32[5,8,128]{2,1,0:T(8,128)S(1)}, f32[5,8,128]{2,1,0:T(8,128)S(1)}, u32[]{:S(2)}, u32[]{:S(2)}) collective-permute-start(f32[5,8,128]{2,1,0:T(8,128)S(1)} %get-tuple-element.48), channel_id=1, source_target_pairs={{0,1},{1,2},{2,3},{3,0},{4,5},{5,6},{6,7},{7,4},{8,9},{9,10},{10,1... | collective-permute-start | bytes 61448 | tf_op jit(solution)/shard_map/ppermute | solution.py:185
  68.5 1.4 %collective-permute-start.9 = (f32[5,8,128]{2,1,0:T(8,128)S(1)}, f32[5,8,128]{2,1,0:T(8,128)S(1)}, u32[]{:S(2)}, u32[]{:S(2)}) collective-permute-start(f32[5,8,128]{2,1,0:T(8,128)S(1)} %get-tuple-element.49), channel_id=1, source_target_pairs={{1,0},{2,1},{3,2},{0,3},{5,4},{6,5},{7,6},{4,7},{9,8},{10,9},{11,1... | collective-permute-start | bytes 61448 | tf_op jit(solution)/shard_map/ppermute | solution.py:180
  69.9 1.2 %collective-permute-done.8.refs_5_ = f32[5,8,128]{2,1,0:T(8,128)S(1)} collective-permute-done((f32[5,8,128]{2,1,0:T(8,128)S(1)}, f32[5,8,128]{2,1,0:T(8,128)S(1)}, u32[]{:S(2)}, u32[]{:S(2)}) %collective-permute-start.8) | collective-permute-done | bytes 20512 | tf_op jit(solution)/shard_map/ppermute | solution.py:185
  71.1 0.1 collective-permute-done.9.refs_6_
  71.2 0.7 shard_map.148
  71.9 6.5 %collective-permute-start.11 = (f32[10,40,128]{2,1,0:T(8,128)S(1)}, f32[10,40,128]{2,1,0:T(8,128)S(1)}, u32[]{:S(2)}, u32[]{:S(2)}) collective-permute-start(f32[10,40,128]{2,1,0:T(8,128)S(1)} %get-tuple-element.56), channel_id=1, source_target_pairs={{4,0},{8,4},{12,8},{16,12},{20,16},{24,20},{28,24},{32,28},{36,32}... | collective-permute-start | bytes 614408 | tf_op jit(solution)/shard_map/ppermute | solution.py:180
  78.4 2.7 %shard_map.149.refs_3_ = f32[10,24,40,128]{3,2,1,0:T(8,128)S(1)} custom-call(f32[4,16,40,128]{3,2,1,0:T(8,128)S(1)} %get-tuple-element.51.refs_0_, f32[10,40,128]{2,1,0:T(8,128)S(1)} %collective-permute-done.10.refs_1_, f32[10,64,128]{2,1,0:T(8,128)S(1)} %collective-permute-done.5.refs_4_.refs_2_), custom_call_target="tpu_custom_call" | custom-call | tf_op jit(solution)/shard_map/pallas_call | solution.py:60
  81.2 5.8 %shard_map.150 = (f32[4,32,128]{2,1,0:T(8,128)S(1)}, f32[64,512]{1,0:T(8,128)S(1)}) custom-call(f32[4,4,40,128]{3,2,1,0:T(8,128)S(1)} %get-tuple-element.50.refs_0_.refs_1_, f32[64,512]{1,0:T(8,128)S(1)} %bitcast.27, s32[64,512]{1,0:T(8,128)S(1)} %bitcast_select_fusion.refs_0_.refs_1_.refs_2_, f32[10,24,40,128]{3,2,1,0:T(8,128)S(1)} %shard_map.149.refs_3_), custom_call_target="tpu_custom_call" | custom-call | tf_op jit(solution)/shard_map/pallas_call | solution.py:60
  87.0 0.8 copy.16
  87.8 5.2 %all-to-all-start.1 = ((f32[64,1,512]{2,1,0:T(1,128)}), f32[64,1,512]{2,1,0:T(1,128)S(1)}, u32[]{:S(2)}, u32[]{:S(2)}) async-start(f32[64,1,512]{2,1,0:T(1,128)} %copy.16), calls=%async_computation.1 | async-start | bytes 262144 | tf_op jit(solution)/shard_map/all_to_all | solution.py:189
  93.0 1.7 %multiply_reduce_fusion.refs_1_ = f32[16,16,128]{2,1,0:T(8,128)} fusion(bf16[12,16,16,128]{3,2,1,0:T(8,128)(2,1)S(1)} %copy-done.19, f32[12]{0:T(128)S(1)} %get-tuple-element.60, f32[12]{0:T(128)S(1)} %get-tuple-element.61, f32[12]{0:T(128)S(1)} %get-tuple-element.58, f32[12]{0:T(128)S(1)} %get-tuple-element.59, f32[16,16,128]{2,1,0:T(8,128)S(1)} %copy-done.5, ...), kind=kLoop, calls=%fused_computation | loop fusion | flops 5079040 | bytes 1048816 | tf_op jit(solution)/shard_map/reduce_sum | solution.py:588
  94.7 6.3 %shard_map.143 = (f32[16,16,128]{2,1,0:T(8,128)}, f32[16,16,128]{2,1,0:T(8,128)}) custom-call(s32[5]{0:T(128)} %copy-done.16, f32[16,16,128]{2,1,0:T(8,128)} %multiply_reduce_fusion.refs_1_, f32[4,16,24,128]{3,2,1,0:T(8,128)} %copy-done.1, f32[10,24,128]{2,1,0:T(8,128)} %copy-done.9, f32[10,64,128]{2,1,0:T(8,128)} %copy-done.6), custom_call_target="tpu_custom_call" | custom-call | tf_op jit(solution)/shard_map/pallas_call | solution.py:60
  101.0 0.7 copy-done.20
  101.6 7.4 %shard_map.152 = f32[16,32,128]{2,1,0:T(8,128)} custom-call(f32[4,32,128]{2,1,0:T(8,128)} %copy-done.15, f32[4,4,40,128]{3,2,1,0:T(8,128)} %copy-done.7, f32[10,40,128]{2,1,0:T(8,128)} %copy-done.20, f32[10,24,40,128]{3,2,1,0:T(8,128)} %copy-done), custom_call_target="tpu_custom_call" | custom-call | tf_op jit(solution)/shard_map/pallas_call | solution.py:60
  109.1 5.2 %shard_map.151 = f32[16,16,128]{2,1,0:T(8,128)} custom-call(s32[5]{0:T(128)S(1)} %copy-done.17, f32[64,512]{1,0:T(8,128)S(1)} %bitcast.28, s32[64,512]{1,0:T(8,128)S(1)} %bitcast_select_fusion.1.refs_3_.refs_2_, f32[16,16,128]{2,1,0:T(8,128)S(1)} %copy-done.14), custom_call_target="tpu_custom_call" | custom-call | tf_op jit(solution)/shard_map/pallas_call | solution.py:60
  (51 shorter events, 0.1 us)
Async XLA Ops:
  0.6 27.0 %copy-start.23 = (s32[1,1,1,64]{3,2,1,0:T(1,128)S(1)}, s32[1,1,1,64]{3,2,1,0:T(1,128)}, u32[]{:S(2)}) copy-start(s32[1,1,1,64]{3,2,1,0:T(1,128)} %param.21) | copy-start | bytes 772
  0.6 27.0 %copy-start.21 = (s32[1,1,1,64,512]{4,3,2,1,0:T(8,128)S(1)}, s32[1,1,1,64,512]{4,3,2,1,0:T(8,128)}, u32[]{:S(2)}) copy-start(s32[1,1,1,64,512]{4,3,2,1,0:T(8,128)} %param.20) | copy-start | bytes 393220
  2.8 8.3 %collective-permute-start = (f32[8,768]{1,0:T(8,128)}, f32[8,768]{1,0:T(8,128)S(1)}, u32[]{:S(2)}, u32[]{:S(2)}) collective-permute-start(f32[8,768]{1,0:T(8,128)} %get-tuple-element.31), channel_id=1, source_target_pairs={{0,64},{64,128},{128,192},{192,0},{1,65},{65,129},{129,193},{193,1... | collective-permute-start | bytes 73736 | tf_op jit(solution)/shard_map/ppermute | solution.py:185
  6.6 5.6 %collective-permute-start.1 = (f32[8,768]{1,0:T(8,128)}, f32[8,768]{1,0:T(8,128)S(1)}, u32[]{:S(2)}, u32[]{:S(2)}) collective-permute-start(f32[8,768]{1,0:T(8,128)} %get-tuple-element.32), channel_id=1, source_target_pairs={{64,0},{128,64},{192,128},{0,192},{65,1},{129,65},{193,129},{1,193... | collective-permute-start | bytes 73736 | tf_op jit(solution)/shard_map/ppermute | solution.py:180
  9.7 61.4 %copy-start.16 = (s32[5]{0:T(128)}, s32[5]{0:T(128)S(1)}, u32[]{:S(2)}) copy-start(s32[5]{0:T(128)S(1)} %stack.11.refs_0_) | copy-start | bytes 64
  12.2 1.0 copy-start.2
  13.2 0.9 copy-start.4
  14.1 0.9 copy-start.8
  15.0 0.9 copy-start.10
  17.2 12.3 %copy-start.12 = (f32[16,32,128]{2,1,0:T(8,128)}, f32[16,32,128]{2,1,0:T(8,128)S(1)}, u32[]{:S(2)}) copy-start(f32[16,32,128]{2,1,0:T(8,128)S(1)} %get-tuple-element.40.refs_5_) | copy-start | bytes 786436
  17.2 26.1 %copy-start.3 = (f32[16,32,128]{2,1,0:T(8,128)S(1)}, f32[16,32,128]{2,1,0:T(8,128)}, u32[]{:S(2)}) copy-start(f32[16,32,128]{2,1,0:T(8,128)} %refs_2_.7) | copy-start | bytes 786436
  17.2 26.1 %copy-start.11 = (f32[16,32,128]{2,1,0:T(8,128)S(1)}, f32[16,32,128]{2,1,0:T(8,128)}, u32[]{:S(2)}) copy-start(f32[16,32,128]{2,1,0:T(8,128)} %get-tuple-element.30.refs_4_.refs_3_) | copy-start | bytes 786436
  17.2 5.2 %collective-permute-start.2 = (f32[34,8,128]{2,1,0:T(8,128)S(1)}, f32[34,8,128]{2,1,0:T(8,128)S(1)}, u32[]{:S(2)}, u32[]{:S(2)}) collective-permute-start(f32[34,8,128]{2,1,0:T(8,128)S(1)} %get-tuple-element.35), channel_id=1, source_target_pairs={{0,1},{1,2},{2,3},{3,0},{4,5},{5,6},{6,7},{7,4},{8,9},{9,10},{10,1... | collective-permute-start | bytes 417800 | tf_op jit(solution)/shard_map/ppermute | solution.py:185
  18.5 3.9 %collective-permute-start.3 = (f32[34,8,128]{2,1,0:T(8,128)S(1)}, f32[34,8,128]{2,1,0:T(8,128)S(1)}, u32[]{:S(2)}, u32[]{:S(2)}) collective-permute-start(f32[34,8,128]{2,1,0:T(8,128)S(1)} %get-tuple-element.36), channel_id=1, source_target_pairs={{1,0},{2,1},{3,2},{0,3},{5,4},{6,5},{7,6},{4,7},{9,8},{10,9},{11,1... | collective-permute-start | bytes 417800 | tf_op jit(solution)/shard_map/ppermute | solution.py:180
  23.1 22.6 %copy-start.1 = (f32[4,16,24,128]{3,2,1,0:T(8,128)}, f32[4,16,24,128]{3,2,1,0:T(8,128)S(1)}, u32[]{:S(2)}) copy-start(f32[4,16,24,128]{3,2,1,0:T(8,128)S(1)} %get-tuple-element.37.refs_1_.refs_2_) | copy-start | bytes 2359300
  23.1 6.4 %collective-permute-start.4 = (f32[10,24,128]{2,1,0:T(8,128)S(1)}, f32[10,24,128]{2,1,0:T(8,128)S(1)}, u32[]{:S(2)}, u32[]{:S(2)}) collective-permute-start(f32[10,24,128]{2,1,0:T(8,128)S(1)} %get-tuple-element.38), channel_id=1, source_target_pairs={{0,4},{4,8},{8,12},{12,16},{16,20},{20,24},{24,28},{28,32},{32,36}... | collective-permute-start | bytes 368648 | tf_op jit(solution)/shard_map/ppermute | solution.py:185
  29.5 16.2 %copy-start.9 = (f32[10,24,128]{2,1,0:T(8,128)}, f32[10,24,128]{2,1,0:T(8,128)S(1)}, u32[]{:S(2)}) copy-start(f32[10,24,128]{2,1,0:T(8,128)S(1)} %collective-permute-done.4.refs_8_.refs_3_.refs_2_) | copy-start | bytes 368644
  34.1 17.7 %all-to-all-start = ((f32[64,1,512]{2,1,0:T(1,128)}), f32[64,1,512]{2,1,0:T(1,128)S(1)}, u32[]{:S(2)}, u32[]{:S(2)}) async-start(f32[64,1,512]{2,1,0:T(1,128)} %copy.15), calls=%async_computation | async-start | bytes 262144 | tf_op jit(solution)/shard_map/all_to_all | solution.py:189
  43.3 1.0 copy-start.13
  44.2 25.7 %copy-start.22 = (f32[5,12]{1,0:T(8,128)S(1)}, f32[5,12]{1,0:T(8,128)}, u32[]{:S(2)}) copy-start(f32[5,12]{1,0:T(8,128)} %param.15) | copy-start | bytes 724
  45.7 0.7 copy-start.18
  46.4 32.0 %collective-permute-start.5 = (f32[10,64,128]{2,1,0:T(8,128)}, f32[10,64,128]{2,1,0:T(8,128)S(1)}, u32[]{:S(2)}, u32[]{:S(2)}) collective-permute-start(f32[10,64,128]{2,1,0:T(8,128)} %get-tuple-element.41), channel_id=1, source_target_pairs={{4,0},{8,4},{12,8},{16,12},{20,16},{24,20},{28,24},{32,28},{36,32}... | collective-permute-start | bytes 983048 | tf_op jit(solution)/shard_map/ppermute | solution.py:180
  58.9 5.5 %collective-permute-start.6 = (f32[8,128]{1,0:T(8,128)S(1)}, f32[8,128]{1,0:T(8,128)S(1)}, u32[]{:S(2)}, u32[]{:S(2)}) collective-permute-start(f32[8,128]{1,0:T(8,128)S(1)} %get-tuple-element.44), channel_id=1, source_target_pairs={{0,64},{64,128},{128,192},{192,0},{1,65},{65,129},{129,193},{193,1... | collective-permute-start | bytes 12296 | tf_op jit(solution)/shard_map/ppermute | solution.py:185
  62.8 3.4 %collective-permute-start.7 = (f32[8,128]{1,0:T(8,128)S(1)}, f32[8,128]{1,0:T(8,128)S(1)}, u32[]{:S(2)}, u32[]{:S(2)}) collective-permute-start(f32[8,128]{1,0:T(8,128)S(1)} %get-tuple-element.45), channel_id=1, source_target_pairs={{64,0},{128,64},{192,128},{0,192},{65,1},{129,65},{193,129},{1,193... | collective-permute-start | bytes 12296 | tf_op jit(solution)/shard_map/ppermute | solution.py:180
  62.8 15.6 %collective-permute-start.10 = (f32[10,40,128]{2,1,0:T(8,128)}, f32[10,40,128]{2,1,0:T(8,128)S(1)}, u32[]{:S(2)}, u32[]{:S(2)}) collective-permute-start(f32[10,40,128]{2,1,0:T(8,128)} %copy-done.18), channel_id=1, source_target_pairs={{0,4},{4,8},{8,12},{12,16},{16,20},{20,24},{24,28},{28,32},{32,36}... | collective-permute-start | bytes 614408 | tf_op jit(solution)/shard_map/ppermute | solution.py:185
  67.0 4.1 %collective-permute-start.8 = (f32[5,8,128]{2,1,0:T(8,128)S(1)}, f32[5,8,128]{2,1,0:T(8,128)S(1)}, u32[]{:S(2)}, u32[]{:S(2)}) collective-permute-start(f32[5,8,128]{2,1,0:T(8,128)S(1)} %get-tuple-element.48), channel_id=1, source_target_pairs={{0,1},{1,2},{2,3},{3,0},{4,5},{5,6},{6,7},{7,4},{8,9},{9,10},{10,1... | collective-permute-start | bytes 61448 | tf_op jit(solution)/shard_map/ppermute | solution.py:185
  68.5 2.6 %collective-permute-start.9 = (f32[5,8,128]{2,1,0:T(8,128)S(1)}, f32[5,8,128]{2,1,0:T(8,128)S(1)}, u32[]{:S(2)}, u32[]{:S(2)}) collective-permute-start(f32[5,8,128]{2,1,0:T(8,128)S(1)} %get-tuple-element.49), channel_id=1, source_target_pairs={{1,0},{2,1},{3,2},{0,3},{5,4},{6,5},{7,6},{4,7},{9,8},{10,9},{11,1... | collective-permute-start | bytes 61448 | tf_op jit(solution)/shard_map/ppermute | solution.py:180
  71.8 9.3 %copy-start.7 = (f32[4,4,40,128]{3,2,1,0:T(8,128)}, f32[4,4,40,128]{3,2,1,0:T(8,128)S(1)}, u32[]{:S(2)}) copy-start(f32[4,4,40,128]{3,2,1,0:T(8,128)S(1)} %get-tuple-element.50.refs_0_.refs_1_) | copy-start | bytes 983044
  71.9 29.1 %collective-permute-start.11 = (f32[10,40,128]{2,1,0:T(8,128)S(1)}, f32[10,40,128]{2,1,0:T(8,128)S(1)}, u32[]{:S(2)}, u32[]{:S(2)}) collective-permute-start(f32[10,40,128]{2,1,0:T(8,128)S(1)} %get-tuple-element.56), channel_id=1, source_target_pairs={{4,0},{8,4},{12,8},{16,12},{20,16},{24,20},{28,24},{32,28},{36,32}... | collective-permute-start | bytes 614408 | tf_op jit(solution)/shard_map/ppermute | solution.py:180
  78.4 2.7 %copy-start.6 = (f32[10,64,128]{2,1,0:T(8,128)}, f32[10,64,128]{2,1,0:T(8,128)S(1)}, u32[]{:S(2)}) copy-start(f32[10,64,128]{2,1,0:T(8,128)S(1)} %collective-permute-done.5.refs_4_.refs_2_) | copy-start | bytes 983044
  81.1 5.9 %copy-start = (f32[10,24,40,128]{3,2,1,0:T(8,128)}, f32[10,24,40,128]{3,2,1,0:T(8,128)S(1)}, u32[]{:S(2)}) copy-start(f32[10,24,40,128]{3,2,1,0:T(8,128)S(1)} %shard_map.149.refs_3_) | copy-start | bytes 14745604
  81.1 11.9 %copy-start.5 = (f32[16,16,128]{2,1,0:T(8,128)S(1)}, f32[16,16,128]{2,1,0:T(8,128)}, u32[]{:S(2)}) copy-start(f32[16,16,128]{2,1,0:T(8,128)} %refs_1_.5) | copy-start | bytes 393220
  81.1 11.9 %copy-start.19 = (bf16[12,16,16,128]{3,2,1,0:T(8,128)(2,1)S(1)}, bf16[12,16,16,128]{3,2,1,0:T(8,128)(2,1)}, u32[]{:S(2)}) copy-start(bf16[12,16,16,128]{3,2,1,0:T(8,128)(2,1)} %param.12) | copy-start | bytes 2359300
  87.0 13.9 %copy-start.15 = (f32[4,32,128]{2,1,0:T(8,128)}, f32[4,32,128]{2,1,0:T(8,128)S(1)}, u32[]{:S(2)}) copy-start(f32[4,32,128]{2,1,0:T(8,128)S(1)} %get-tuple-element.55.refs_0_) | copy-start | bytes 196612
  87.8 21.2 %all-to-all-start.1 = ((f32[64,1,512]{2,1,0:T(1,128)}), f32[64,1,512]{2,1,0:T(1,128)S(1)}, u32[]{:S(2)}, u32[]{:S(2)}) async-start(f32[64,1,512]{2,1,0:T(1,128)} %copy.16), calls=%async_computation.1 | async-start | bytes 262144 | tf_op jit(solution)/shard_map/all_to_all | solution.py:189
  101.0 0.7 copy-start.20
  101.6 7.4 %copy-start.14 = (f32[16,16,128]{2,1,0:T(8,128)S(1)}, f32[16,16,128]{2,1,0:T(8,128)}, u32[]{:S(2)}) copy-start(f32[16,16,128]{2,1,0:T(8,128)} %get-tuple-element.54.refs_3_) | copy-start | bytes 393220
  101.6 7.4 %copy-start.17 = (s32[5]{0:T(128)S(1)}, s32[5]{0:T(128)}, u32[]{:S(2)}) copy-start(s32[5]{0:T(128)} %copy-done.16) | copy-start | bytes 64
where the time goes:
time: 115 us; the launch traced here: 114 us
  Pallas kernels  49.3 us (43%)
  starting transfers between devices  43.8 us (38%)
  waiting for transfers between devices  9.78 us (9%)
  local copies, waits for them, and re-layouts  7.78 us (7%)
  other arithmetic  2.73 us (2%)
    pallas_call x14, Pallas kernels, placed(): return made(*args, *after)  49.3 us
    ppermute x6, starting transfers between devices, from_last(): lax.ppermute(value, axis, [(i, (i + 1) % count) for i in range(count)])  16.6 us
    all_to_all x2, starting transfers between devices, swap(): lax.all_to_all(value, ('gx', 'gy'), split_axis=0, concat_axis=0, tiled=True)  14.3 us
    ppermute x6, starting transfers between devices, from_next(): lax.ppermute(value, axis, [((i + 1) % count, i) for i in range(count)])  12.9 us
    ppermute x6, waiting for transfers between devices, from_last(): lax.ppermute(value, axis, [(i, (i + 1) % count) for i in range(count)])  6.72 us
    unnamed x50, local copies, waits for them, and re-layouts  6.11 us
    ppermute x6, waiting for transfers between devices, from_next(): lax.ppermute(value, axis, [((i + 1) % count, i) for i in range(count)])  3.04 us
  transfers between devices with their start and end apart: 14, of which 7 were waited for; matrix products, arithmetic and copies ran while one was open for 3% of the time, Pallas kernels for 32%

commit v1 on v0

--- a/solution.py
+++ b/solution.py
@@ -41,14 +41,10 @@
     return jax.ShapeDtypeStruct(shape, jnp.float32)
 
 
-def call(body, outs, n_in, scratch=(), smem=(), after=(), whole=False):
-    spaces = [pltpu.SMEM if i in smem else pltpu.VMEM for i in range(n_in)] + [pl.ANY] * len(after)
-
-    def run(*refs):
-        body(*refs[:n_in], *refs[n_in + len(after) :])
-
-    made = pl.pallas_call(
-        run,
+def call(body, outs, n_in, scratch=(), smem=(), left=(), whole=False):
+    spaces = [pltpu.SMEM if i in smem else pl.ANY if i in left else pltpu.VMEM for i in range(n_in)]
+    return pl.pallas_call(
+        body,
         out_shape=outs,
         in_specs=[pl.BlockSpec(memory_space=space) for space in spaces],
         out_specs=jax.tree.map(lambda _: pl.BlockSpec(memory_space=pltpu.VMEM), outs),
@@ -56,19 +52,16 @@
         compiler_params=pltpu.CompilerParams(vmem_limit_bytes=VMEM_WHOLE if whole else VMEM_LIMIT),
     )
 
-    def placed(*args):
-        return made(*args, *after)
-
-    return placed
-
-
-def loop(first, last, body, unroll=2):
+
+def loop(first, last, body, steps=2):
+    unroll = (last - first + 1) // steps
+
     def step(i, carry):
         for u in range(unroll):
             body(i * unroll + u + first)
         return carry
 
-    lax.fori_loop(0, (last - first + 1) // unroll, step, 0)
+    lax.fori_loop(0, steps, step, 0)
 
 
 def lane_iota(rows):
@@ -257,7 +250,7 @@
     return m, h, sm, sh
 
 
-def gather_rows(table, index, store):
+def gather_rows(table, index, out):
     rows_n = table.shape[0]
 
     def tile(i, carry):
@@ -271,41 +264,54 @@
                 line = jnp.broadcast_to(table[r : r + 1, :], (8, LANES))
                 got = jnp.take_along_axis(line, cols, axis=1, mode="promise_in_bounds")
                 total = jnp.where(rows == r, got, total)
-            store(spot, where, total)
+            out[spot[0], 0, spot[1]] = total
         return carry
 
     lax.fori_loop(0, index.shape[0] // 8, tile, 0)
 
 
-def scatter_rows(values, index, rows_n, total, unroll):
+def scatter_rows(value_of, index, rows_n, total, batch):
     cap = index.shape[1]
     total[...] = jnp.zeros_like(total)
-
-    def hot(count, key, weight):
-        same = lax.broadcasted_iota(jnp.int32, (count, cap), 0) == key
-        return jnp.where(same, weight, 0.0).astype(jnp.bfloat16)
+    half = jnp.bfloat16
+
+    def rows_iota(count):
+        return lax.broadcasted_iota(jnp.int32, (count, cap), 0).astype(jnp.float32).astype(half)
+
+    row_ids, col_ids = rows_iota(rows_n), rows_iota(LANES)
+    ones = jnp.ones((1, cap), half)
+
+    def hot(ids, key, weight):
+        key = jnp.broadcast_to(key.astype(jnp.float32).astype(half), ids.shape)
+        return jnp.where(ids == key, jnp.broadcast_to(weight, ids.shape), jnp.zeros((), half))
 
     def one(s):
         where = index[pl.ds(s, 1), :]
         rows, cols = where >> 7, where & (LANES - 1)
-        if values is None:
-            left = hot(rows_n, rows, 1.0)
+        if value_of is None:
+            left = hot(row_ids, rows, ones)
         else:
-            value = values[pl.ds(s, 1), :]
-            high = value.astype(jnp.bfloat16).astype(jnp.float32)
-            left = jnp.concatenate([hot(rows_n, rows, high), hot(rows_n, rows, value - high)], 0)
-        return lax.dot_general(
-            left, hot(LANES, cols, 1.0), (((1,), (1,)), ((), ())), preferred_element_type=jnp.float32
-        )
+            value = value_of(s)
+            high = value.astype(half)
+            low = (value - high.astype(jnp.float32)).astype(half)
+            left = jnp.concatenate([hot(row_ids, rows, high), hot(row_ids, rows, low)], 0)
+        return left, hot(col_ids, cols, ones)
 
     def step(i, carry):
-        part = one(i * unroll)
-        for u in range(1, unroll):
-            part = part + one(i * unroll + u)
+        part = None
+        for b in range(batch):
+            sides = [one(i * (8 * batch) + 8 * b + k) for k in range(8)]
+            product = lax.dot_general(
+                jnp.concatenate([side[0] for side in sides], 1),
+                jnp.concatenate([side[1] for side in sides], 1),
+                (((1,), (1,)), ((), ())),
+                preferred_element_type=jnp.float32,
+            )
+            part = product if part is None else part + product
         total[...] += part
         return carry
 
-    lax.fori_loop(0, index.shape[0] // unroll, step, 0)
+    lax.fori_loop(0, index.shape[0] // (8 * batch), step, 0)
 
 
 def start_body(table, m, p, phi, scale, labels, cond, zlo, zhi):
@@ -326,7 +332,7 @@
 
 
 def weight_body(index, weight, total):
-    scatter_rows(None, index, total.shape[0], total, 8)
+    scatter_rows(None, index, total.shape[0], total, 2)
     weight[...] = (penalty * total[...]).reshape(weight.shape)
 
 
@@ -380,10 +386,7 @@
                 table[(x - W) * Y : (x - W + 1) * Y, :] = (a + va)[0:Y]
         old, new = new, old
 
-    def store(spot, where, value):
-        sent[spot[0], spot[1]] = value
-
-    gather_rows(table, index, store)
+    gather_rows(table, index, sent)
 
 
 def heart_body(
@@ -431,13 +434,13 @@
 
 def right_body(arrived, index, weight, right, zlo, zhi, total):
     rows = index_rows = weight.shape[0] * weight.shape[1]
-    scatter_rows(arrived, index, rows, total, 8)
+    scatter_rows(lambda s: arrived[pl.ds(s, 1), 0, :], index, rows, total, 4)
     value = penalty * (total[0:rows] + total[rows : 2 * rows])
     right[...] = value.reshape(right.shape)
     z_faces([value, weight[...].reshape(index_rows, LANES)], zlo, zhi)
 
 
-def faces_body(E, rxl, rxr, F, cM, cH):
+def faces_body(E, rxl, rxr, F, middle, cM, cH, aM, aH, bM, bH, vM, vH, iM, iH):
     uM, uH, fxM, fxH, fyM, fyH, fzM, fzH, dM, dH = (F.at[k] for k in range(10))
     X, rows = E.shape[1], E.shape[2]
     count = X + 2 * W
@@ -457,7 +460,7 @@
         fyM[x], fyH[x] = harmonic(a, y_next(a)), harmonic(b, y_next(b))
         fzM[x], fzH[x] = harmonic(a, za), harmonic(b, zb)
 
-    loop(0, count - 1, prepare)
+    loop(0, count - 1, prepare, 4)
 
     def total(x):
         xl = wrapped(x - 1, count)
@@ -465,7 +468,32 @@
         dM[x] = fxM[x] + fxM[xl] + fyM[x] + y_last(fyM[x]) + fzM[x] + za
         dH[x] = fxH[x] + fxH[xl] + fyH[x] + y_last(fyH[x]) + fzH[x] + zb
 
-    loop(0, count - 1, total)
+    loop(0, count - 1, total, 4)
+
+    first = 2 * W - 1
+    last = first + middle.shape[0] - 1
+    old, new = (uM, uH), (aM, aH)
+    for number, (carry_coef, resid_coef) in enumerate(cheb_coeffs(SWEEPS_T)):
+
+        def sweep(x, old=old, new=new, cc=carry_coef, rc=resid_coef, number=number):
+            xn, xl = x + 1, x - 1
+            m, h = old[0][x], old[1][x]
+            if number == 0:
+                iM[x], iH[x] = reciprocal(dM[x]), reciprocal(dH[x])
+            sm, sh = flow(
+                m, h, old[0][xn], old[1][xn], old[0][xl], old[1][xl],
+                fxM[x], fxH[x], fxM[xl], fxH[xl], fyM[x], fyH[x], fzM[x], fzH[x],
+            )
+            va, vb = rc * (sm * iM[x] - m), rc * (sh * iH[x] - h)
+            if number > 0:
+                va, vb = cc * vM[x] + va, cc * vH[x] + vb
+            vM[x], vH[x] = va, vb
+            new[0][x], new[1][x] = m + va, h + vb
+
+        reach = SWEEPS_T - 1 - number
+        loop(first - reach, last + reach, sweep)
+        old, new = new, ((bM, bH) if number == 0 else old)
+    middle[...] = old[0][first : last + 1, 0 : middle.shape[1]]
 
 
 def reciprocal(value):
@@ -481,10 +509,11 @@
 
 
 def torso_surface_body(
-    R, arrived, index, F, surface, returned, aM, aH, bM, bH, vM, vH, iM, iH
+    R, index, F, surface, returned, aM, aH, bM, bH, vM, vH, iM, iH
 ):
     uM, uH, fxM, fxH, fyM, fyH, fzM, fzH, dM, dH = (F.at[k] for k in range(10))
-    S, Y, _ = surface.shape
+    S, Y = R.shape[1], surface.shape[1]
+    N = surface.shape[0]
     count = F.shape[1]
     old, new = None, (aM, aH)
     for number, (carry_coef, resid_coef) in enumerate(cheb_coeffs(SWEEPS_T)):
@@ -493,7 +522,7 @@
         def value(x, tile, old=old):
             return (uM, uH)[tile][x % count] if old is None else old[tile][x + W]
 
-        for x in range(-reach, S + reach):
+        for x in range(-reach, N + reach):
             at, last = x % count, (x - 1) % count
             m, h = value(x, 0), value(x, 1)
             sm, sh = flow(
@@ -520,57 +549,63 @@
             else:
                 surface[x] = (m + va)[0:Y]
         old, new = new, ((bM, bH) if number == 0 else old)
-    table = surface[...].reshape(S * Y, LANES)
-
-    def store(spot, where, value):
-        returned[spot[0], spot[1]] = jnp.where(
-            where >= 0, penalty * (arrived[spot[0], spot[1]] - value), 0.0
-        )
-
-    gather_rows(table, index, store)
+    table = surface[0:S].reshape(S * Y, LANES)
+
+    gather_rows(table, index, returned)
 
 
 def torso_body(
-    surface, R, rxr, F, torso_out, aM, aH, bM, bH, vM, vH, rM, rH, iM, iH
+    surface, middle, rxr, F, torso_out, G, aM, aH, bM, bH, vM, vH, iM, iH, sem
 ):
-    uM, uH, fxM, fxH, fyM, fyH, fzM, fzH, dM, dH = (F.at[k] for k in range(10))
-    X, Y = torso_out.shape[0], torso_out.shape[1]
-    S = surface.shape[0]
-    for ref in (rM, rH, iM, iH):
-        ref[S:X] = jnp.zeros((X - S,) + ref.shape[1:], jnp.float32)
-    assemble(rM, rH, 0, R, None, rxr)
-    assemble(iM, iH, 1, R, None, rxr)
-
+    N, M = surface.shape[0], middle.shape[0]
+    X, Y, _ = torso_out.shape
+    first = N + M - W
+    copy = pltpu.make_async_copy(F.at[:, pl.ds(first, G.shape[1])], G, sem)
+    copy.start()
+    torso_out[0:N] = surface[...]
+    torso_out[N : N + M] = middle[...]
+    copy.wait()
+    uM, uH, fxM, fxH, fyM, fyH, fzM, fzH, dM, dH = (G.at[k] for k in range(10))
     old, new = (uM, uH), (aM, aH)
     for number, (carry_coef, resid_coef) in enumerate(cheb_coeffs(SWEEPS_T)):
-
-        def sweep(x, old=old, new=new, cc=carry_coef, rc=resid_coef, number=number):
-            xn, xl = x + 1, x - 1
-            m, h = old[0][x], old[1][x]
+        reach = SWEEPS_T - 1 - number
+        for x in range(N + M - reach, X + reach):
+            at = x - first
+            m, h = old[0][at], old[1][at]
+            sm, sh = flow(
+                m, h, old[0][at + 1], old[1][at + 1], old[0][at - 1], old[1][at - 1],
+                fxM[at], fxH[at], fxM[at - 1], fxH[at - 1], fyM[at], fyH[at], fzM[at], fzH[at],
+            )
+            beyond = x - X
             if number == 0:
-                iM[x], iH[x] = reciprocal(dM[x] + iM[x]), reciprocal(dH[x] + iH[x])
-            sm, sh = flow(
-                m, h, old[0][xn], old[1][xn], old[0][xl], old[1][xl],
-                fxM[x], fxH[x], fxM[xl], fxH[xl], fyM[x], fyH[x], fzM[x], fzH[x],
-            )
-            va = rc * ((rM[x] + sm) * iM[x] - m)
-            vb = rc * ((rH[x] + sh) * iH[x] - h)
+                wm, wh = dM[at], dH[at]
+                if beyond >= 0:
+                    wm = wm + rxr[W + 1 + beyond]
+                    wh = wh + lane_unpack(rxr[2 * W + 1], beyond)
+                wm, wh = reciprocal(wm), reciprocal(wh)
+                iM[at], iH[at] = wm, wh
+            else:
+                wm, wh = iM[at], iH[at]
+            if beyond >= 0:
+                sm = sm + rxr[beyond]
+                sh = sh + lane_unpack(rxr[W], beyond)
+            va, vb = resid_coef * (sm * wm - m), resid_coef * (sh * wh - h)
             if number > 0:
-                va, vb = cc * vM[x] + va, cc * vH[x] + vb
-            vM[x], vH[x] = va, vb
-            new[0][x], new[1][x] = m + va, h + vb
-
-        reach = SWEEPS_T - 1 - number
-        loop(S - reach, X - 1 + reach, sweep)
+                va, vb = carry_coef * vM[at] + va, carry_coef * vH[at] + vb
+            if number < SWEEPS_T - 1:
+                vM[at], vH[at] = va, vb
+                new[0][at], new[1][at] = m + va, h + vb
+            else:
+                torso_out[x] = (m + va)[0:Y]
         old, new = new, ((bM, bH) if number == 0 else old)
-    torso_out[0:S] = surface[...]
-    torso_out[S:X] = old[0][S:X, 0:Y]
-
-
-def final_body(place, back, index, phi, out, total):
+
+
+def final_body(place, sent, back, index, phi, out, total):
     X, Y, _ = phi.shape
     rows = X // 4 * Y
-    scatter_rows(back, index, rows, total, 8)
+    scatter_rows(
+        lambda s: penalty * (sent[pl.ds(s, 1), 0, :] - back[pl.ds(s, 1), 0, :]), index, rows, total, 2
+    )
     flux = (total[0:rows] + total[rows : 2 * rows]).reshape(X // 4, Y, LANES)
     (dm, _, _), _ = heart_tiles(place, Y)
     out[X // 4 :] = phi[X // 4 :]
@@ -622,13 +657,13 @@
     hxl = from_last(high, "gx")
     torso_wide, high, low = call(
         torso_x_body, (wide_of(TX, TY), face_of(TY), face_of(Y + 2 * W + TY)), 8,
-        smem=(0,), after=(hxl,),
+        smem=(0,),
     )(place, heart_wide, *torso, *halos[2:], ryl, ryr)
     txl, xr = from_last(high, "gx"), from_next(low, "gx")
 
     thin = pltpu.VMEM((3 * W, Y + 2 * W, LANES), jnp.float32)
     sent = call(
-        heart_surface_body, f32(peers, cap), 4,
+        heart_surface_body, f32(peers, 1, cap), 4,
         scratch=[pltpu.VMEM((X // 4 * Y, LANES), jnp.float32)] + [thin] * 10, smem=(0,),
     )(place, heart_wide, hxl, send_index)
     arrived = swap(sent)
@@ -636,7 +671,7 @@
     ext = pltpu.VMEM((X + 2 * W, Y + 2 * W, LANES), jnp.float32)
     phi_new, new_membrane = call(
         heart_body, (f32(X, Y, LANES), f32(X, Y, LANES)), 5,
-        scratch=[ext] * 10, smem=(0,), whole=True,
+        scratch=[ext] * 10, smem=(0,),
     )(place, current, heart_wide, hxl, xr)
     right, rzlo, rzhi = call(
         right_body,
@@ -645,25 +680,34 @@
     )(arrived, recv_index, weight)
     text = (TX + 2 * W, TY + 2 * W, LANES)
     big = pltpu.VMEM(text, jnp.float32)
-    faces = call(faces_body, f32(10, *text), 3, scratch=[big] * 2)(torso_wide, txl, xr)
+    N = S + SWEEPS_T - 1
+    middle_n = TX - S - 2 * (SWEEPS_T - 1)
+    faces, middle = call(
+        faces_body, (f32(10, *text), f32(middle_n, TY, LANES)), 3, scratch=[big] * 10
+    )(torso_wide, txl, xr)
     halos, ryl, ryr = two_stages(place, ((right, weight),), rzlo, rzhi)
     right_wide, low = call(
         right_x_body, (wide_of(S, TY), face_of(TY)), 7, smem=(0,)
     )(place, right, weight, *halos, ryl, ryr)
     rxr = from_next(low, "gx")
-    flat = pltpu.VMEM((3 * W, TY + 2 * W, LANES), jnp.float32)
+    flat = pltpu.VMEM((N + 2 * W, TY + 2 * W, LANES), jnp.float32)
     surface, returned = call(
-        torso_surface_body, (f32(S, TY, LANES), f32(peers, cap)), 4,
+        torso_surface_body, (f32(N, TY, LANES), f32(peers, 1, cap)), 3,
         scratch=[flat] * 8,
-    )(right_wide, arrived, recv_index, faces)
+    )(right_wide, recv_index, faces)
     back = swap(returned)
+    last_n = TX - N - middle_n + 2 * W
+    thin = pltpu.VMEM((last_n, TY + 2 * W, LANES), jnp.float32)
     torso_out = call(
-        torso_body, f32(TX, TY, LANES), 4, scratch=[big] * 10, whole=True,
-    )(surface, right_wide, rxr, faces)
+        torso_body, f32(TX, TY, LANES), 4,
+        scratch=[pltpu.VMEM((10, last_n, TY + 2 * W, LANES), jnp.float32)]
+        + [thin] * 8 + [pltpu.SemaphoreType.DMA(())],
+        left=(3,), whole=True,
+    )(surface, middle, rxr, faces)
     heart_phi = call(
-        final_body, f32(X, Y, LANES), 4,
+        final_body, f32(X, Y, LANES), 5,
         scratch=[pltpu.VMEM((2 * X // 4 * Y, LANES), jnp.float32)], smem=(0,),
-    )(place, back, send_index, phi_new)
+    )(place, sent, back, send_index, phi_new)
     return (new_membrane, heart_phi, torso_out)
 
 

time: 115 us -> 104 us (0.904)
  Pallas kernels: 49.3 us -> 42.1 us
  starting transfers between devices: 43.8 us -> 40.6 us
    pallas_call x14, Pallas kernels: 49.3 us -> 42.1 us  [the longest x1 7.13 us: per_device(): call(torso_surface_body, (f32(N, TY, LANES), f32(peers, 1, cap)), 3, scra...]
    ppermute x6, starting transfers between devices: 16.6 us -> 15.1 us  [from_last(): lax.ppermute(value, axis, [(i, (i + 1) % count) for i in range(count)])]
    all_to_all x2 -> x0, local copies, waits for them, and re-layouts: 1.58 us -> none  [swap(): lax.all_to_all(value, ('gx', 'gy'), split_axis=0, concat_axis=0, tiled=True)]
    unnamed x50 -> x38, local copies, waits for them, and re-layouts: 6.11 us -> 7.67 us
    ppermute x6, waiting for transfers between devices: 6.72 us -> 5.57 us  [from_last(): lax.ppermute(value, axis, [(i, (i + 1) % count) for i in range(count)])]
  transfers between devices with their start and end apart: 14 -> 14, of which waited for: 7 -> 6; matrix products, arithmetic and copies ran while one was open for 3% -> 2% of each run, Pallas kernels for 32% -> 27%
where the time goes in v1:
time: 104 us; the launch traced here: 103 us
  Pallas kernels  42.1 us (40%)
  starting transfers between devices  40.6 us (39%)
  waiting for transfers between devices  9.84 us (9%)
  local copies, waits for them, and re-layouts  7.76 us (7%)
  other arithmetic  2.09 us (2%)
    ppermute x6, starting transfers between devices, from_last(): lax.ppermute(value, axis, [(i, (i + 1) % count) for i in range(count)])  15.1 us
    all_to_all x2, starting transfers between devices, swap(): lax.all_to_all(value, ('gx', 'gy'), split_axis=0, concat_axis=0, tiled=True)  13.4 us
    ppermute x6, starting transfers between devices, from_next(): lax.ppermute(value, axis, [((i + 1) % count, i) for i in range(count)])  12.1 us
    unnamed x38, local copies, waits for them, and re-layouts  7.67 us
    pallas_call x1, Pallas kernels, per_device(): call(torso_surface_body, (f32(N, TY, LANES), f32(peers, 1, cap)), 3, scra...  7.13 us
    ppermute x6, waiting for transfers between devices, from_last(): lax.ppermute(value, axis, [(i, (i + 1) % count) for i in range(count)])  5.57 us
    pallas_call x1, Pallas kernels, per_device(): call(right_body, (f32(S, TY, LANES), f32(2 * W, S * TY), f32(2 * W, S * T...  4.82 us
    pallas_call x1, Pallas kernels, per_device(): call(heart_surface_body, f32(peers, 1, cap), 4, scratch=[pltpu.VMEM((X //...  4.57 us
  transfers between devices with their start and end apart: 14, of which 6 were waited for; matrix products, arithmetic and copies ran while one was open for 2% of the time, Pallas kernels for 27%

profile of v1, /device:TPU:1, one launch (start us, length us, event | category | flops | bytes accessed | tf_op | source)
XLA Modules:
  0.0 103.3 jit_solution(7057652415104320275)
XLA Ops:
  0.7 2.2 %shard_map.139 = (f32[16,32,128]{2,1,0:T(8,128)}, f32[8,768]{1,0:T(8,128)}, f32[8,768]{1,0:T(8,128)}) custom-call(f32[4]{0:T(128)} %table.1, f32[16,16,128]{2,1,0:T(8,128)} %f0.2, f32[16,16,128]{2,1,0:T(8,128)} %f1.1, f32[16,32,128]{2,1,0:T(8,128)} %f0.3, f32[16,32,128]{2,1,0:T(8,128)} %scale.1, s32[16,32,128]{2,1,0:T(8,128)} %labels.1), custom_call_target="tpu_custom_call" | custom-call | tf_op jit(solution)/shard_map/pallas_call | solution.py:644
  2.8 3.8 %collective-permute-start = (f32[8,768]{1,0:T(8,128)}, f32[8,768]{1,0:T(8,128)S(1)}, u32[]{:S(2)}, u32[]{:S(2)}) collective-permute-start(f32[8,768]{1,0:T(8,128)} %get-tuple-element.33), channel_id=1, source_target_pairs={{0,64},{64,128},{128,192},{192,0},{1,65},{65,129},{129,193},{193,1... | collective-permute-start | bytes 73736 | tf_op jit(solution)/shard_map/ppermute | solution.py:178
  6.6 3.0 %collective-permute-start.1 = (f32[8,768]{1,0:T(8,128)}, f32[8,768]{1,0:T(8,128)S(1)}, u32[]{:S(2)}, u32[]{:S(2)}) collective-permute-start(f32[8,768]{1,0:T(8,128)} %get-tuple-element.34), channel_id=1, source_target_pairs={{64,0},{128,64},{192,128},{0,192},{65,1},{129,65},{193,129},{1,193... | collective-permute-start | bytes 73736 | tf_op jit(solution)/shard_map/ppermute | solution.py:173
  9.7 0.1 stack.11.place
  9.7 1.3 %collective-permute-done.refs_4_ = f32[8,768]{1,0:T(8,128)S(1)} collective-permute-done((f32[8,768]{1,0:T(8,128)}, f32[8,768]{1,0:T(8,128)S(1)}, u32[]{:S(2)}, u32[]{:S(2)}) %collective-permute-start) | collective-permute-done | bytes 24608 | tf_op jit(solution)/shard_map/ppermute | solution.py:178
  11.1 1.2 %collective-permute-done.1.refs_5_ = f32[8,768]{1,0:T(8,128)S(1)} collective-permute-done((f32[8,768]{1,0:T(8,128)}, f32[8,768]{1,0:T(8,128)S(1)}, u32[]{:S(2)}, u32[]{:S(2)}) %collective-permute-start.1) | collective-permute-done | bytes 24608 | tf_op jit(solution)/shard_map/ppermute | solution.py:173
  12.2 0.9 copy-done.1
  13.2 0.9 copy-done.3
  14.1 0.9 copy-done.5
  15.0 0.9 copy-done.6
  16.0 1.2 %shard_map.140 = (f32[16,16,128]{2,1,0:T(8,128)S(1)}, f32[16,16,128]{2,1,0:T(8,128)S(1)}, f32[16,32,128]{2,1,0:T(8,128)S(1)}, f32[16,32,128]{2,1,0:T(8,128)S(1)}...) custom-call(s32[5]{0:T(128)S(1)} %stack.11.place, f32[16,16,128]{2,1,0:T(8,128)S(1)} %copy-done.3, ...), custom_call_target="tpu_custom_call" | custom-call | tf_op jit(solution)/shard_map/pallas_call | solution.py:190
  17.2 0.7 copy-done.10
  17.9 1.2 %collective-permute-start.2 = (f32[34,8,128]{2,1,0:T(8,128)S(1)}, f32[34,8,128]{2,1,0:T(8,128)S(1)}, u32[]{:S(2)}, u32[]{:S(2)}) collective-permute-start(f32[34,8,128]{2,1,0:T(8,128)S(1)} %get-tuple-element.37), channel_id=1, source_target_pairs={{0,1},{1,2},{2,3},{3,0},{4,5},{5,6},{6,7},{7,4},{8,9},{9,10},{10,1... | collective-permute-start | bytes 417800 | tf_op jit(solution)/shard_map/ppermute | solution.py:178
  19.1 1.5 %collective-permute-start.3 = (f32[34,8,128]{2,1,0:T(8,128)S(1)}, f32[34,8,128]{2,1,0:T(8,128)S(1)}, u32[]{:S(2)}, u32[]{:S(2)}) collective-permute-start(f32[34,8,128]{2,1,0:T(8,128)S(1)} %get-tuple-element.38), channel_id=1, source_target_pairs={{1,0},{2,1},{3,2},{0,3},{5,4},{6,5},{7,6},{4,7},{9,8},{10,9},{11,1... | collective-permute-start | bytes 417800 | tf_op jit(solution)/shard_map/ppermute | solution.py:173
  20.6 2.4 %collective-permute-done.2.ryl = f32[34,8,128]{2,1,0:T(8,128)S(1)} collective-permute-done((f32[34,8,128]{2,1,0:T(8,128)S(1)}, f32[34,8,128]{2,1,0:T(8,128)S(1)}, u32[]{:S(2)}, u32[]{:S(2)}) %collective-permute-start.2) | collective-permute-done | bytes 139296 | tf_op jit(solution)/shard_map/ppermute | solution.py:178
  23.0 0.0 collective-permute-done.3.ryr
  23.0 0.7 shard_map.141
  23.7 4.5 %collective-permute-start.4 = (f32[10,24,128]{2,1,0:T(8,128)S(1)}, f32[10,24,128]{2,1,0:T(8,128)S(1)}, u32[]{:S(2)}, u32[]{:S(2)}) collective-permute-start(f32[10,24,128]{2,1,0:T(8,128)S(1)} %get-tuple-element.40), channel_id=1, source_target_pairs={{0,4},{4,8},{8,12},{12,16},{16,20},{20,24},{24,28},{28,32},{32,36}... | collective-permute-start | bytes 368648 | tf_op jit(solution)/shard_map/ppermute | solution.py:178
  28.2 0.1 bitcast_select_fusion.1.index
  28.3 1.8 %collective-permute-done.4.rxl = f32[10,24,128]{2,1,0:T(8,128)S(1)} collective-permute-done((f32[10,24,128]{2,1,0:T(8,128)S(1)}, f32[10,24,128]{2,1,0:T(8,128)S(1)}, u32[]{:S(2)}, u32[]{:S(2)}) %collective-permute-start.4) | collective-permute-done | bytes 122912 | tf_op jit(solution)/shard_map/ppermute | solution.py:178
  30.1 4.6 %shard_map.144.sent = f32[64,1,512]{2,1,0:T(1,128)} custom-call(s32[5]{0:T(128)S(1)} %stack.11.place, f32[4,16,24,128]{3,2,1,0:T(8,128)S(1)} %get-tuple-element.39.heart.E, f32[10,24,128]{2,1,0:T(8,128)S(1)} %collective-permute-done.4.rxl, s32[64,512]{1,0:T(8,128)S(1)} %bitcast_select_fusion.1.index), custom_call_target="tpu_custom_call" | custom-call | tf_op jit(solution)/shard_map/pallas_call | solution.py:665
  34.7 9.3 %all-to-all-start = ((f32[64,1,512]{2,1,0:T(1,128)}), f32[64,1,512]{2,1,0:T(1,128)S(1)}, u32[]{:S(2)}, u32[]{:S(2)}) async-start(f32[64,1,512]{2,1,0:T(1,128)} %shard_map.144.sent), calls=%async_computation | async-start | bytes 262144 | tf_op jit(solution)/shard_map/all_to_all | solution.py:182
  44.0 0.9 copy-done.9
  44.9 0.9 copy-done.11
  45.9 1.5 %shard_map.142 = (f32[4,16,40,128]{3,2,1,0:T(8,128)S(1)}, f32[10,40,128]{2,1,0:T(8,128)S(1)}, f32[10,64,128]{2,1,0:T(8,128)}) custom-call(s32[5]{0:T(128)S(1)} %stack.11.place, f32[4,16,24,128]{3,2,1,0:T(8,128)S(1)} %get-tuple-element.39.heart.E, f32[16,32,128]{2,1,0:T(8,128)S(1)} %copy-done.2, f32[16,32,128]{2,1,0:T(8,128)S(1)} %copy-done.7, ...), custom_call_target="tpu_custom_call" | custom-call | tf_op jit(solution)/shard_map/pallas_call | solution.py:658
  47.4 0.5 collective-permute-start.5
  47.8 1.0 bitcast_select_fusion.index
  48.8 2.9 %shard_map.145.weight.refs_1_.f1 = f32[4,32,128]{2,1,0:T(8,128)S(1)} custom-call(s32[64,512]{1,0:T(8,128)S(1)} %bitcast_select_fusion.index), custom_call_target="tpu_custom_call" | custom-call | tf_op jit(solution)/shard_map/pallas_call | solution.py:647
  51.8 0.7 all-to-all-done.arrived
  52.5 4.8 %shard_map.146 = (f32[4,32,128]{2,1,0:T(8,128)S(1)}, f32[8,128]{1,0:T(8,128)S(1)}, f32[8,128]{1,0:T(8,128)S(1)}) custom-call(f32[64,1,512]{2,1,0:T(1,128)S(1)} %all-to-all-done.arrived, s32[64,512]{1,0:T(8,128)S(1)} %bitcast_select_fusion.index, f32[4,32,128]{2,1,0:T(8,128)S(1)} %shard_map.145.weight.refs_1_.f1), custom_call_target="tpu_custom_call" | custom-call | tf_op jit(solution)/shard_map/pallas_call | solution.py:676
  57.3 3.9 %collective-permute-start.6 = (f32[8,128]{1,0:T(8,128)S(1)}, f32[8,128]{1,0:T(8,128)S(1)}, u32[]{:S(2)}, u32[]{:S(2)}) collective-permute-start(f32[8,128]{1,0:T(8,128)S(1)} %get-tuple-element.46), channel_id=1, source_target_pairs={{0,64},{64,128},{128,192},{192,0},{1,65},{65,129},{129,193},{193,1... | collective-permute-start | bytes 12296 | tf_op jit(solution)/shard_map/ppermute | solution.py:178
  61.2 0.0 collective-permute-start.7
  61.2 1.0 collective-permute-start.10
  62.2 2.4 %collective-permute-done.7.refs_3_ = f32[8,128]{1,0:T(8,128)S(1)} collective-permute-done((f32[8,128]{1,0:T(8,128)S(1)}, f32[8,128]{1,0:T(8,128)S(1)}, u32[]{:S(2)}, u32[]{:S(2)}) %collective-permute-start.7) | collective-permute-done | bytes 4128 | tf_op jit(solution)/shard_map/ppermute | solution.py:173
  64.6 0.8 shard_map.147
  65.4 0.6 collective-permute-start.8
  66.1 2.1 %collective-permute-start.9 = (f32[5,8,128]{2,1,0:T(8,128)S(1)}, f32[5,8,128]{2,1,0:T(8,128)S(1)}, u32[]{:S(2)}, u32[]{:S(2)}) collective-permute-start(f32[5,8,128]{2,1,0:T(8,128)S(1)} %get-tuple-element.51), channel_id=1, source_target_pairs={{1,0},{2,1},{3,2},{0,3},{5,4},{6,5},{7,6},{4,7},{9,8},{10,9},{11,1... | collective-permute-start | bytes 61448 | tf_op jit(solution)/shard_map/ppermute | solution.py:173
  68.2 3.5 %shard_map.149 = (f32[10,24,40,128]{3,2,1,0:T(8,128)S(1)}, f32[6,32,128]{2,1,0:T(8,128)S(1)}) custom-call(f32[4,16,40,128]{3,2,1,0:T(8,128)S(1)} %get-tuple-element.53.E, f32[10,40,128]{2,1,0:T(8,128)S(1)} %collective-permute-done.10.rxl, f32[10,64,128]{2,1,0:T(8,128)S(1)} %collective-permute-done.5.rxr), custom_call_target="tpu_custom_call" | custom-call | tf_op jit(solution)/shard_map/pallas_call | solution.py:685
  71.7 0.7 shard_map.148
  72.4 5.1 %collective-permute-start.11 = (f32[10,40,128]{2,1,0:T(8,128)S(1)}, f32[10,40,128]{2,1,0:T(8,128)S(1)}, u32[]{:S(2)}, u32[]{:S(2)}) collective-permute-start(f32[10,40,128]{2,1,0:T(8,128)S(1)} %get-tuple-element.60), channel_id=1, source_target_pairs={{4,0},{8,4},{12,8},{16,12},{20,16},{24,20},{28,24},{32,28},{36,32}... | collective-permute-start | bytes 614408 | tf_op jit(solution)/shard_map/ppermute | solution.py:173
  77.5 7.1 %shard_map.150 = (f32[7,32,128]{2,1,0:T(8,128)S(1)}, f32[64,1,512]{2,1,0:T(1,128)}) custom-call(f32[4,4,40,128]{3,2,1,0:T(8,128)S(1)} %get-tuple-element.52.R, s32[64,512]{1,0:T(8,128)S(1)} %bitcast_select_fusion.index, f32[10,24,40,128]{3,2,1,0:T(8,128)S(1)} %get-tuple-element.55.F), custom_call_target="tpu_custom_call" | custom-call | tf_op jit(solution)/shard_map/pallas_call | solution.py:694
  84.6 0.6 copy-done.12
  85.3 4.2 %all-to-all-start.1 = ((f32[64,1,512]{2,1,0:T(1,128)}), f32[64,1,512]{2,1,0:T(1,128)S(1)}, u32[]{:S(2)}, u32[]{:S(2)}) async-start(f32[64,1,512]{2,1,0:T(1,128)} %get-tuple-element.56), calls=%async_computation.1 | async-start | bytes 262144 | tf_op jit(solution)/shard_map/all_to_all | solution.py:182
  89.5 1.0 multiply_reduce_fusion.current
  90.5 3.4 %shard_map.143 = (f32[16,16,128]{2,1,0:T(8,128)S(1)}, f32[16,16,128]{2,1,0:T(8,128)}) custom-call(s32[5]{0:T(128)S(1)} %stack.11.place, f32[16,16,128]{2,1,0:T(8,128)S(1)} %multiply_reduce_fusion.current, f32[4,16,24,128]{3,2,1,0:T(8,128)S(1)} %get-tuple-element.39.heart.E, f32[10,24,128]{2,1,0:T(8,128)S(1)} %collective-permute-done.4.rxl, ...), custom_call_target="tpu_custom_call" | custom-call | tf_op jit(solution)/shard_map/pallas_call | solution.py:672
  94.0 0.7 copy-done.15
  94.6 4.1 %shard_map.152 = f32[16,32,128]{2,1,0:T(8,128)} custom-call(f32[7,32,128]{2,1,0:T(8,128)} %copy-done.12, f32[6,32,128]{2,1,0:T(8,128)} %copy-done.13, f32[10,40,128]{2,1,0:T(8,128)} %copy-done.15, f32[10,24,40,128]{3,2,1,0:T(8,128)} %copy-done), custom_call_target="tpu_custom_call" | custom-call | tf_op jit(solution)/shard_map/pallas_call | solution.py:701
  98.7 4.6 %shard_map.151 = f32[16,16,128]{2,1,0:T(8,128)} custom-call(s32[5]{0:T(128)S(1)} %stack.11.place, f32[64,1,512]{2,1,0:T(1,128)} %shard_map.144.sent, f32[64,1,512]{2,1,0:T(1,128)S(1)} %all-to-all-done.1.back, s32[64,512]{1,0:T(8,128)S(1)} %bitcast_select_fusion.1.index, f32[16,16,128]{2,1,0:T(8,128)S(1)} %get-tuple-element.57.phi), custom_call_target="tpu_custom_call" | custom-call | tf_op jit(solution)/shard_map/pallas_call | solution.py:707
  (37 shorter events, 0.1 us)
Async XLA Ops:
  0.6 27.6 %copy-start.18 = (s32[1,1,1,64]{3,2,1,0:T(1,128)S(1)}, s32[1,1,1,64]{3,2,1,0:T(1,128)}, u32[]{:S(2)}) copy-start(s32[1,1,1,64]{3,2,1,0:T(1,128)} %param.21) | copy-start | bytes 772
  0.6 27.6 %copy-start.16 = (s32[1,1,1,64,512]{4,3,2,1,0:T(8,128)S(1)}, s32[1,1,1,64,512]{4,3,2,1,0:T(8,128)}, u32[]{:S(2)}) copy-start(s32[1,1,1,64,512]{4,3,2,1,0:T(8,128)} %param.20) | copy-start | bytes 393220
  2.8 8.3 %collective-permute-start = (f32[8,768]{1,0:T(8,128)}, f32[8,768]{1,0:T(8,128)S(1)}, u32[]{:S(2)}, u32[]{:S(2)}) collective-permute-start(f32[8,768]{1,0:T(8,128)} %get-tuple-element.33), channel_id=1, source_target_pairs={{0,64},{64,128},{128,192},{192,0},{1,65},{65,129},{129,193},{193,1... | collective-permute-start | bytes 73736 | tf_op jit(solution)/shard_map/ppermute | solution.py:178
  6.6 5.6 %collective-permute-start.1 = (f32[8,768]{1,0:T(8,128)}, f32[8,768]{1,0:T(8,128)S(1)}, u32[]{:S(2)}, u32[]{:S(2)}) collective-permute-start(f32[8,768]{1,0:T(8,128)} %get-tuple-element.34), channel_id=1, source_target_pairs={{64,0},{128,64},{192,128},{0,192},{65,1},{129,65},{193,129},{1,193... | collective-permute-start | bytes 73736 | tf_op jit(solution)/shard_map/ppermute | solution.py:173
  12.2 1.0 copy-start.1
  13.2 0.9 copy-start.3
  14.1 0.9 copy-start.5
  15.0 0.9 copy-start.6
  16.0 28.0 %copy-start.2 = (f32[16,32,128]{2,1,0:T(8,128)S(1)}, f32[16,32,128]{2,1,0:T(8,128)}, u32[]{:S(2)}) copy-start(f32[16,32,128]{2,1,0:T(8,128)} %f0.3) | copy-start | bytes 786436
  16.0 28.0 %copy-start.7 = (f32[16,32,128]{2,1,0:T(8,128)S(1)}, f32[16,32,128]{2,1,0:T(8,128)}, u32[]{:S(2)}) copy-start(f32[16,32,128]{2,1,0:T(8,128)} %get-tuple-element.32.refs_3_.f1) | copy-start | bytes 786436
  17.2 0.7 copy-start.10
  17.9 12.2 %copy-start.8 = (f32[16,32,128]{2,1,0:T(8,128)}, f32[16,32,128]{2,1,0:T(8,128)S(1)}, u32[]{:S(2)}) copy-start(f32[16,32,128]{2,1,0:T(8,128)S(1)} %get-tuple-element.41.h0) | copy-start | bytes 786436
  17.9 5.1 %collective-permute-start.2 = (f32[34,8,128]{2,1,0:T(8,128)S(1)}, f32[34,8,128]{2,1,0:T(8,128)S(1)}, u32[]{:S(2)}, u32[]{:S(2)}) collective-permute-start(f32[34,8,128]{2,1,0:T(8,128)S(1)} %get-tuple-element.37), channel_id=1, source_target_pairs={{0,1},{1,2},{2,3},{3,0},{4,5},{5,6},{6,7},{7,4},{8,9},{9,10},{10,1... | collective-permute-start | bytes 417800 | tf_op jit(solution)/shard_map/ppermute | solution.py:178
  19.1 3.9 %collective-permute-start.3 = (f32[34,8,128]{2,1,0:T(8,128)S(1)}, f32[34,8,128]{2,1,0:T(8,128)S(1)}, u32[]{:S(2)}, u32[]{:S(2)}) collective-permute-start(f32[34,8,128]{2,1,0:T(8,128)S(1)} %get-tuple-element.38), channel_id=1, source_target_pairs={{1,0},{2,1},{3,2},{0,3},{5,4},{6,5},{7,6},{4,7},{9,8},{10,9},{11,1... | collective-permute-start | bytes 417800 | tf_op jit(solution)/shard_map/ppermute | solution.py:173
  23.7 6.4 %collective-permute-start.4 = (f32[10,24,128]{2,1,0:T(8,128)S(1)}, f32[10,24,128]{2,1,0:T(8,128)S(1)}, u32[]{:S(2)}, u32[]{:S(2)}) collective-permute-start(f32[10,24,128]{2,1,0:T(8,128)S(1)} %get-tuple-element.40), channel_id=1, source_target_pairs={{0,4},{4,8},{8,12},{12,16},{16,20},{20,24},{24,28},{28,32},{32,36}... | collective-permute-start | bytes 368648 | tf_op jit(solution)/shard_map/ppermute | solution.py:178
  34.7 33.5 %copy-start.17 = (f32[5,12]{1,0:T(8,128)S(1)}, f32[5,12]{1,0:T(8,128)}, u32[]{:S(2)}) copy-start(f32[5,12]{1,0:T(8,128)} %param.15) | copy-start | bytes 724
  34.7 17.8 %all-to-all-start = ((f32[64,1,512]{2,1,0:T(1,128)}), f32[64,1,512]{2,1,0:T(1,128)S(1)}, u32[]{:S(2)}, u32[]{:S(2)}) async-start(f32[64,1,512]{2,1,0:T(1,128)} %shard_map.144.sent), calls=%async_computation | async-start | bytes 262144 | tf_op jit(solution)/shard_map/all_to_all | solution.py:182
  44.0 1.0 copy-start.9
  44.9 0.9 copy-start.11
  47.4 20.8 %collective-permute-start.5 = (f32[10,64,128]{2,1,0:T(8,128)}, f32[10,64,128]{2,1,0:T(8,128)S(1)}, u32[]{:S(2)}, u32[]{:S(2)}) collective-permute-start(f32[10,64,128]{2,1,0:T(8,128)} %get-tuple-element.43), channel_id=1, source_target_pairs={{4,0},{8,4},{12,8},{16,12},{20,16},{24,20},{28,24},{32,28},{36,32}... | collective-permute-start | bytes 983048 | tf_op jit(solution)/shard_map/ppermute | solution.py:173
  57.3 4.9 %collective-permute-start.6 = (f32[8,128]{1,0:T(8,128)S(1)}, f32[8,128]{1,0:T(8,128)S(1)}, u32[]{:S(2)}, u32[]{:S(2)}) collective-permute-start(f32[8,128]{1,0:T(8,128)S(1)} %get-tuple-element.46), channel_id=1, source_target_pairs={{0,64},{64,128},{128,192},{192,0},{1,65},{65,129},{129,193},{193,1... | collective-permute-start | bytes 12296 | tf_op jit(solution)/shard_map/ppermute | solution.py:178
  61.2 3.4 %collective-permute-start.7 = (f32[8,128]{1,0:T(8,128)S(1)}, f32[8,128]{1,0:T(8,128)S(1)}, u32[]{:S(2)}, u32[]{:S(2)}) collective-permute-start(f32[8,128]{1,0:T(8,128)S(1)} %get-tuple-element.47), channel_id=1, source_target_pairs={{64,0},{128,64},{192,128},{0,192},{65,1},{129,65},{193,129},{1,193... | collective-permute-start | bytes 12296 | tf_op jit(solution)/shard_map/ppermute | solution.py:173
  61.2 6.9 %collective-permute-start.10 = (f32[10,40,128]{2,1,0:T(8,128)S(1)}, f32[10,40,128]{2,1,0:T(8,128)S(1)}, u32[]{:S(2)}, u32[]{:S(2)}) collective-permute-start(f32[10,40,128]{2,1,0:T(8,128)S(1)} %get-tuple-element.54), channel_id=1, source_target_pairs={{0,4},{4,8},{8,12},{12,16},{16,20},{20,24},{24,28},{28,32},{32,36}... | collective-permute-start | bytes 614408 | tf_op jit(solution)/shard_map/ppermute | solution.py:178
  65.4 6.3 %collective-permute-start.8 = (f32[5,8,128]{2,1,0:T(8,128)S(1)}, f32[5,8,128]{2,1,0:T(8,128)S(1)}, u32[]{:S(2)}, u32[]{:S(2)}) collective-permute-start(f32[5,8,128]{2,1,0:T(8,128)S(1)} %get-tuple-element.50), channel_id=1, source_target_pairs={{0,1},{1,2},{2,3},{3,0},{4,5},{5,6},{6,7},{7,4},{8,9},{9,10},{10,1... | collective-permute-start | bytes 61448 | tf_op jit(solution)/shard_map/ppermute | solution.py:178
  66.1 5.7 %collective-permute-start.9 = (f32[5,8,128]{2,1,0:T(8,128)S(1)}, f32[5,8,128]{2,1,0:T(8,128)S(1)}, u32[]{:S(2)}, u32[]{:S(2)}) collective-permute-start(f32[5,8,128]{2,1,0:T(8,128)S(1)} %get-tuple-element.51), channel_id=1, source_target_pairs={{1,0},{2,1},{3,2},{0,3},{5,4},{6,5},{7,6},{4,7},{9,8},{10,9},{11,1... | collective-permute-start | bytes 61448 | tf_op jit(solution)/shard_map/ppermute | solution.py:173
  71.7 12.9 %copy-start = (f32[10,24,40,128]{3,2,1,0:T(8,128)}, f32[10,24,40,128]{3,2,1,0:T(8,128)S(1)}, u32[]{:S(2)}) copy-start(f32[10,24,40,128]{3,2,1,0:T(8,128)S(1)} %get-tuple-element.55.F) | copy-start | bytes 14745604
  71.7 12.9 %copy-start.13 = (f32[6,32,128]{2,1,0:T(8,128)}, f32[6,32,128]{2,1,0:T(8,128)S(1)}, u32[]{:S(2)}) copy-start(f32[6,32,128]{2,1,0:T(8,128)S(1)} %get-tuple-element.59.middle) | copy-start | bytes 294916
  72.4 21.5 %collective-permute-start.11 = (f32[10,40,128]{2,1,0:T(8,128)S(1)}, f32[10,40,128]{2,1,0:T(8,128)S(1)}, u32[]{:S(2)}, u32[]{:S(2)}) collective-permute-start(f32[10,40,128]{2,1,0:T(8,128)S(1)} %get-tuple-element.60), channel_id=1, source_target_pairs={{4,0},{8,4},{12,8},{16,12},{20,16},{24,20},{28,24},{32,28},{36,32}... | collective-permute-start | bytes 614408 | tf_op jit(solution)/shard_map/ppermute | solution.py:173
  77.5 12.0 %copy-start.4 = (f32[16,16,128]{2,1,0:T(8,128)S(1)}, f32[16,16,128]{2,1,0:T(8,128)}, u32[]{:S(2)}) copy-start(f32[16,16,128]{2,1,0:T(8,128)} %f0.2) | copy-start | bytes 393220
  77.5 12.0 %copy-start.14 = (bf16[12,16,16,128]{3,2,1,0:T(8,128)(2,1)S(1)}, bf16[12,16,16,128]{3,2,1,0:T(8,128)(2,1)}, u32[]{:S(2)}) copy-start(bf16[12,16,16,128]{3,2,1,0:T(8,128)(2,1)} %param.12) | copy-start | bytes 2359300
  84.6 0.7 copy-start.12
  85.3 13.5 %all-to-all-start.1 = ((f32[64,1,512]{2,1,0:T(1,128)}), f32[64,1,512]{2,1,0:T(1,128)S(1)}, u32[]{:S(2)}, u32[]{:S(2)}) async-start(f32[64,1,512]{2,1,0:T(1,128)} %get-tuple-element.56), calls=%async_computation.1 | async-start | bytes 262144 | tf_op jit(solution)/shard_map/all_to_all | solution.py:182
  94.0 0.7 copy-start.15

commit v2 on v1

--- a/solution.py
+++ b/solution.py
@@ -1,5 +1,3 @@
-import functools
-
 import jax
 import jax.numpy as jnp
 from jax import lax
@@ -131,20 +129,19 @@
         out[base + W] = lane_pack([E[2 * number + 1, start + x] for x in range(W)])
 
 
-def y_body(groups, place, *refs):
-    fields, rest = refs[: 2 * groups], refs[2 * groups :]
-    rl, rr, halos, ylo, yhi = rest[0], rest[1], rest[2:-2], rest[-2], rest[-1]
+def static_y_body(place, table, m, p, phi, scale, labels, rl, rr, h0, h1, g0, g1, cond, ylo, yhi):
     near = edges(place)[1]
-    col = row = 0
-    for k in range(groups):
-        f0, f1 = fields[2 * k : 2 * k + 2]
-        X, Y, _ = f0.shape
-        cols, rows = pl.ds(col, X * Y), pl.ds(row, X + 1)
-        y_part(
-            f0, f1, rl.at[:, cols], rr.at[:, cols], halos[2 * k], halos[2 * k + 1],
-            ylo.at[rows], yhi.at[rows], near,
-        )
-        col, row = col + X * Y, row + X + 1
+    X, Y, _ = m.shape
+    TX, TY, _ = phi.shape
+    cond[...] = conductivity(table, scale, labels)
+    cols, rows = pl.ds(0, X * Y), pl.ds(0, X + 1)
+    y_part(m, p, rl.at[:, cols], rr.at[:, cols], h0, h1, ylo.at[rows], yhi.at[rows], near)
+    cols, rows = pl.ds(X * Y, TX * TY), pl.ds(X + 1, TX + 1)
+    y_part(phi, cond, rl.at[:, cols], rr.at[:, cols], g0, g1, ylo.at[rows], yhi.at[rows], near)
+
+
+def right_y_body(place, right, weight, rl, rr, h0, h1, ylo, yhi):
+    y_part(right, weight, rl, rr, h0, h1, ylo, yhi, edges(place)[1])
 
 
 def heart_x_body(place, f0, f1, h0, h1, ryl, ryr, E, high):
@@ -182,17 +179,9 @@
     return lax.all_to_all(value, ("gx", "gy"), split_axis=0, concat_axis=0, tiled=True)
 
 
-def two_stages(place, groups, zlo, zhi):
-    count = len(groups)
-    fields = [f for group in groups for f in group]
-    rr, rl = from_next(zlo, "grp"), from_last(zhi, "grp")
-    tall = f32(sum(group[0].shape[0] + 1 for group in groups), 2 * W, LANES)
-    *halos, ylo, yhi = call(
-        functools.partial(y_body, count),
-        tuple(f32(*f.shape) for f in fields) + (tall, tall),
-        3 + len(fields), smem=(0,),
-    )(place, *fields, rl, rr)
-    return halos, from_last(yhi, "gy"), from_next(ylo, "gy")
+def both_ways(low, high, axis):
+    after = from_next(low, axis)
+    return from_last(high, axis), after
 
 
 def wide_of(X, Y):
@@ -314,18 +303,21 @@
     lax.fori_loop(0, index.shape[0] // (8 * batch), step, 0)
 
 
-def start_body(table, m, p, phi, scale, labels, cond, zlo, zhi):
+def conductivity(table, scale, labels):
+    picked = jnp.zeros(labels.shape, jnp.float32)
+    for number in range(LABELS):
+        picked = jnp.where(labels[...] == number, table[number], picked)
+    return scale[...] * picked
+
+
+def start_body(table, m, p, phi, scale, labels, zlo, zhi):
     X, Y, _ = m.shape
     TX, TY, _ = phi.shape
     cols, more = pl.ds(0, X * Y), pl.ds(X * Y, TX * TY)
     z_faces(
         [m[...].reshape(X * Y, LANES), p[...].reshape(X * Y, LANES)], zlo.at[:, cols], zhi.at[:, cols]
     )
-    picked = jnp.zeros(labels.shape, jnp.float32)
-    for number in range(LABELS):
-        picked = jnp.where(labels[...] == number, table[number], picked)
-    value = scale[...] * picked
-    cond[...] = value
+    value = conductivity(table, scale, labels)
     z_faces(
         [phi[...].reshape(TX * TY, LANES), value.reshape(TX * TY, LANES)], zlo.at[:, more], zhi.at[:, more]
     )
@@ -641,16 +633,23 @@
 
     S = TX // 4
     wide = f32(2 * W, X * Y + TX * TY)
-    cond, zlo, zhi = call(
-        start_body, (f32(TX, TY, LANES), wide, wide), 6, smem=(0,), whole=True,
-    )(cond_table, membrane, phi_heart, torso_phi, tissue_scale, labels)
+    zlo, zhi = call(start_body, (wide, wide), 6, smem=(0,), whole=True)(
+        cond_table, membrane, phi_heart, torso_phi, tissue_scale, labels
+    )
     weight = call(
         weight_body, f32(S, TY, LANES), 1, scratch=[pltpu.VMEM((S * TY, LANES), jnp.float32)]
     )(recv_index)
     current = ionic_current(states, membrane, ion_params)
 
+    hbox, tbox, tall = f32(X, Y, LANES), f32(TX, TY, LANES), f32(X + TX + 2, 2 * W, LANES)
+    *halos, cond, ylo, yhi = call(
+        static_y_body, (hbox, hbox, tbox, tbox, tbox, tall, tall), 9, smem=(0, 1),
+    )(
+        place, cond_table, membrane, phi_heart, torso_phi, tissue_scale, labels,
+        *both_ways(zlo, zhi, "grp"),
+    )
     heart, torso = (membrane, phi_heart), (torso_phi, cond)
-    halos, ryl, ryr = two_stages(place, (heart, torso), zlo, zhi)
+    ryl, ryr = both_ways(ylo, yhi, "gy")
     heart_wide, high = call(
         heart_x_body, (wide_of(X, Y), face_of(Y)), 7, smem=(0,)
     )(place, *heart, *halos[:2], ryl, ryr)
@@ -685,7 +684,11 @@
     faces, middle = call(
         faces_body, (f32(10, *text), f32(middle_n, TY, LANES)), 3, scratch=[big] * 10
     )(torso_wide, txl, xr)
-    halos, ryl, ryr = two_stages(place, ((right, weight),), rzlo, rzhi)
+    tall = f32(S + 1, 2 * W, LANES)
+    *halos, ylo, yhi = call(
+        right_y_body, (f32(S, TY, LANES),) * 2 + (tall, tall), 5, smem=(0,),
+    )(place, right, weight, *both_ways(rzlo, rzhi, "grp"))
+    ryl, ryr = both_ways(ylo, yhi, "gy")
     right_wide, low = call(
         right_x_body, (wide_of(S, TY), face_of(TY)), 7, smem=(0,)
     )(place, right, weight, *halos, ryl, ryr)
@@ -702,7 +705,7 @@
         torso_body, f32(TX, TY, LANES), 4,
         scratch=[pltpu.VMEM((10, last_n, TY + 2 * W, LANES), jnp.float32)]
         + [thin] * 8 + [pltpu.SemaphoreType.DMA(())],
-        left=(3,), whole=True,
+        left=(3,),
     )(surface, middle, rxr, faces)
     heart_phi = call(
         final_body, f32(X, Y, LANES), 5,

time: 104 us -> 107 us (1.029)
  local copies, waits for them, and re-layouts: 7.76 us -> 12.1 us
  Pallas kernels: 42.1 us -> 39.8 us
  waiting for transfers between devices: 9.84 us -> 8.53 us
  starting transfers between devices: 40.6 us -> 41.8 us
  other arithmetic: 2.09 us -> 3.2 us
    unnamed x38 -> x42, local copies, waits for them, and re-layouts: 7.67 us -> 12 us
    pallas_call x1, Pallas kernels: 4.08 us -> 1.61 us  [per_device(): call(torso_body, f32(TX, TY, LANES), 4, scratch=[pltpu.VMEM((10, last_n,...]
    ppermute x6, starting transfers between devices: 15.1 us -> 16.4 us  [from_last(): lax.ppermute(value, axis, [(i, (i + 1) % count) for i in range(count)])]
    reduce_sum x1, other arithmetic: 1.02 us -> 2.13 us  [ionic_current(): jnp.sum(params_col[3] * gate_vals * (voltage - params_col[4]), axis=0)]
  transfers between devices with their start and end apart: 14 -> 14, of which waited for: 6 -> 5; matrix products, arithmetic and copies ran while one was open for 2% -> 3% of each run, Pallas kernels for 27% -> 24%
where the time goes in v2:
time: 107 us; the launch traced here: 106 us
  starting transfers between devices  41.8 us (39%)
  Pallas kernels  39.8 us (37%)
  local copies, waits for them, and re-layouts  12.1 us (11%)
  waiting for transfers between devices  8.53 us (8%)
  other arithmetic  3.2 us (3%)
    ppermute x6, starting transfers between devices, from_last(): lax.ppermute(value, axis, [(i, (i + 1) % count) for i in range(count)])  16.4 us
    all_to_all x2, starting transfers between devices, swap(): lax.all_to_all(value, ('gx', 'gy'), split_axis=0, concat_axis=0, tiled=True)  13.3 us
    ppermute x6, starting transfers between devices, from_next(): lax.ppermute(value, axis, [((i + 1) % count, i) for i in range(count)])  12.1 us
    unnamed x42, local copies, waits for them, and re-layouts  12 us
    pallas_call x1, Pallas kernels, per_device(): call(torso_surface_body, (f32(N, TY, LANES), f32(peers, 1, cap)), 3, scra...  7.13 us
    ppermute x6, waiting for transfers between devices, from_last(): lax.ppermute(value, axis, [(i, (i + 1) % count) for i in range(count)])  5.57 us
    pallas_call x1, Pallas kernels, per_device(): call(right_body, (f32(S, TY, LANES), f32(2 * W, S * TY), f32(2 * W, S * T...  4.82 us
    pallas_call x1, Pallas kernels, per_device(): call(heart_surface_body, f32(peers, 1, cap), 4, scratch=[pltpu.VMEM((X //...  4.56 us
  transfers between devices with their start and end apart: 14, of which 5 were waited for; matrix products, arithmetic and copies ran while one was open for 3% of the time, Pallas kernels for 24%

profile of v2, /device:TPU:1, one launch (start us, length us, event | category | flops | bytes accessed | tf_op | source)
XLA Modules:
  0.0 106.2 jit_solution(17197393295683486610)
XLA Ops:
  0.7 2.2 %shard_map.139 = (f32[8,768]{1,0:T(8,128)}, f32[8,768]{1,0:T(8,128)}) custom-call(f32[4]{0:T(128)} %table.3, f32[16,16,128]{2,1,0:T(8,128)} %f0.2, f32[16,16,128]{2,1,0:T(8,128)} %f1.1, f32[16,32,128]{2,1,0:T(8,128)} %f0.3, f32[16,32,128]{2,1,0:T(8,128)} %scale.3, s32[16,32,128]{2,1,0:T(8,128)} %labels.3), custom_call_target="tpu_custom_call" | custom-call | tf_op jit(solution)/shard_map/pallas_call | solution.py:636
  2.9 3.8 %collective-permute-start = (f32[8,768]{1,0:T(8,128)}, f32[8,768]{1,0:T(8,128)S(1)}, u32[]{:S(2)}, u32[]{:S(2)}) collective-permute-start(f32[8,768]{1,0:T(8,128)} %get-tuple-element.32), channel_id=1, source_target_pairs={{0,64},{64,128},{128,192},{192,0},{1,65},{65,129},{129,193},{193,1... | collective-permute-start | bytes 73736 | tf_op jit(solution)/shard_map/ppermute | solution.py:175
  6.7 3.0 %collective-permute-start.1 = (f32[8,768]{1,0:T(8,128)}, f32[8,768]{1,0:T(8,128)S(1)}, u32[]{:S(2)}, u32[]{:S(2)}) collective-permute-start(f32[8,768]{1,0:T(8,128)} %get-tuple-element.33), channel_id=1, source_target_pairs={{64,0},{128,64},{192,128},{0,192},{65,1},{129,65},{193,129},{1,193... | collective-permute-start | bytes 73736 | tf_op jit(solution)/shard_map/ppermute | solution.py:170
  9.7 0.1 stack.11.place
  9.8 1.3 %collective-permute-done.rl = f32[8,768]{1,0:T(8,128)S(1)} collective-permute-done((f32[8,768]{1,0:T(8,128)}, f32[8,768]{1,0:T(8,128)S(1)}, u32[]{:S(2)}, u32[]{:S(2)}) %collective-permute-start) | collective-permute-done | bytes 24608 | tf_op jit(solution)/shard_map/ppermute | solution.py:175
  11.1 1.2 %collective-permute-done.1.rr = f32[8,768]{1,0:T(8,128)S(1)} collective-permute-done((f32[8,768]{1,0:T(8,128)}, f32[8,768]{1,0:T(8,128)S(1)}, u32[]{:S(2)}, u32[]{:S(2)}) %collective-permute-start.1) | collective-permute-done | bytes 24608 | tf_op jit(solution)/shard_map/ppermute | solution.py:170
  12.3 0.9 copy-done.2
  13.3 0.9 copy-done.4
  14.2 0.9 copy-done.6
  15.1 0.9 copy-done.8
  16.0 0.9 copy-done.9
  17.0 0.7 copy-done.16
  17.6 1.3 %shard_map.140 = (f32[16,16,128]{2,1,0:T(8,128)S(1)}, f32[16,16,128]{2,1,0:T(8,128)S(1)}, f32[16,32,128]{2,1,0:T(8,128)S(1)}, f32[16,32,128]{2,1,0:T(8,128)S(1)}...) custom-call(s32[5]{0:T(128)S(1)} %stack.11.place, f32[4]{0:T(128)S(1)} %copy-done.16, ...), custom_call_target="tpu_custom_call" | custom-call | tf_op jit(solution)/shard_map/pallas_call | solution.py:645
  19.0 0.7 copy-done.10
  19.6 0.7 copy-done.12
  20.4 1.2 %collective-permute-start.2 = (f32[34,8,128]{2,1,0:T(8,128)S(1)}, f32[34,8,128]{2,1,0:T(8,128)S(1)}, u32[]{:S(2)}, u32[]{:S(2)}) collective-permute-start(f32[34,8,128]{2,1,0:T(8,128)S(1)} %get-tuple-element.36), channel_id=1, source_target_pairs={{0,1},{1,2},{2,3},{3,0},{4,5},{5,6},{6,7},{7,4},{8,9},{9,10},{10,1... | collective-permute-start | bytes 417800 | tf_op jit(solution)/shard_map/ppermute | solution.py:175
  21.6 1.5 %collective-permute-start.3 = (f32[34,8,128]{2,1,0:T(8,128)S(1)}, f32[34,8,128]{2,1,0:T(8,128)S(1)}, u32[]{:S(2)}, u32[]{:S(2)}) collective-permute-start(f32[34,8,128]{2,1,0:T(8,128)S(1)} %get-tuple-element.37), channel_id=1, source_target_pairs={{1,0},{2,1},{3,2},{0,3},{5,4},{6,5},{7,6},{4,7},{9,8},{10,9},{11,1... | collective-permute-start | bytes 417800 | tf_op jit(solution)/shard_map/ppermute | solution.py:170
  23.0 2.4 %collective-permute-done.2.ryl = f32[34,8,128]{2,1,0:T(8,128)S(1)} collective-permute-done((f32[34,8,128]{2,1,0:T(8,128)S(1)}, f32[34,8,128]{2,1,0:T(8,128)S(1)}, u32[]{:S(2)}, u32[]{:S(2)}) %collective-permute-start.2) | collective-permute-done | bytes 139296 | tf_op jit(solution)/shard_map/ppermute | solution.py:175
  25.5 0.7 shard_map.141
  26.2 4.5 %collective-permute-start.4 = (f32[10,24,128]{2,1,0:T(8,128)S(1)}, f32[10,24,128]{2,1,0:T(8,128)S(1)}, u32[]{:S(2)}, u32[]{:S(2)}) collective-permute-start(f32[10,24,128]{2,1,0:T(8,128)S(1)} %get-tuple-element.39), channel_id=1, source_target_pairs={{0,4},{4,8},{8,12},{12,16},{16,20},{20,24},{24,28},{28,32},{32,36}... | collective-permute-start | bytes 368648 | tf_op jit(solution)/shard_map/ppermute | solution.py:175
  30.7 0.1 bitcast_select_fusion.1.index
  30.8 1.8 %collective-permute-done.4.rxl = f32[10,24,128]{2,1,0:T(8,128)S(1)} collective-permute-done((f32[10,24,128]{2,1,0:T(8,128)S(1)}, f32[10,24,128]{2,1,0:T(8,128)S(1)}, u32[]{:S(2)}, u32[]{:S(2)}) %collective-permute-start.4) | collective-permute-done | bytes 122912 | tf_op jit(solution)/shard_map/ppermute | solution.py:175
  32.6 4.6 %shard_map.144.sent = f32[64,1,512]{2,1,0:T(1,128)} custom-call(s32[5]{0:T(128)S(1)} %stack.11.place, f32[4,16,24,128]{3,2,1,0:T(8,128)S(1)} %get-tuple-element.38.heart.E, f32[10,24,128]{2,1,0:T(8,128)S(1)} %collective-permute-done.4.rxl, s32[64,512]{1,0:T(8,128)S(1)} %bitcast_select_fusion.1.index), custom_call_target="tpu_custom_call" | custom-call | tf_op jit(solution)/shard_map/pallas_call | solution.py:664
  37.1 9.1 %all-to-all-start = ((f32[64,1,512]{2,1,0:T(1,128)}), f32[64,1,512]{2,1,0:T(1,128)S(1)}, u32[]{:S(2)}, u32[]{:S(2)}) async-start(f32[64,1,512]{2,1,0:T(1,128)} %shard_map.144.sent), calls=%async_computation | async-start | bytes 262144 | tf_op jit(solution)/shard_map/all_to_all | solution.py:179
  46.3 0.9 copy-done.11
  47.2 0.9 copy-done.13
  48.2 0.9 copy-done.15
  49.1 1.5 %shard_map.142 = (f32[4,16,40,128]{3,2,1,0:T(8,128)S(1)}, f32[10,40,128]{2,1,0:T(8,128)S(1)}, f32[10,64,128]{2,1,0:T(8,128)}) custom-call(s32[5]{0:T(128)S(1)} %stack.11.place, f32[4,16,24,128]{3,2,1,0:T(8,128)S(1)} %get-tuple-element.38.heart.E, f32[16,32,128]{2,1,0:T(8,128)S(1)} %copy-done.3, f32[16,32,128]{2,1,0:T(8,128)S(1)} %copy-done.15, ...), custom_call_target="tpu_custom_call" | custom-call | tf_op jit(solution)/shard_map/pallas_call | solution.py:657
  50.6 0.5 collective-permute-start.5
  51.1 1.0 bitcast_select_fusion.index
  52.1 2.9 %shard_map.145.weight.f1 = f32[4,32,128]{2,1,0:T(8,128)S(1)} custom-call(s32[64,512]{1,0:T(8,128)S(1)} %bitcast_select_fusion.index), custom_call_target="tpu_custom_call" | custom-call | tf_op jit(solution)/shard_map/pallas_call | solution.py:639
  55.0 4.8 %shard_map.146 = (f32[4,32,128]{2,1,0:T(8,128)S(1)}, f32[8,128]{1,0:T(8,128)S(1)}, f32[8,128]{1,0:T(8,128)S(1)}) custom-call(f32[64,1,512]{2,1,0:T(1,128)S(1)} %all-to-all-done.arrived, s32[64,512]{1,0:T(8,128)S(1)} %bitcast_select_fusion.index, f32[4,32,128]{2,1,0:T(8,128)S(1)} %shard_map.145.weight.f1), custom_call_target="tpu_custom_call" | custom-call | tf_op jit(solution)/shard_map/pallas_call | solution.py:675
  59.9 3.9 %collective-permute-start.6 = (f32[8,128]{1,0:T(8,128)S(1)}, f32[8,128]{1,0:T(8,128)S(1)}, u32[]{:S(2)}, u32[]{:S(2)}) collective-permute-start(f32[8,128]{1,0:T(8,128)S(1)} %get-tuple-element.46), channel_id=1, source_target_pairs={{0,64},{64,128},{128,192},{192,0},{1,65},{65,129},{129,193},{193,1... | collective-permute-start | bytes 12296 | tf_op jit(solution)/shard_map/ppermute | solution.py:175
  63.8 1.6 %collective-permute-start.10 = (f32[10,40,128]{2,1,0:T(8,128)S(1)}, f32[10,40,128]{2,1,0:T(8,128)S(1)}, u32[]{:S(2)}, u32[]{:S(2)}) collective-permute-start(f32[10,40,128]{2,1,0:T(8,128)S(1)} %get-tuple-element.54), channel_id=1, source_target_pairs={{0,4},{4,8},{8,12},{12,16},{16,20},{20,24},{24,28},{28,32},{32,36}... | collective-permute-start | bytes 614408 | tf_op jit(solution)/shard_map/ppermute | solution.py:175
  65.4 1.8 %collective-permute-done.7.rr = f32[8,128]{1,0:T(8,128)S(1)} collective-permute-done((f32[8,128]{1,0:T(8,128)S(1)}, f32[8,128]{1,0:T(8,128)S(1)}, u32[]{:S(2)}, u32[]{:S(2)}) %collective-permute-start.7) | collective-permute-done | bytes 4128 | tf_op jit(solution)/shard_map/ppermute | solution.py:170
  67.1 0.8 shard_map.147
  68.0 1.3 %collective-permute-start.8 = (f32[5,8,128]{2,1,0:T(8,128)S(1)}, f32[5,8,128]{2,1,0:T(8,128)S(1)}, u32[]{:S(2)}, u32[]{:S(2)}) collective-permute-start(f32[5,8,128]{2,1,0:T(8,128)S(1)} %get-tuple-element.50), channel_id=1, source_target_pairs={{0,1},{1,2},{2,3},{3,0},{4,5},{5,6},{6,7},{7,4},{8,9},{9,10},{10,1... | collective-permute-start | bytes 61448 | tf_op jit(solution)/shard_map/ppermute | solution.py:175
  69.3 1.4 %collective-permute-start.9 = (f32[5,8,128]{2,1,0:T(8,128)S(1)}, f32[5,8,128]{2,1,0:T(8,128)S(1)}, u32[]{:S(2)}, u32[]{:S(2)}) collective-permute-start(f32[5,8,128]{2,1,0:T(8,128)S(1)} %get-tuple-element.51), channel_id=1, source_target_pairs={{1,0},{2,1},{3,2},{0,3},{5,4},{6,5},{7,6},{4,7},{9,8},{10,9},{11,1... | collective-permute-start | bytes 61448 | tf_op jit(solution)/shard_map/ppermute | solution.py:170
  70.7 3.5 %shard_map.149 = (f32[10,24,40,128]{3,2,1,0:T(8,128)S(1)}, f32[6,32,128]{2,1,0:T(8,128)S(1)}) custom-call(f32[4,16,40,128]{3,2,1,0:T(8,128)S(1)} %get-tuple-element.53.E, f32[10,40,128]{2,1,0:T(8,128)S(1)} %collective-permute-done.10.rxl, f32[10,64,128]{2,1,0:T(8,128)S(1)} %collective-permute-done.5.rxr), custom_call_target="tpu_custom_call" | custom-call | tf_op jit(solution)/shard_map/pallas_call | solution.py:684
  74.3 0.7 shard_map.148
  75.0 5.8 %collective-permute-start.11 = (f32[10,40,128]{2,1,0:T(8,128)S(1)}, f32[10,40,128]{2,1,0:T(8,128)S(1)}, u32[]{:S(2)}, u32[]{:S(2)}) collective-permute-start(f32[10,40,128]{2,1,0:T(8,128)S(1)} %get-tuple-element.60), channel_id=1, source_target_pairs={{4,0},{8,4},{12,8},{16,12},{20,16},{24,20},{28,24},{32,28},{36,32}... | collective-permute-start | bytes 614408 | tf_op jit(solution)/shard_map/ppermute | solution.py:170
  80.7 7.1 %shard_map.150 = (f32[7,32,128]{2,1,0:T(8,128)S(1)}, f32[64,1,512]{2,1,0:T(1,128)}) custom-call(f32[4,4,40,128]{3,2,1,0:T(8,128)S(1)} %get-tuple-element.52.R, s32[64,512]{1,0:T(8,128)S(1)} %bitcast_select_fusion.index, f32[10,24,40,128]{3,2,1,0:T(8,128)S(1)} %get-tuple-element.55.F), custom_call_target="tpu_custom_call" | custom-call | tf_op jit(solution)/shard_map/pallas_call | solution.py:697
  87.9 4.2 %all-to-all-start.1 = ((f32[64,1,512]{2,1,0:T(1,128)}), f32[64,1,512]{2,1,0:T(1,128)S(1)}, u32[]{:S(2)}, u32[]{:S(2)}) async-start(f32[64,1,512]{2,1,0:T(1,128)} %get-tuple-element.56), calls=%async_computation.1 | async-start | bytes 262144 | tf_op jit(solution)/shard_map/all_to_all | solution.py:179
  92.1 2.1 %multiply_reduce_fusion.current = f32[16,16,128]{2,1,0:T(8,128)S(1)} fusion(bf16[12,16,16,128]{3,2,1,0:T(8,128)(2,1)} %param.12, f32[12]{0:T(128)S(1)} %get-tuple-element.64, f32[12]{0:T(128)S(1)} %get-tuple-element.65, f32[12]{0:T(128)S(1)} %get-tuple-element.62, f32[12]{0:T(128)S(1)} %get-tuple-element.63, f32[16,16,128]{2,1,0:T(8,128)S(1)} %copy-done.5, ...), kind=kLoop, calls=%fused_computation | loop fusion | flops 5079040 | bytes 1048816 | tf_op jit(solution)/shard_map/reduce_sum | solution.py:615
  94.2 3.4 %shard_map.143 = (f32[16,16,128]{2,1,0:T(8,128)S(1)}, f32[16,16,128]{2,1,0:T(8,128)}) custom-call(s32[5]{0:T(128)S(1)} %stack.11.place, f32[16,16,128]{2,1,0:T(8,128)S(1)} %multiply_reduce_fusion.current, f32[4,16,24,128]{3,2,1,0:T(8,128)S(1)} %get-tuple-element.38.heart.E, f32[10,24,128]{2,1,0:T(8,128)S(1)} %collective-permute-done.4.rxl, ...), custom_call_target="tpu_custom_call" | custom-call | tf_op jit(solution)/shard_map/pallas_call | solution.py:671
  97.6 2.4 %copy-done.1 = f32[10,24,40,128]{3,2,1,0:T(8,128)S(1)} copy-done((f32[10,24,40,128]{3,2,1,0:T(8,128)S(1)}, f32[10,24,40,128]{3,2,1,0:T(8,128)}, u32[]{:S(2)}) %copy-start.1) | copy-done | bytes 4915224
  100.0 1.6 %shard_map.152 = f32[16,32,128]{2,1,0:T(8,128)} custom-call(f32[7,32,128]{2,1,0:T(8,128)S(1)} %get-tuple-element.58.surface, f32[6,32,128]{2,1,0:T(8,128)S(1)} %get-tuple-element.59.middle, f32[10,40,128]{2,1,0:T(8,128)S(1)} %collective-permute-done.11.rxr, f32[10,24,40,128]{3,2,1,0:T(8,128)S(1)} %copy-done.1), custom_call_target="tpu_custom_call" | custom-call | tf_op jit(solution)/shard_map/pallas_call | solution.py:704
  101.7 4.5 %shard_map.151 = f32[16,16,128]{2,1,0:T(8,128)} custom-call(s32[5]{0:T(128)S(1)} %stack.11.place, f32[64,1,512]{2,1,0:T(1,128)} %shard_map.144.sent, f32[64,1,512]{2,1,0:T(1,128)S(1)} %all-to-all-done.1.back, s32[64,512]{1,0:T(8,128)S(1)} %bitcast_select_fusion.1.index, f32[16,16,128]{2,1,0:T(8,128)S(1)} %get-tuple-element.57.phi), custom_call_target="tpu_custom_call" | custom-call | tf_op jit(solution)/shard_map/pallas_call | solution.py:710
  (41 shorter events, 0.1 us)
Async XLA Ops:
  0.6 24.9 %copy-start.5 = (f32[16,16,128]{2,1,0:T(8,128)S(1)}, f32[16,16,128]{2,1,0:T(8,128)}, u32[]{:S(2)}) copy-start(f32[16,16,128]{2,1,0:T(8,128)} %f0.2) | copy-start | bytes 393220
  0.6 24.8 %copy-start.7 = (f32[16,16,128]{2,1,0:T(8,128)S(1)}, f32[16,16,128]{2,1,0:T(8,128)}, u32[]{:S(2)}) copy-start(f32[16,16,128]{2,1,0:T(8,128)} %f1.1) | copy-start | bytes 393220
  0.7 30.0 %copy-start.19 = (s32[1,1,1,64]{3,2,1,0:T(1,128)S(1)}, s32[1,1,1,64]{3,2,1,0:T(1,128)}, u32[]{:S(2)}) copy-start(s32[1,1,1,64]{3,2,1,0:T(1,128)} %param.21) | copy-start | bytes 772
  0.7 30.0 %copy-start.17 = (s32[1,1,1,64,512]{4,3,2,1,0:T(8,128)S(1)}, s32[1,1,1,64,512]{4,3,2,1,0:T(8,128)}, u32[]{:S(2)}) copy-start(s32[1,1,1,64,512]{4,3,2,1,0:T(8,128)} %param.20) | copy-start | bytes 393220
  2.9 8.3 %collective-permute-start = (f32[8,768]{1,0:T(8,128)}, f32[8,768]{1,0:T(8,128)S(1)}, u32[]{:S(2)}, u32[]{:S(2)}) collective-permute-start(f32[8,768]{1,0:T(8,128)} %get-tuple-element.32), channel_id=1, source_target_pairs={{0,64},{64,128},{128,192},{192,0},{1,65},{65,129},{129,193},{193,1... | collective-permute-start | bytes 73736 | tf_op jit(solution)/shard_map/ppermute | solution.py:175
  6.7 5.6 %collective-permute-start.1 = (f32[8,768]{1,0:T(8,128)}, f32[8,768]{1,0:T(8,128)S(1)}, u32[]{:S(2)}, u32[]{:S(2)}) collective-permute-start(f32[8,768]{1,0:T(8,128)} %get-tuple-element.33), channel_id=1, source_target_pairs={{64,0},{128,64},{192,128},{0,192},{65,1},{129,65},{193,129},{1,193... | collective-permute-start | bytes 73736 | tf_op jit(solution)/shard_map/ppermute | solution.py:170
  12.3 1.0 copy-start.2
  13.3 0.9 copy-start.4
  14.2 0.9 copy-start.6
  15.1 0.9 copy-start.8
  16.0 0.9 copy-start.9
  17.0 0.7 copy-start.16
  17.6 28.7 %copy-start.3 = (f32[16,32,128]{2,1,0:T(8,128)S(1)}, f32[16,32,128]{2,1,0:T(8,128)}, u32[]{:S(2)}) copy-start(f32[16,32,128]{2,1,0:T(8,128)} %f0.3) | copy-start | bytes 786436
  18.9 0.7 copy-start.10
  19.6 0.7 copy-start.12
  20.4 12.2 %copy-start.14 = (f32[16,32,128]{2,1,0:T(8,128)}, f32[16,32,128]{2,1,0:T(8,128)S(1)}, u32[]{:S(2)}) copy-start(f32[16,32,128]{2,1,0:T(8,128)S(1)} %get-tuple-element.40.f1) | copy-start | bytes 786436
  20.4 5.1 %collective-permute-start.2 = (f32[34,8,128]{2,1,0:T(8,128)S(1)}, f32[34,8,128]{2,1,0:T(8,128)S(1)}, u32[]{:S(2)}, u32[]{:S(2)}) collective-permute-start(f32[34,8,128]{2,1,0:T(8,128)S(1)} %get-tuple-element.36), channel_id=1, source_target_pairs={{0,1},{1,2},{2,3},{3,0},{4,5},{5,6},{6,7},{7,4},{8,9},{9,10},{10,1... | collective-permute-start | bytes 417800 | tf_op jit(solution)/shard_map/ppermute | solution.py:175
  21.6 3.9 %collective-permute-start.3 = (f32[34,8,128]{2,1,0:T(8,128)S(1)}, f32[34,8,128]{2,1,0:T(8,128)S(1)}, u32[]{:S(2)}, u32[]{:S(2)}) collective-permute-start(f32[34,8,128]{2,1,0:T(8,128)S(1)} %get-tuple-element.37), channel_id=1, source_target_pairs={{1,0},{2,1},{3,2},{0,3},{5,4},{6,5},{7,6},{4,7},{9,8},{10,9},{11,1... | collective-permute-start | bytes 417800 | tf_op jit(solution)/shard_map/ppermute | solution.py:170
  26.2 6.4 %collective-permute-start.4 = (f32[10,24,128]{2,1,0:T(8,128)S(1)}, f32[10,24,128]{2,1,0:T(8,128)S(1)}, u32[]{:S(2)}, u32[]{:S(2)}) collective-permute-start(f32[10,24,128]{2,1,0:T(8,128)S(1)} %get-tuple-element.39), channel_id=1, source_target_pairs={{0,4},{4,8},{8,12},{12,16},{16,20},{20,24},{24,28},{28,32},{32,36}... | collective-permute-start | bytes 368648 | tf_op jit(solution)/shard_map/ppermute | solution.py:175
  32.6 18.5 %copy-start.20 = (s32[1,1,1,64]{3,2,1,0:T(1,128)S(1)}, s32[1,1,1,64]{3,2,1,0:T(1,128)}, u32[]{:S(2)}) copy-start(s32[1,1,1,64]{3,2,1,0:T(1,128)} %param.23) | copy-start | bytes 772
  37.1 17.9 %all-to-all-start = ((f32[64,1,512]{2,1,0:T(1,128)}), f32[64,1,512]{2,1,0:T(1,128)S(1)}, u32[]{:S(2)}, u32[]{:S(2)}) async-start(f32[64,1,512]{2,1,0:T(1,128)} %shard_map.144.sent), calls=%async_computation | async-start | bytes 262144 | tf_op jit(solution)/shard_map/all_to_all | solution.py:179
  46.3 24.5 %copy-start.18 = (f32[5,12]{1,0:T(8,128)S(1)}, f32[5,12]{1,0:T(8,128)}, u32[]{:S(2)}) copy-start(f32[5,12]{1,0:T(8,128)} %param.15) | copy-start | bytes 724
  46.3 1.0 copy-start.11
  47.2 0.9 copy-start.13
  48.2 0.9 copy-start.15
  50.6 20.1 %collective-permute-start.5 = (f32[10,64,128]{2,1,0:T(8,128)}, f32[10,64,128]{2,1,0:T(8,128)S(1)}, u32[]{:S(2)}, u32[]{:S(2)}) collective-permute-start(f32[10,64,128]{2,1,0:T(8,128)} %get-tuple-element.43), channel_id=1, source_target_pairs={{4,0},{8,4},{12,8},{16,12},{20,16},{24,20},{28,24},{32,28},{36,32}... | collective-permute-start | bytes 983048 | tf_op jit(solution)/shard_map/ppermute | solution.py:170
  59.9 5.5 %collective-permute-start.6 = (f32[8,128]{1,0:T(8,128)S(1)}, f32[8,128]{1,0:T(8,128)S(1)}, u32[]{:S(2)}, u32[]{:S(2)}) collective-permute-start(f32[8,128]{1,0:T(8,128)S(1)} %get-tuple-element.46), channel_id=1, source_target_pairs={{0,64},{64,128},{128,192},{192,0},{1,65},{65,129},{129,193},{193,1... | collective-permute-start | bytes 12296 | tf_op jit(solution)/shard_map/ppermute | solution.py:175
  63.8 3.4 %collective-permute-start.7 = (f32[8,128]{1,0:T(8,128)S(1)}, f32[8,128]{1,0:T(8,128)S(1)}, u32[]{:S(2)}, u32[]{:S(2)}) collective-permute-start(f32[8,128]{1,0:T(8,128)S(1)} %get-tuple-element.47), channel_id=1, source_target_pairs={{64,0},{128,64},{192,128},{0,192},{65,1},{129,65},{193,129},{1,193... | collective-permute-start | bytes 12296 | tf_op jit(solution)/shard_map/ppermute | solution.py:170
  63.8 6.9 %collective-permute-start.10 = (f32[10,40,128]{2,1,0:T(8,128)S(1)}, f32[10,40,128]{2,1,0:T(8,128)S(1)}, u32[]{:S(2)}, u32[]{:S(2)}) collective-permute-start(f32[10,40,128]{2,1,0:T(8,128)S(1)} %get-tuple-element.54), channel_id=1, source_target_pairs={{0,4},{4,8},{8,12},{12,16},{16,20},{20,24},{24,28},{28,32},{32,36}... | collective-permute-start | bytes 614408 | tf_op jit(solution)/shard_map/ppermute | solution.py:175
  68.0 6.3 %collective-permute-start.8 = (f32[5,8,128]{2,1,0:T(8,128)S(1)}, f32[5,8,128]{2,1,0:T(8,128)S(1)}, u32[]{:S(2)}, u32[]{:S(2)}) collective-permute-start(f32[5,8,128]{2,1,0:T(8,128)S(1)} %get-tuple-element.50), channel_id=1, source_target_pairs={{0,1},{1,2},{2,3},{3,0},{4,5},{5,6},{6,7},{7,4},{8,9},{9,10},{10,1... | collective-permute-start | bytes 61448 | tf_op jit(solution)/shard_map/ppermute | solution.py:175
  69.3 4.9 %collective-permute-start.9 = (f32[5,8,128]{2,1,0:T(8,128)S(1)}, f32[5,8,128]{2,1,0:T(8,128)S(1)}, u32[]{:S(2)}, u32[]{:S(2)}) collective-permute-start(f32[5,8,128]{2,1,0:T(8,128)S(1)} %get-tuple-element.51), channel_id=1, source_target_pairs={{1,0},{2,1},{3,2},{0,3},{5,4},{6,5},{7,6},{4,7},{9,8},{10,9},{11,1... | collective-permute-start | bytes 61448 | tf_op jit(solution)/shard_map/ppermute | solution.py:170
  74.2 13.6 %copy-start = (f32[10,24,40,128]{3,2,1,0:T(8,128)}, f32[10,24,40,128]{3,2,1,0:T(8,128)S(1)}, u32[]{:S(2)}) copy-start(f32[10,24,40,128]{3,2,1,0:T(8,128)S(1)} %get-tuple-element.55.F) | copy-start | bytes 14745604
  75.0 22.7 %collective-permute-start.11 = (f32[10,40,128]{2,1,0:T(8,128)S(1)}, f32[10,40,128]{2,1,0:T(8,128)S(1)}, u32[]{:S(2)}, u32[]{:S(2)}) collective-permute-start(f32[10,40,128]{2,1,0:T(8,128)S(1)} %get-tuple-element.60), channel_id=1, source_target_pairs={{4,0},{8,4},{12,8},{16,12},{20,16},{24,20},{28,24},{32,28},{36,32}... | collective-permute-start | bytes 614408 | tf_op jit(solution)/shard_map/ppermute | solution.py:170
  87.9 13.8 %all-to-all-start.1 = ((f32[64,1,512]{2,1,0:T(1,128)}), f32[64,1,512]{2,1,0:T(1,128)S(1)}, u32[]{:S(2)}, u32[]{:S(2)}) async-start(f32[64,1,512]{2,1,0:T(1,128)} %get-tuple-element.56), calls=%async_computation.1 | async-start | bytes 262144 | tf_op jit(solution)/shard_map/all_to_all | solution.py:179
  97.6 2.4 %copy-start.1 = (f32[10,24,40,128]{3,2,1,0:T(8,128)S(1)}, f32[10,24,40,128]{3,2,1,0:T(8,128)}, u32[]{:S(2)}) copy-start(f32[10,24,40,128]{3,2,1,0:T(8,128)} %copy-done) | copy-start | bytes 14745604

commit v3 on v2

--- a/solution.py
+++ b/solution.py
@@ -432,7 +432,7 @@
     z_faces([value, weight[...].reshape(index_rows, LANES)], zlo, zhi)
 
 
-def faces_body(E, rxl, rxr, F, middle, cM, cH, aM, aH, bM, bH, vM, vH, iM, iH):
+def faces_body(E, rxl, rxr, F, G, middle, cM, cH, aM, aH, bM, bH, vM, vH, iM, iH):
     uM, uH, fxM, fxH, fyM, fyH, fzM, fzH, dM, dH = (F.at[k] for k in range(10))
     X, rows = E.shape[1], E.shape[2]
     count = X + 2 * W
@@ -486,6 +486,7 @@
         loop(first - reach, last + reach, sweep)
         old, new = new, ((bM, bH) if number == 0 else old)
     middle[...] = old[0][first : last + 1, 0 : middle.shape[1]]
+    G[...] = F[:, last + 1 - W : last + 1 - W + G.shape[1]]
 
 
 def reciprocal(value):
@@ -547,16 +548,13 @@
 
 
 def torso_body(
-    surface, middle, rxr, F, torso_out, G, aM, aH, bM, bH, vM, vH, iM, iH, sem
+    surface, middle, rxr, G, torso_out, aM, aH, bM, bH, vM, vH, iM, iH
 ):
     N, M = surface.shape[0], middle.shape[0]
     X, Y, _ = torso_out.shape
     first = N + M - W
-    copy = pltpu.make_async_copy(F.at[:, pl.ds(first, G.shape[1])], G, sem)
-    copy.start()
     torso_out[0:N] = surface[...]
     torso_out[N : N + M] = middle[...]
-    copy.wait()
     uM, uH, fxM, fxH, fyM, fyH, fzM, fzH, dM, dH = (G.at[k] for k in range(10))
     old, new = (uM, uH), (aM, aH)
     for number, (carry_coef, resid_coef) in enumerate(cheb_coeffs(SWEEPS_T)):
@@ -681,8 +679,11 @@
     big = pltpu.VMEM(text, jnp.float32)
     N = S + SWEEPS_T - 1
     middle_n = TX - S - 2 * (SWEEPS_T - 1)
-    faces, middle = call(
-        faces_body, (f32(10, *text), f32(middle_n, TY, LANES)), 3, scratch=[big] * 10
+    last_n = TX - N - middle_n + 2 * W
+    faces, last_faces, middle = call(
+        faces_body,
+        (f32(10, *text), f32(10, last_n, *text[1:]), f32(middle_n, TY, LANES)),
+        3, scratch=[big] * 10,
     )(torso_wide, txl, xr)
     tall = f32(S + 1, 2 * W, LANES)
     *halos, ylo, yhi = call(
@@ -699,14 +700,11 @@
         scratch=[flat] * 8,
     )(right_wide, recv_index, faces)
     back = swap(returned)
-    last_n = TX - N - middle_n + 2 * W
     thin = pltpu.VMEM((last_n, TY + 2 * W, LANES), jnp.float32)
     torso_out = call(
         torso_body, f32(TX, TY, LANES), 4,
-        scratch=[pltpu.VMEM((10, last_n, TY + 2 * W, LANES), jnp.float32)]
-        + [thin] * 8 + [pltpu.SemaphoreType.DMA(())],
-        left=(3,),
-    )(surface, middle, rxr, faces)
+        scratch=[thin] * 8,
+    )(surface, middle, rxr, last_faces)
     heart_phi = call(
         final_body, f32(X, Y, LANES), 5,
         scratch=[pltpu.VMEM((2 * X // 4 * Y, LANES), jnp.float32)], smem=(0,),

time: 107 us -> 112 us (1.047)
  local copies, waits for them, and re-layouts: 12.1 us -> 17.1 us
  starting transfers between devices: 41.8 us -> 39.5 us
  waiting for transfers between devices: 8.53 us -> 10.7 us
    unnamed x42 -> x70, local copies, waits for them, and re-layouts: 12 us -> 17 us
    ppermute x6, starting transfers between devices: 16.4 us -> 14.5 us  [from_last(): lax.ppermute(value, axis, [(i, (i + 1) % count) for i in range(count)])]
    all_to_all x2, waiting for transfers between devices: 0.01 us -> 1.27 us  [swap(): lax.all_to_all(value, ('gx', 'gy'), split_axis=0, concat_axis=0, tiled=True)]
  transfers between devices with their start and end apart: 14 -> 14, of which waited for: 5 -> 6; matrix products, arithmetic and copies ran while one was open for 3% -> 3% of each run, Pallas kernels for 24% -> 23%
where the time goes in v3:
time: 112 us; the launch traced here: 111 us
  Pallas kernels  39.8 us (36%)
  starting transfers between devices  39.5 us (35%)
  local copies, waits for them, and re-layouts  17.1 us (15%)
  waiting for transfers between devices  10.7 us (10%)
  other arithmetic  2.95 us (3%)
    unnamed x70, local copies, waits for them, and re-layouts  17 us
    ppermute x6, starting transfers between devices, from_last(): lax.ppermute(value, axis, [(i, (i + 1) % count) for i in range(count)])  14.5 us
    all_to_all x2, starting transfers between devices, swap(): lax.all_to_all(value, ('gx', 'gy'), split_axis=0, concat_axis=0, tiled=True)  13.3 us
    ppermute x6, starting transfers between devices, from_next(): lax.ppermute(value, axis, [((i + 1) % count, i) for i in range(count)])  11.7 us
    pallas_call x1, Pallas kernels, per_device(): call(torso_surface_body, (f32(N, TY, LANES), f32(peers, 1, cap)), 3, scra...  6.45 us
    ppermute x6, waiting for transfers between devices, from_last(): lax.ppermute(value, axis, [(i, (i + 1) % count) for i in range(count)])  5.57 us
    pallas_call x1, Pallas kernels, per_device(): call(right_body, (f32(S, TY, LANES), f32(2 * W, S * TY), f32(2 * W, S * T...  4.82 us
    pallas_call x1, Pallas kernels, per_device(): call(final_body, f32(X, Y, LANES), 5, scratch=[pltpu.VMEM((2 * X // 4 * Y...  4.55 us
  transfers between devices with their start and end apart: 14, of which 6 were waited for; matrix products, arithmetic and copies ran while one was open for 3% of the time, Pallas kernels for 23%

profile of v3, /device:TPU:1, one launch (start us, length us, event | category | flops | bytes accessed | tf_op | source)
XLA Modules:
  0.0 111.0 jit_solution(11417682022216597185)
XLA Ops:
  0.7 2.2 %shard_map.139 = (f32[8,768]{1,0:T(8,128)}, f32[8,768]{1,0:T(8,128)}) custom-call(f32[4]{0:T(128)} %table.3, f32[16,16,128]{2,1,0:T(8,128)} %f0.2, f32[16,16,128]{2,1,0:T(8,128)} %f1.1, f32[16,32,128]{2,1,0:T(8,128)} %f0.3, f32[16,32,128]{2,1,0:T(8,128)} %scale.3, s32[16,32,128]{2,1,0:T(8,128)} %labels.3), custom_call_target="tpu_custom_call" | custom-call | tf_op jit(solution)/shard_map/pallas_call | solution.py:634
  2.9 3.8 %collective-permute-start = (f32[8,768]{1,0:T(8,128)}, f32[8,768]{1,0:T(8,128)S(1)}, u32[]{:S(2)}, u32[]{:S(2)}) collective-permute-start(f32[8,768]{1,0:T(8,128)} %get-tuple-element.33), channel_id=1, source_target_pairs={{0,64},{64,128},{128,192},{192,0},{1,65},{65,129},{129,193},{193,1... | collective-permute-start | bytes 73736 | tf_op jit(solution)/shard_map/ppermute | solution.py:175
  6.7 3.0 %collective-permute-start.1 = (f32[8,768]{1,0:T(8,128)}, f32[8,768]{1,0:T(8,128)S(1)}, u32[]{:S(2)}, u32[]{:S(2)}) collective-permute-start(f32[8,768]{1,0:T(8,128)} %get-tuple-element.34), channel_id=1, source_target_pairs={{64,0},{128,64},{192,128},{0,192},{65,1},{129,65},{193,129},{1,193... | collective-permute-start | bytes 73736 | tf_op jit(solution)/shard_map/ppermute | solution.py:170
  9.8 1.3 %collective-permute-done.rl = f32[8,768]{1,0:T(8,128)S(1)} collective-permute-done((f32[8,768]{1,0:T(8,128)}, f32[8,768]{1,0:T(8,128)S(1)}, u32[]{:S(2)}, u32[]{:S(2)}) %collective-permute-start) | collective-permute-done | bytes 24608 | tf_op jit(solution)/shard_map/ppermute | solution.py:175
  11.1 1.2 %collective-permute-done.1.rr = f32[8,768]{1,0:T(8,128)S(1)} collective-permute-done((f32[8,768]{1,0:T(8,128)}, f32[8,768]{1,0:T(8,128)S(1)}, u32[]{:S(2)}, u32[]{:S(2)}) %collective-permute-start.1) | collective-permute-done | bytes 24608 | tf_op jit(solution)/shard_map/ppermute | solution.py:170
  12.3 0.9 copy-done
  13.3 0.9 copy-done.2
  14.2 0.9 copy-done.9
  15.1 0.9 copy-done.11
  16.0 0.9 copy-done.12
  17.6 1.3 %shard_map.140 = (f32[16,16,128]{2,1,0:T(8,128)S(1)}, f32[16,16,128]{2,1,0:T(8,128)S(1)}, f32[16,32,128]{2,1,0:T(8,128)S(1)}, f32[16,32,128]{2,1,0:T(8,128)S(1)}...) custom-call(s32[5]{0:T(128)S(1)} %stack.11.place, f32[4]{0:T(128)S(1)} %copy-done.29, ...), custom_call_target="tpu_custom_call" | custom-call | tf_op jit(solution)/shard_map/pallas_call | solution.py:643
  18.9 0.7 copy-done.15
  19.6 0.7 copy-done.17
  20.3 1.2 %collective-permute-start.2 = (f32[34,8,128]{2,1,0:T(8,128)S(1)}, f32[34,8,128]{2,1,0:T(8,128)S(1)}, u32[]{:S(2)}, u32[]{:S(2)}) collective-permute-start(f32[34,8,128]{2,1,0:T(8,128)S(1)} %get-tuple-element.37), channel_id=1, source_target_pairs={{0,1},{1,2},{2,3},{3,0},{4,5},{5,6},{6,7},{7,4},{8,9},{9,10},{10,1... | collective-permute-start | bytes 417800 | tf_op jit(solution)/shard_map/ppermute | solution.py:175
  21.5 1.5 %collective-permute-start.3 = (f32[34,8,128]{2,1,0:T(8,128)S(1)}, f32[34,8,128]{2,1,0:T(8,128)S(1)}, u32[]{:S(2)}, u32[]{:S(2)}) collective-permute-start(f32[34,8,128]{2,1,0:T(8,128)S(1)} %get-tuple-element.38), channel_id=1, source_target_pairs={{1,0},{2,1},{3,2},{0,3},{5,4},{6,5},{7,6},{4,7},{9,8},{10,9},{11,1... | collective-permute-start | bytes 417800 | tf_op jit(solution)/shard_map/ppermute | solution.py:170
  23.0 2.4 %collective-permute-done.2.ryl = f32[34,8,128]{2,1,0:T(8,128)S(1)} collective-permute-done((f32[34,8,128]{2,1,0:T(8,128)S(1)}, f32[34,8,128]{2,1,0:T(8,128)S(1)}, u32[]{:S(2)}, u32[]{:S(2)}) %collective-permute-start.2) | collective-permute-done | bytes 139296 | tf_op jit(solution)/shard_map/ppermute | solution.py:175
  25.5 0.7 shard_map.141
  26.2 4.5 %collective-permute-start.4 = (f32[10,24,128]{2,1,0:T(8,128)S(1)}, f32[10,24,128]{2,1,0:T(8,128)S(1)}, u32[]{:S(2)}, u32[]{:S(2)}) collective-permute-start(f32[10,24,128]{2,1,0:T(8,128)S(1)} %get-tuple-element.40), channel_id=1, source_target_pairs={{0,4},{4,8},{8,12},{12,16},{16,20},{20,24},{24,28},{28,32},{32,36}... | collective-permute-start | bytes 368648 | tf_op jit(solution)/shard_map/ppermute | solution.py:175
  30.8 1.8 %collective-permute-done.4.rxl = f32[10,24,128]{2,1,0:T(8,128)S(1)} collective-permute-done((f32[10,24,128]{2,1,0:T(8,128)S(1)}, f32[10,24,128]{2,1,0:T(8,128)S(1)}, u32[]{:S(2)}, u32[]{:S(2)}) %collective-permute-start.4) | collective-permute-done | bytes 122912 | tf_op jit(solution)/shard_map/ppermute | solution.py:175
  32.5 4.5 %shard_map.144.sent = f32[64,1,512]{2,1,0:T(1,128)} custom-call(s32[5]{0:T(128)S(1)} %stack.11.place, f32[4,16,24,128]{3,2,1,0:T(8,128)S(1)} %get-tuple-element.39.heart.E, f32[10,24,128]{2,1,0:T(8,128)S(1)} %collective-permute-done.4.rxl, s32[64,512]{1,0:T(8,128)S(1)} %bitcast_select_fusion.1.index), custom_call_target="tpu_custom_call" | custom-call | tf_op jit(solution)/shard_map/pallas_call | solution.py:662
  37.7 9.1 %all-to-all-start = ((f32[64,1,512]{2,1,0:T(1,128)}), f32[64,1,512]{2,1,0:T(1,128)S(1)}, u32[]{:S(2)}, u32[]{:S(2)}) async-start(f32[64,1,512]{2,1,0:T(1,128)} %shard_map.144.sent), calls=%async_computation | async-start | bytes 262144 | tf_op jit(solution)/shard_map/all_to_all | solution.py:179
  46.9 0.9 copy-done.16
  47.8 0.9 copy-done.18
  48.8 0.8 shard_map.142
  49.6 1.1 copy-done.7
  51.2 2.9 %shard_map.145.weight.f1 = f32[4,32,128]{2,1,0:T(8,128)S(1)} custom-call(s32[64,512]{1,0:T(8,128)S(1)} %bitcast_select_fusion.index), custom_call_target="tpu_custom_call" | custom-call | tf_op jit(solution)/shard_map/pallas_call | solution.py:637
  54.1 1.3 %all-to-all-done.arrived = f32[64,1,512]{2,1,0:T(1,128)S(1)} async-done(((f32[64,1,512]{2,1,0:T(1,128)}), f32[64,1,512]{2,1,0:T(1,128)S(1)}, u32[]{:S(2)}, u32[]{:S(2)}) %all-to-all-start) | async-done | bytes 131104 | tf_op jit(solution)/shard_map/all_to_all | solution.py:179
  55.4 4.8 %shard_map.146 = (f32[4,32,128]{2,1,0:T(8,128)S(1)}, f32[8,128]{1,0:T(8,128)S(1)}, f32[8,128]{1,0:T(8,128)S(1)}) custom-call(f32[64,1,512]{2,1,0:T(1,128)S(1)} %all-to-all-done.arrived, s32[64,512]{1,0:T(8,128)S(1)} %bitcast_select_fusion.index, f32[4,32,128]{2,1,0:T(8,128)S(1)} %shard_map.145.weight.f1), custom_call_target="tpu_custom_call" | custom-call | tf_op jit(solution)/shard_map/pallas_call | solution.py:673
  60.2 3.9 %collective-permute-start.6 = (f32[8,128]{1,0:T(8,128)S(1)}, f32[8,128]{1,0:T(8,128)S(1)}, u32[]{:S(2)}, u32[]{:S(2)}) collective-permute-start(f32[8,128]{1,0:T(8,128)S(1)} %get-tuple-element.47), channel_id=1, source_target_pairs={{0,64},{64,128},{128,192},{192,0},{1,65},{65,129},{129,193},{193,1... | collective-permute-start | bytes 12296 | tf_op jit(solution)/shard_map/ppermute | solution.py:175
  64.1 1.0 collective-permute-start.10
  65.1 2.7 %collective-permute-done.7.rr = f32[8,128]{1,0:T(8,128)S(1)} collective-permute-done((f32[8,128]{1,0:T(8,128)S(1)}, f32[8,128]{1,0:T(8,128)S(1)}, u32[]{:S(2)}, u32[]{:S(2)}) %collective-permute-start.7) | collective-permute-done | bytes 4128 | tf_op jit(solution)/shard_map/ppermute | solution.py:170
  67.8 0.8 shard_map.147
  68.7 2.7 %collective-permute-start.9 = (f32[5,8,128]{2,1,0:T(8,128)S(1)}, f32[5,8,128]{2,1,0:T(8,128)S(1)}, u32[]{:S(2)}, u32[]{:S(2)}) collective-permute-start(f32[5,8,128]{2,1,0:T(8,128)S(1)} %get-tuple-element.52), channel_id=1, source_target_pairs={{1,0},{2,1},{3,2},{0,3},{5,4},{6,5},{7,6},{4,7},{9,8},{10,9},{11,1... | collective-permute-start | bytes 61448 | tf_op jit(solution)/shard_map/ppermute | solution.py:170
  72.0 0.7 copy-done.4
  72.7 1.0 copy-done.5
  73.7 1.3 %copy-done.8 = f32[4,16,40,128]{3,2,1,0:T(8,128)S(1)} copy-done((f32[4,16,40,128]{3,2,1,0:T(8,128)S(1)}, f32[4,16,40,128]{3,2,1,0:T(8,128)}, u32[]{:S(2)}) %copy-start.8) | copy-done | bytes 1310744
  75.0 3.6 %shard_map.149 = (f32[10,24,40,128]{3,2,1,0:T(8,128)S(1)}, f32[10,11,40,128]{3,2,1,0:T(8,128)S(1)}, f32[6,32,128]{2,1,0:T(8,128)S(1)}) custom-call(f32[4,16,40,128]{3,2,1,0:T(8,128)S(1)} %copy-done.8, f32[10,40,128]{2,1,0:T(8,128)S(1)} %collective-permute-done.10.rxl, f32[10,64,128]{2,1,0:T(8,128)S(1)} %copy-done.5), custom_call_target="tpu_custom_call" | custom-call | tf_op jit(solution)/shard_map/pallas_call | solution.py:683
  78.6 1.4 %shard_map.148 = (f32[4,4,40,128]{3,2,1,0:T(8,128)S(1)}, f32[10,40,128]{2,1,0:T(8,128)}) custom-call(s32[5]{0:T(128)S(1)} %stack.11.place, f32[4,32,128]{2,1,0:T(8,128)S(1)} %get-tuple-element.46.right.f0, f32[4,32,128]{2,1,0:T(8,128)S(1)} %shard_map.145.weight.f1, f32[4,32,128]{2,1,0:T(8,128)S(1)} %get-tuple-element.49.h0, ...), custom_call_target="tpu_custom_call" | custom-call | tf_op jit(solution)/shard_map/pallas_call | solution.py:693
  80.0 4.1 %collective-permute-start.11 = (f32[10,40,128]{2,1,0:T(8,128)}, f32[10,40,128]{2,1,0:T(8,128)}, u32[]{:S(2)}, u32[]{:S(2)}) collective-permute-start(f32[10,40,128]{2,1,0:T(8,128)} %get-tuple-element.61), channel_id=1, source_target_pairs={{4,0},{8,4},{12,8},{16,12},{20,16},{24,20},{28,24},{32,28},{36,32}... | collective-permute-start | bytes 614408 | tf_op jit(solution)/shard_map/ppermute | solution.py:170
  84.1 6.5 %shard_map.150 = (f32[7,32,128]{2,1,0:T(8,128)S(1)}, f32[64,1,512]{2,1,0:T(1,128)S(1)}) custom-call(f32[4,4,40,128]{3,2,1,0:T(8,128)S(1)} %get-tuple-element.53.R, s32[64,512]{1,0:T(8,128)S(1)} %bitcast_select_fusion.index, f32[10,24,40,128]{3,2,1,0:T(8,128)S(1)} %get-tuple-element.56.F), custom_call_target="tpu_custom_call" | custom-call | tf_op jit(solution)/shard_map/pallas_call | solution.py:698
  91.9 4.2 %all-to-all-start.1 = ((f32[64,1,512]{2,1,0:T(1,128)}), f32[64,1,512]{2,1,0:T(1,128)S(1)}, u32[]{:S(2)}, u32[]{:S(2)}) async-start(f32[64,1,512]{2,1,0:T(1,128)} %copy-done.19), calls=%async_computation.1 | async-start | bytes 262144 | tf_op jit(solution)/shard_map/all_to_all | solution.py:179
  96.1 2.2 %multiply_reduce_fusion.current = f32[16,16,128]{2,1,0:T(8,128)S(1)} fusion(bf16[12,16,16,128]{3,2,1,0:T(8,128)(2,1)} %param.12, f32[12]{0:T(128)} %get-tuple-element.66, f32[12]{0:T(128)} %get-tuple-element.67, f32[12]{0:T(128)} %get-tuple-element.64, f32[12]{0:T(128)} %get-tuple-element.65, f32[16,16,128]{2,1,0:T(8,128)S(1)} %copy-done.3, f32[12]{0:T(128)} %get-tuple-element.63), kind=kLoop, calls=%fused_computation | loop fusion | flops 5079040 | bytes 1048816 | tf_op jit(solution)/shard_map/reduce_sum | solution.py:613
  98.3 1.0 copy-done.6
  99.3 0.7 copy-done.27
  100.0 3.4 %shard_map.143 = (f32[16,16,128]{2,1,0:T(8,128)S(1)}, f32[16,16,128]{2,1,0:T(8,128)}) custom-call(s32[5]{0:T(128)S(1)} %copy-done.27, f32[16,16,128]{2,1,0:T(8,128)S(1)} %multiply_reduce_fusion.current, f32[4,16,24,128]{3,2,1,0:T(8,128)S(1)} %get-tuple-element.39.heart.E, f32[10,24,128]{2,1,0:T(8,128)S(1)} %copy-done.14, f32[10,64,128]{2,1,0:T(8,128)S(1)} %copy-done.6), custom_call_target="tpu_custom_call" | custom-call | tf_op jit(solution)/shard_map/pallas_call | solution.py:669
  103.4 0.7 copy-done.20
  104.1 2.4 %shard_map.152 = f32[16,32,128]{2,1,0:T(8,128)} custom-call(f32[7,32,128]{2,1,0:T(8,128)S(1)} %copy-done.23, f32[6,32,128]{2,1,0:T(8,128)S(1)} %copy-done.25, f32[10,40,128]{2,1,0:T(8,128)} %collective-permute-done.11.rxr, f32[10,11,40,128]{3,2,1,0:T(8,128)S(1)} %get-tuple-element.62.G), custom_call_target="tpu_custom_call" | custom-call | tf_op jit(solution)/shard_map/pallas_call | solution.py:704
  106.4 4.6 %shard_map.151 = f32[16,16,128]{2,1,0:T(8,128)} custom-call(s32[5]{0:T(128)S(1)} %copy-done.28, f32[64,1,512]{2,1,0:T(1,128)} %shard_map.144.sent, f32[64,1,512]{2,1,0:T(1,128)S(1)} %all-to-all-done.1.back, s32[64,512]{1,0:T(8,128)S(1)} %bitcast_select_fusion.1.index, f32[16,16,128]{2,1,0:T(8,128)S(1)} %copy-done.21), custom_call_target="tpu_custom_call" | custom-call | tf_op jit(solution)/shard_map/pallas_call | solution.py:708
  (69 shorter events, 4.1 us)
Async XLA Ops:
  0.6 24.8 %copy-start.3 = (f32[16,16,128]{2,1,0:T(8,128)S(1)}, f32[16,16,128]{2,1,0:T(8,128)}, u32[]{:S(2)}) copy-start(f32[16,16,128]{2,1,0:T(8,128)} %f0.2) | copy-start | bytes 393220
  0.6 24.8 %copy-start.10 = (f32[16,16,128]{2,1,0:T(8,128)S(1)}, f32[16,16,128]{2,1,0:T(8,128)}, u32[]{:S(2)}) copy-start(f32[16,16,128]{2,1,0:T(8,128)} %f1.1) | copy-start | bytes 393220
  0.7 30.0 %copy-start.33 = (s32[1,1,1,64]{3,2,1,0:T(1,128)S(1)}, s32[1,1,1,64]{3,2,1,0:T(1,128)}, u32[]{:S(2)}) copy-start(s32[1,1,1,64]{3,2,1,0:T(1,128)} %param.21) | copy-start | bytes 772
  0.7 30.0 %copy-start.30 = (s32[1,1,1,64,512]{4,3,2,1,0:T(8,128)S(1)}, s32[1,1,1,64,512]{4,3,2,1,0:T(8,128)}, u32[]{:S(2)}) copy-start(s32[1,1,1,64,512]{4,3,2,1,0:T(8,128)} %param.20) | copy-start | bytes 393220
  2.9 8.3 %collective-permute-start = (f32[8,768]{1,0:T(8,128)}, f32[8,768]{1,0:T(8,128)S(1)}, u32[]{:S(2)}, u32[]{:S(2)}) collective-permute-start(f32[8,768]{1,0:T(8,128)} %get-tuple-element.33), channel_id=1, source_target_pairs={{0,64},{64,128},{128,192},{192,0},{1,65},{65,129},{129,193},{193,1... | collective-permute-start | bytes 73736 | tf_op jit(solution)/shard_map/ppermute | solution.py:175
  6.7 5.6 %collective-permute-start.1 = (f32[8,768]{1,0:T(8,128)}, f32[8,768]{1,0:T(8,128)S(1)}, u32[]{:S(2)}, u32[]{:S(2)}) collective-permute-start(f32[8,768]{1,0:T(8,128)} %get-tuple-element.34), channel_id=1, source_target_pairs={{64,0},{128,64},{192,128},{0,192},{65,1},{129,65},{193,129},{1,193... | collective-permute-start | bytes 73736 | tf_op jit(solution)/shard_map/ppermute | solution.py:170
  9.8 68.8 %copy-start.26 = (s32[5]{0:T(128)}, s32[5]{0:T(128)S(1)}, u32[]{:S(2)}) copy-start(s32[5]{0:T(128)S(1)} %stack.11.place) | copy-start | bytes 64
  12.3 1.0 copy-start
  13.3 0.9 copy-start.2
  14.2 0.9 copy-start.9
  15.1 0.9 copy-start.11
  16.0 0.9 copy-start.12
  17.0 0.7 copy-start.29
  17.6 29.2 %copy-start.1 = (f32[16,32,128]{2,1,0:T(8,128)S(1)}, f32[16,32,128]{2,1,0:T(8,128)}, u32[]{:S(2)}) copy-start(f32[16,32,128]{2,1,0:T(8,128)} %f0.3) | copy-start | bytes 786436
  18.9 0.7 copy-start.15
  19.6 0.7 copy-start.17
  20.3 5.1 %collective-permute-start.2 = (f32[34,8,128]{2,1,0:T(8,128)S(1)}, f32[34,8,128]{2,1,0:T(8,128)S(1)}, u32[]{:S(2)}, u32[]{:S(2)}) collective-permute-start(f32[34,8,128]{2,1,0:T(8,128)S(1)} %get-tuple-element.37), channel_id=1, source_target_pairs={{0,1},{1,2},{2,3},{3,0},{4,5},{5,6},{6,7},{7,4},{8,9},{9,10},{10,1... | collective-permute-start | bytes 417800 | tf_op jit(solution)/shard_map/ppermute | solution.py:175
  21.5 3.9 %collective-permute-start.3 = (f32[34,8,128]{2,1,0:T(8,128)S(1)}, f32[34,8,128]{2,1,0:T(8,128)S(1)}, u32[]{:S(2)}, u32[]{:S(2)}) collective-permute-start(f32[34,8,128]{2,1,0:T(8,128)S(1)} %get-tuple-element.38), channel_id=1, source_target_pairs={{1,0},{2,1},{3,2},{0,3},{5,4},{6,5},{7,6},{4,7},{9,8},{10,9},{11,1... | collective-permute-start | bytes 417800 | tf_op jit(solution)/shard_map/ppermute | solution.py:170
  26.2 6.4 %collective-permute-start.4 = (f32[10,24,128]{2,1,0:T(8,128)S(1)}, f32[10,24,128]{2,1,0:T(8,128)S(1)}, u32[]{:S(2)}, u32[]{:S(2)}) collective-permute-start(f32[10,24,128]{2,1,0:T(8,128)S(1)} %get-tuple-element.40), channel_id=1, source_target_pairs={{0,4},{4,8},{8,12},{12,16},{16,20},{20,24},{24,28},{28,32},{32,36}... | collective-permute-start | bytes 368648 | tf_op jit(solution)/shard_map/ppermute | solution.py:175
  32.5 18.6 %copy-start.31 = (s32[1,1,1,64,512]{4,3,2,1,0:T(8,128)S(1)}, s32[1,1,1,64,512]{4,3,2,1,0:T(8,128)}, u32[]{:S(2)}) copy-start(s32[1,1,1,64,512]{4,3,2,1,0:T(8,128)} %param.22) | copy-start | bytes 393220
  32.5 18.6 %copy-start.34 = (s32[1,1,1,64]{3,2,1,0:T(1,128)S(1)}, s32[1,1,1,64]{3,2,1,0:T(1,128)}, u32[]{:S(2)}) copy-start(s32[1,1,1,64]{3,2,1,0:T(1,128)} %param.23) | copy-start | bytes 772
  37.1 0.6 copy-start.13
  37.7 17.7 %all-to-all-start = ((f32[64,1,512]{2,1,0:T(1,128)}), f32[64,1,512]{2,1,0:T(1,128)S(1)}, u32[]{:S(2)}, u32[]{:S(2)}) async-start(f32[64,1,512]{2,1,0:T(1,128)} %shard_map.144.sent), calls=%async_computation | async-start | bytes 262144 | tf_op jit(solution)/shard_map/all_to_all | solution.py:179
  46.8 24.5 %copy-start.32 = (f32[5,12]{1,0:T(8,128)S(1)}, f32[5,12]{1,0:T(8,128)}, u32[]{:S(2)}) copy-start(f32[5,12]{1,0:T(8,128)} %param.15) | copy-start | bytes 724
  46.9 1.0 copy-start.16
  47.8 0.9 copy-start.18
  49.5 1.1 copy-start.7
  50.6 21.3 %collective-permute-start.5 = (f32[10,64,128]{2,1,0:T(8,128)S(1)}, f32[10,64,128]{2,1,0:T(8,128)S(1)}, u32[]{:S(2)}, u32[]{:S(2)}) collective-permute-start(f32[10,64,128]{2,1,0:T(8,128)S(1)} %get-tuple-element.44), channel_id=1, source_target_pairs={{4,0},{8,4},{12,8},{16,12},{20,16},{24,20},{28,24},{32,28},{36,32}... | collective-permute-start | bytes 983048 | tf_op jit(solution)/shard_map/ppermute | solution.py:170
  60.2 4.9 %collective-permute-start.6 = (f32[8,128]{1,0:T(8,128)S(1)}, f32[8,128]{1,0:T(8,128)S(1)}, u32[]{:S(2)}, u32[]{:S(2)}) collective-permute-start(f32[8,128]{1,0:T(8,128)S(1)} %get-tuple-element.47), channel_id=1, source_target_pairs={{0,64},{64,128},{128,192},{192,0},{1,65},{65,129},{129,193},{193,1... | collective-permute-start | bytes 12296 | tf_op jit(solution)/shard_map/ppermute | solution.py:175
  64.1 3.7 %collective-permute-start.7 = (f32[8,128]{1,0:T(8,128)S(1)}, f32[8,128]{1,0:T(8,128)S(1)}, u32[]{:S(2)}, u32[]{:S(2)}) collective-permute-start(f32[8,128]{1,0:T(8,128)S(1)} %get-tuple-element.48), channel_id=1, source_target_pairs={{64,0},{128,64},{192,128},{0,192},{65,1},{129,65},{193,129},{1,193... | collective-permute-start | bytes 12296 | tf_op jit(solution)/shard_map/ppermute | solution.py:170
  64.1 7.8 %collective-permute-start.10 = (f32[10,40,128]{2,1,0:T(8,128)S(1)}, f32[10,40,128]{2,1,0:T(8,128)S(1)}, u32[]{:S(2)}, u32[]{:S(2)}) collective-permute-start(f32[10,40,128]{2,1,0:T(8,128)S(1)} %get-tuple-element.55), channel_id=1, source_target_pairs={{0,4},{4,8},{8,12},{12,16},{16,20},{20,24},{24,28},{28,32},{32,36}... | collective-permute-start | bytes 614408 | tf_op jit(solution)/shard_map/ppermute | solution.py:175
  68.6 9.9 %collective-permute-start.8 = (f32[5,8,128]{2,1,0:T(8,128)S(1)}, f32[5,8,128]{2,1,0:T(8,128)S(1)}, u32[]{:S(2)}, u32[]{:S(2)}) collective-permute-start(f32[5,8,128]{2,1,0:T(8,128)S(1)} %get-tuple-element.51), channel_id=1, source_target_pairs={{0,1},{1,2},{2,3},{3,0},{4,5},{5,6},{6,7},{7,4},{8,9},{9,10},{10,1... | collective-permute-start | bytes 61448 | tf_op jit(solution)/shard_map/ppermute | solution.py:175
  68.7 9.9 %collective-permute-start.9 = (f32[5,8,128]{2,1,0:T(8,128)S(1)}, f32[5,8,128]{2,1,0:T(8,128)S(1)}, u32[]{:S(2)}, u32[]{:S(2)}) collective-permute-start(f32[5,8,128]{2,1,0:T(8,128)S(1)} %get-tuple-element.52), channel_id=1, source_target_pairs={{1,0},{2,1},{3,2},{0,3},{5,4},{6,5},{7,6},{4,7},{9,8},{10,9},{11,1... | collective-permute-start | bytes 61448 | tf_op jit(solution)/shard_map/ppermute | solution.py:170
  72.0 0.7 copy-start.4
  72.7 1.0 copy-start.5
  73.7 1.3 %copy-start.8 = (f32[4,16,40,128]{3,2,1,0:T(8,128)S(1)}, f32[4,16,40,128]{3,2,1,0:T(8,128)}, u32[]{:S(2)}) copy-start(f32[4,16,40,128]{3,2,1,0:T(8,128)} %copy-done.7) | copy-start | bytes 3932164
  78.6 12.0 %copy-start.24 = (f32[6,32,128]{2,1,0:T(8,128)}, f32[6,32,128]{2,1,0:T(8,128)S(1)}, u32[]{:S(2)}) copy-start(f32[6,32,128]{2,1,0:T(8,128)S(1)} %get-tuple-element.60.middle) | copy-start | bytes 294916
  80.0 24.1 %collective-permute-start.11 = (f32[10,40,128]{2,1,0:T(8,128)}, f32[10,40,128]{2,1,0:T(8,128)}, u32[]{:S(2)}, u32[]{:S(2)}) collective-permute-start(f32[10,40,128]{2,1,0:T(8,128)} %get-tuple-element.61), channel_id=1, source_target_pairs={{4,0},{8,4},{12,8},{16,12},{20,16},{24,20},{28,24},{32,28},{36,32}... | collective-permute-start | bytes 614408 | tf_op jit(solution)/shard_map/ppermute | solution.py:170
  84.1 14.2 %copy-start.14 = (f32[10,24,128]{2,1,0:T(8,128)S(1)}, f32[10,24,128]{2,1,0:T(8,128)}, u32[]{:S(2)}) copy-start(f32[10,24,128]{2,1,0:T(8,128)} %copy-done.13) | copy-start | bytes 368644
  90.6 0.7 copy-start.19
  91.9 14.6 %all-to-all-start.1 = ((f32[64,1,512]{2,1,0:T(1,128)}), f32[64,1,512]{2,1,0:T(1,128)S(1)}, u32[]{:S(2)}, u32[]{:S(2)}) async-start(f32[64,1,512]{2,1,0:T(1,128)} %copy-done.19), calls=%async_computation.1 | async-start | bytes 262144 | tf_op jit(solution)/shard_map/all_to_all | solution.py:179
  96.1 8.0 %copy-start.23 = (f32[7,32,128]{2,1,0:T(8,128)S(1)}, f32[7,32,128]{2,1,0:T(8,128)}, u32[]{:S(2)}) copy-start(f32[7,32,128]{2,1,0:T(8,128)} %copy-done.22) | copy-start | bytes 344068
  96.1 8.0 %copy-start.25 = (f32[6,32,128]{2,1,0:T(8,128)S(1)}, f32[6,32,128]{2,1,0:T(8,128)}, u32[]{:S(2)}) copy-start(f32[6,32,128]{2,1,0:T(8,128)} %copy-done.24) | copy-start | bytes 294916
  98.3 1.0 copy-start.6
  99.3 0.7 copy-start.27
  103.4 0.7 copy-start.20
  104.0 2.4 %copy-start.28 = (s32[5]{0:T(128)S(1)}, s32[5]{0:T(128)}, u32[]{:S(2)}) copy-start(s32[5]{0:T(128)} %copy-done.26) | copy-start | bytes 64
  104.0 2.4 %copy-start.21 = (f32[16,16,128]{2,1,0:T(8,128)S(1)}, f32[16,16,128]{2,1,0:T(8,128)}, u32[]{:S(2)}) copy-start(f32[16,16,128]{2,1,0:T(8,128)} %copy-done.20) | copy-start | bytes 393220
  (1 other events, 0.6 us)

commit v4 on v3

--- a/solution.py
+++ b/solution.py
@@ -242,7 +242,7 @@
 def gather_rows(table, index, out):
     rows_n = table.shape[0]
 
-    def tile(i, carry):
+    def tile(i):
         top = pl.multiple_of(i * 8, 8)
         for j in range(index.shape[1] // LANES):
             spot = (pl.ds(top, 8), slice(j * LANES, (j + 1) * LANES))
@@ -254,9 +254,8 @@
                 got = jnp.take_along_axis(line, cols, axis=1, mode="promise_in_bounds")
                 total = jnp.where(rows == r, got, total)
             out[spot[0], 0, spot[1]] = total
-        return carry
-
-    lax.fori_loop(0, index.shape[0] // 8, tile, 0)
+
+    loop(0, index.shape[0] // 8 - 1, tile, 2)
 
 
 def scatter_rows(value_of, index, rows_n, total, batch):
@@ -324,7 +323,7 @@
 
 
 def weight_body(index, weight, total):
-    scatter_rows(None, index, total.shape[0], total, 2)
+    scatter_rows(None, index, total.shape[0], total, 4)
     weight[...] = (penalty * total[...]).reshape(weight.shape)
 
 
@@ -426,7 +425,7 @@
 
 def right_body(arrived, index, weight, right, zlo, zhi, total):
     rows = index_rows = weight.shape[0] * weight.shape[1]
-    scatter_rows(lambda s: arrived[pl.ds(s, 1), 0, :], index, rows, total, 4)
+    scatter_rows(lambda s: arrived[pl.ds(s, 1), 0, :], index, rows, total, 8)
     value = penalty * (total[0:rows] + total[rows : 2 * rows])
     right[...] = value.reshape(right.shape)
     z_faces([value, weight[...].reshape(index_rows, LANES)], zlo, zhi)
@@ -594,7 +593,7 @@
     X, Y, _ = phi.shape
     rows = X // 4 * Y
     scatter_rows(
-        lambda s: penalty * (sent[pl.ds(s, 1), 0, :] - back[pl.ds(s, 1), 0, :]), index, rows, total, 2
+        lambda s: penalty * (sent[pl.ds(s, 1), 0, :] - back[pl.ds(s, 1), 0, :]), index, rows, total, 4
     )
     flux = (total[0:rows] + total[rows : 2 * rows]).reshape(X // 4, Y, LANES)
     (dm, _, _), _ = heart_tiles(place, Y)

time: 112 us -> 110 us (0.982)
  Pallas kernels: 39.8 us -> 37.9 us
  transfers between devices with their start and end apart: 14 -> 14, of which waited for: 6 -> 6; matrix products, arithmetic and copies ran while one was open for 3% -> 3% of each run, Pallas kernels for 23% -> 22%
where the time goes in v4:
time: 110 us; the launch traced here: 109 us
  starting transfers between devices  39.3 us (36%)
  Pallas kernels  37.9 us (34%)
  local copies, waits for them, and re-layouts  17.1 us (16%)
  waiting for transfers between devices  10.9 us (10%)
  other arithmetic  2.95 us (3%)
    unnamed x70, local copies, waits for them, and re-layouts  17 us
    ppermute x6, starting transfers between devices, from_last(): lax.ppermute(value, axis, [(i, (i + 1) % count) for i in range(count)])  14.6 us
    all_to_all x2, starting transfers between devices, swap(): lax.all_to_all(value, ('gx', 'gy'), split_axis=0, concat_axis=0, tiled=True)  13.3 us
    ppermute x6, starting transfers between devices, from_next(): lax.ppermute(value, axis, [((i + 1) % count, i) for i in range(count)])  11.4 us
    pallas_call x1, Pallas kernels, per_device(): call(torso_surface_body, (f32(N, TY, LANES), f32(peers, 1, cap)), 3, scra...  6 us
    ppermute x6, waiting for transfers between devices, from_last(): lax.ppermute(value, axis, [(i, (i + 1) % count) for i in range(count)])  5.57 us
    pallas_call x1, Pallas kernels, per_device(): call(right_body, (f32(S, TY, LANES), f32(2 * W, S * TY), f32(2 * W, S * T...  4.54 us
    pallas_call x1, Pallas kernels, per_device(): call(final_body, f32(X, Y, LANES), 5, scratch=[pltpu.VMEM((2 * X // 4 * Y...  4.18 us
  transfers between devices with their start and end apart: 14, of which 6 were waited for; matrix products, arithmetic and copies ran while one was open for 3% of the time, Pallas kernels for 22%

profile of v4, /device:TPU:1, one launch (start us, length us, event | category | flops | bytes accessed | tf_op | source)
XLA Modules:
  0.0 109.1 jit_solution(5243518662372838021)
XLA Ops:
  0.7 2.2 %shard_map.139 = (f32[8,768]{1,0:T(8,128)}, f32[8,768]{1,0:T(8,128)}) custom-call(f32[4]{0:T(128)} %table.3, f32[16,16,128]{2,1,0:T(8,128)} %f0.2, f32[16,16,128]{2,1,0:T(8,128)} %f1.1, f32[16,32,128]{2,1,0:T(8,128)} %f0.3, f32[16,32,128]{2,1,0:T(8,128)} %scale.3, s32[16,32,128]{2,1,0:T(8,128)} %labels.3), custom_call_target="tpu_custom_call" | custom-call | tf_op jit(solution)/shard_map/pallas_call | solution.py:633
  2.9 3.8 %collective-permute-start = (f32[8,768]{1,0:T(8,128)}, f32[8,768]{1,0:T(8,128)S(1)}, u32[]{:S(2)}, u32[]{:S(2)}) collective-permute-start(f32[8,768]{1,0:T(8,128)} %get-tuple-element.33), channel_id=1, source_target_pairs={{0,64},{64,128},{128,192},{192,0},{1,65},{65,129},{129,193},{193,1... | collective-permute-start | bytes 73736 | tf_op jit(solution)/shard_map/ppermute | solution.py:175
  6.7 3.0 %collective-permute-start.1 = (f32[8,768]{1,0:T(8,128)}, f32[8,768]{1,0:T(8,128)S(1)}, u32[]{:S(2)}, u32[]{:S(2)}) collective-permute-start(f32[8,768]{1,0:T(8,128)} %get-tuple-element.34), channel_id=1, source_target_pairs={{64,0},{128,64},{192,128},{0,192},{65,1},{129,65},{193,129},{1,193... | collective-permute-start | bytes 73736 | tf_op jit(solution)/shard_map/ppermute | solution.py:170
  9.8 1.3 %collective-permute-done.rl = f32[8,768]{1,0:T(8,128)S(1)} collective-permute-done((f32[8,768]{1,0:T(8,128)}, f32[8,768]{1,0:T(8,128)S(1)}, u32[]{:S(2)}, u32[]{:S(2)}) %collective-permute-start) | collective-permute-done | bytes 24608 | tf_op jit(solution)/shard_map/ppermute | solution.py:175
  11.1 1.2 %collective-permute-done.1.rr = f32[8,768]{1,0:T(8,128)S(1)} collective-permute-done((f32[8,768]{1,0:T(8,128)}, f32[8,768]{1,0:T(8,128)S(1)}, u32[]{:S(2)}, u32[]{:S(2)}) %collective-permute-start.1) | collective-permute-done | bytes 24608 | tf_op jit(solution)/shard_map/ppermute | solution.py:170
  12.3 0.9 copy-done
  13.3 0.9 copy-done.2
  14.2 0.9 copy-done.9
  15.1 0.9 copy-done.11
  16.0 0.9 copy-done.12
  17.6 1.3 %shard_map.140 = (f32[16,16,128]{2,1,0:T(8,128)S(1)}, f32[16,16,128]{2,1,0:T(8,128)S(1)}, f32[16,32,128]{2,1,0:T(8,128)S(1)}, f32[16,32,128]{2,1,0:T(8,128)S(1)}...) custom-call(s32[5]{0:T(128)S(1)} %stack.11.place, f32[4]{0:T(128)S(1)} %copy-done.29, ...), custom_call_target="tpu_custom_call" | custom-call | tf_op jit(solution)/shard_map/pallas_call | solution.py:642
  18.9 0.7 copy-done.15
  19.6 0.7 copy-done.17
  20.3 1.2 %collective-permute-start.2 = (f32[34,8,128]{2,1,0:T(8,128)S(1)}, f32[34,8,128]{2,1,0:T(8,128)S(1)}, u32[]{:S(2)}, u32[]{:S(2)}) collective-permute-start(f32[34,8,128]{2,1,0:T(8,128)S(1)} %get-tuple-element.37), channel_id=1, source_target_pairs={{0,1},{1,2},{2,3},{3,0},{4,5},{5,6},{6,7},{7,4},{8,9},{9,10},{10,1... | collective-permute-start | bytes 417800 | tf_op jit(solution)/shard_map/ppermute | solution.py:175
  21.5 1.5 %collective-permute-start.3 = (f32[34,8,128]{2,1,0:T(8,128)S(1)}, f32[34,8,128]{2,1,0:T(8,128)S(1)}, u32[]{:S(2)}, u32[]{:S(2)}) collective-permute-start(f32[34,8,128]{2,1,0:T(8,128)S(1)} %get-tuple-element.38), channel_id=1, source_target_pairs={{1,0},{2,1},{3,2},{0,3},{5,4},{6,5},{7,6},{4,7},{9,8},{10,9},{11,1... | collective-permute-start | bytes 417800 | tf_op jit(solution)/shard_map/ppermute | solution.py:170
  23.0 2.4 %collective-permute-done.2.ryl = f32[34,8,128]{2,1,0:T(8,128)S(1)} collective-permute-done((f32[34,8,128]{2,1,0:T(8,128)S(1)}, f32[34,8,128]{2,1,0:T(8,128)S(1)}, u32[]{:S(2)}, u32[]{:S(2)}) %collective-permute-start.2) | collective-permute-done | bytes 139296 | tf_op jit(solution)/shard_map/ppermute | solution.py:175
  25.5 0.7 shard_map.141
  26.2 4.5 %collective-permute-start.4 = (f32[10,24,128]{2,1,0:T(8,128)S(1)}, f32[10,24,128]{2,1,0:T(8,128)S(1)}, u32[]{:S(2)}, u32[]{:S(2)}) collective-permute-start(f32[10,24,128]{2,1,0:T(8,128)S(1)} %get-tuple-element.40), channel_id=1, source_target_pairs={{0,4},{4,8},{8,12},{12,16},{16,20},{20,24},{24,28},{28,32},{32,36}... | collective-permute-start | bytes 368648 | tf_op jit(solution)/shard_map/ppermute | solution.py:175
  30.8 1.8 %collective-permute-done.4.rxl = f32[10,24,128]{2,1,0:T(8,128)S(1)} collective-permute-done((f32[10,24,128]{2,1,0:T(8,128)S(1)}, f32[10,24,128]{2,1,0:T(8,128)S(1)}, u32[]{:S(2)}, u32[]{:S(2)}) %collective-permute-start.4) | collective-permute-done | bytes 122912 | tf_op jit(solution)/shard_map/ppermute | solution.py:175
  32.5 4.1 %shard_map.144.sent = f32[64,1,512]{2,1,0:T(1,128)} custom-call(s32[5]{0:T(128)S(1)} %stack.11.place, f32[4,16,24,128]{3,2,1,0:T(8,128)S(1)} %get-tuple-element.39.heart.E, f32[10,24,128]{2,1,0:T(8,128)S(1)} %collective-permute-done.4.rxl, s32[64,512]{1,0:T(8,128)S(1)} %bitcast_select_fusion.1.index), custom_call_target="tpu_custom_call" | custom-call | tf_op jit(solution)/shard_map/pallas_call | solution.py:661
  37.2 9.1 %all-to-all-start = ((f32[64,1,512]{2,1,0:T(1,128)}), f32[64,1,512]{2,1,0:T(1,128)S(1)}, u32[]{:S(2)}, u32[]{:S(2)}) async-start(f32[64,1,512]{2,1,0:T(1,128)} %shard_map.144.sent), calls=%async_computation | async-start | bytes 262144 | tf_op jit(solution)/shard_map/all_to_all | solution.py:179
  46.4 0.9 copy-done.16
  47.4 0.9 copy-done.18
  48.3 0.8 shard_map.142
  49.1 1.1 copy-done.7
  50.7 2.6 %shard_map.145.weight.f1 = f32[4,32,128]{2,1,0:T(8,128)S(1)} custom-call(s32[64,512]{1,0:T(8,128)S(1)} %bitcast_select_fusion.index), custom_call_target="tpu_custom_call" | custom-call | tf_op jit(solution)/shard_map/pallas_call | solution.py:636
  53.3 1.6 %all-to-all-done.arrived = f32[64,1,512]{2,1,0:T(1,128)S(1)} async-done(((f32[64,1,512]{2,1,0:T(1,128)}), f32[64,1,512]{2,1,0:T(1,128)S(1)}, u32[]{:S(2)}, u32[]{:S(2)}) %all-to-all-start) | async-done | bytes 131104 | tf_op jit(solution)/shard_map/all_to_all | solution.py:179
  54.9 4.5 %shard_map.146 = (f32[4,32,128]{2,1,0:T(8,128)S(1)}, f32[8,128]{1,0:T(8,128)S(1)}, f32[8,128]{1,0:T(8,128)S(1)}) custom-call(f32[64,1,512]{2,1,0:T(1,128)S(1)} %all-to-all-done.arrived, s32[64,512]{1,0:T(8,128)S(1)} %bitcast_select_fusion.index, f32[4,32,128]{2,1,0:T(8,128)S(1)} %shard_map.145.weight.f1), custom_call_target="tpu_custom_call" | custom-call | tf_op jit(solution)/shard_map/pallas_call | solution.py:672
  59.5 3.9 %collective-permute-start.6 = (f32[8,128]{1,0:T(8,128)S(1)}, f32[8,128]{1,0:T(8,128)S(1)}, u32[]{:S(2)}, u32[]{:S(2)}) collective-permute-start(f32[8,128]{1,0:T(8,128)S(1)} %get-tuple-element.47), channel_id=1, source_target_pairs={{0,64},{64,128},{128,192},{192,0},{1,65},{65,129},{129,193},{193,1... | collective-permute-start | bytes 12296 | tf_op jit(solution)/shard_map/ppermute | solution.py:175
  63.4 1.0 collective-permute-start.10
  64.4 2.6 %collective-permute-done.7.rr = f32[8,128]{1,0:T(8,128)S(1)} collective-permute-done((f32[8,128]{1,0:T(8,128)S(1)}, f32[8,128]{1,0:T(8,128)S(1)}, u32[]{:S(2)}, u32[]{:S(2)}) %collective-permute-start.7) | collective-permute-done | bytes 4128 | tf_op jit(solution)/shard_map/ppermute | solution.py:170
  66.9 0.8 shard_map.147
  67.9 2.6 %collective-permute-start.9 = (f32[5,8,128]{2,1,0:T(8,128)S(1)}, f32[5,8,128]{2,1,0:T(8,128)S(1)}, u32[]{:S(2)}, u32[]{:S(2)}) collective-permute-start(f32[5,8,128]{2,1,0:T(8,128)S(1)} %get-tuple-element.52), channel_id=1, source_target_pairs={{1,0},{2,1},{3,2},{0,3},{5,4},{6,5},{7,6},{4,7},{9,8},{10,9},{11,1... | collective-permute-start | bytes 61448 | tf_op jit(solution)/shard_map/ppermute | solution.py:170
  71.1 0.7 copy-done.4
  71.9 1.0 copy-done.5
  72.8 1.3 %copy-done.8 = f32[4,16,40,128]{3,2,1,0:T(8,128)S(1)} copy-done((f32[4,16,40,128]{3,2,1,0:T(8,128)S(1)}, f32[4,16,40,128]{3,2,1,0:T(8,128)}, u32[]{:S(2)}) %copy-start.8) | copy-done | bytes 1310744
  74.1 3.6 %shard_map.149 = (f32[10,24,40,128]{3,2,1,0:T(8,128)S(1)}, f32[10,11,40,128]{3,2,1,0:T(8,128)S(1)}, f32[6,32,128]{2,1,0:T(8,128)S(1)}) custom-call(f32[4,16,40,128]{3,2,1,0:T(8,128)S(1)} %copy-done.8, f32[10,40,128]{2,1,0:T(8,128)S(1)} %collective-permute-done.10.rxl, f32[10,64,128]{2,1,0:T(8,128)S(1)} %copy-done.5), custom_call_target="tpu_custom_call" | custom-call | tf_op jit(solution)/shard_map/pallas_call | solution.py:682
  77.8 1.4 %shard_map.148 = (f32[4,4,40,128]{3,2,1,0:T(8,128)S(1)}, f32[10,40,128]{2,1,0:T(8,128)}) custom-call(s32[5]{0:T(128)S(1)} %stack.11.place, f32[4,32,128]{2,1,0:T(8,128)S(1)} %get-tuple-element.46.right.f0, f32[4,32,128]{2,1,0:T(8,128)S(1)} %shard_map.145.weight.f1, f32[4,32,128]{2,1,0:T(8,128)S(1)} %get-tuple-element.49.h0, ...), custom_call_target="tpu_custom_call" | custom-call | tf_op jit(solution)/shard_map/pallas_call | solution.py:692
  79.1 3.9 %collective-permute-start.11 = (f32[10,40,128]{2,1,0:T(8,128)}, f32[10,40,128]{2,1,0:T(8,128)}, u32[]{:S(2)}, u32[]{:S(2)}) collective-permute-start(f32[10,40,128]{2,1,0:T(8,128)} %get-tuple-element.61), channel_id=1, source_target_pairs={{4,0},{8,4},{12,8},{16,12},{20,16},{24,20},{28,24},{32,28},{36,32}... | collective-permute-start | bytes 614408 | tf_op jit(solution)/shard_map/ppermute | solution.py:170
  83.0 6.0 %shard_map.150 = (f32[7,32,128]{2,1,0:T(8,128)S(1)}, f32[64,1,512]{2,1,0:T(1,128)S(1)}) custom-call(f32[4,4,40,128]{3,2,1,0:T(8,128)S(1)} %get-tuple-element.53.R, s32[64,512]{1,0:T(8,128)S(1)} %bitcast_select_fusion.index, f32[10,24,40,128]{3,2,1,0:T(8,128)S(1)} %get-tuple-element.56.F), custom_call_target="tpu_custom_call" | custom-call | tf_op jit(solution)/shard_map/pallas_call | solution.py:697
  90.3 4.2 %all-to-all-start.1 = ((f32[64,1,512]{2,1,0:T(1,128)}), f32[64,1,512]{2,1,0:T(1,128)S(1)}, u32[]{:S(2)}, u32[]{:S(2)}) async-start(f32[64,1,512]{2,1,0:T(1,128)} %copy-done.19), calls=%async_computation.1 | async-start | bytes 262144 | tf_op jit(solution)/shard_map/all_to_all | solution.py:179
  94.5 2.2 %multiply_reduce_fusion.current = f32[16,16,128]{2,1,0:T(8,128)S(1)} fusion(bf16[12,16,16,128]{3,2,1,0:T(8,128)(2,1)} %param.12, f32[12]{0:T(128)} %get-tuple-element.66, f32[12]{0:T(128)} %get-tuple-element.67, f32[12]{0:T(128)} %get-tuple-element.64, f32[12]{0:T(128)} %get-tuple-element.65, f32[16,16,128]{2,1,0:T(8,128)S(1)} %copy-done.3, f32[12]{0:T(128)} %get-tuple-element.63), kind=kLoop, calls=%fused_computation | loop fusion | flops 5079040 | bytes 1048816 | tf_op jit(solution)/shard_map/reduce_sum | solution.py:612
  96.8 1.0 copy-done.6
  97.7 0.7 copy-done.27
  98.4 3.4 %shard_map.143 = (f32[16,16,128]{2,1,0:T(8,128)S(1)}, f32[16,16,128]{2,1,0:T(8,128)}) custom-call(s32[5]{0:T(128)S(1)} %copy-done.27, f32[16,16,128]{2,1,0:T(8,128)S(1)} %multiply_reduce_fusion.current, f32[4,16,24,128]{3,2,1,0:T(8,128)S(1)} %get-tuple-element.39.heart.E, f32[10,24,128]{2,1,0:T(8,128)S(1)} %copy-done.14, f32[10,64,128]{2,1,0:T(8,128)S(1)} %copy-done.6), custom_call_target="tpu_custom_call" | custom-call | tf_op jit(solution)/shard_map/pallas_call | solution.py:668
  101.8 0.7 copy-done.20
  102.5 2.4 %shard_map.152 = f32[16,32,128]{2,1,0:T(8,128)} custom-call(f32[7,32,128]{2,1,0:T(8,128)S(1)} %copy-done.23, f32[6,32,128]{2,1,0:T(8,128)S(1)} %copy-done.25, f32[10,40,128]{2,1,0:T(8,128)} %collective-permute-done.11.rxr, f32[10,11,40,128]{3,2,1,0:T(8,128)S(1)} %get-tuple-element.62.G), custom_call_target="tpu_custom_call" | custom-call | tf_op jit(solution)/shard_map/pallas_call | solution.py:703
  104.9 4.2 %shard_map.151 = f32[16,16,128]{2,1,0:T(8,128)} custom-call(s32[5]{0:T(128)S(1)} %copy-done.28, f32[64,1,512]{2,1,0:T(1,128)} %shard_map.144.sent, f32[64,1,512]{2,1,0:T(1,128)S(1)} %all-to-all-done.1.back, s32[64,512]{1,0:T(8,128)S(1)} %bitcast_select_fusion.1.index, f32[16,16,128]{2,1,0:T(8,128)S(1)} %copy-done.21), custom_call_target="tpu_custom_call" | custom-call | tf_op jit(solution)/shard_map/pallas_call | solution.py:707
  (69 shorter events, 4.2 us)
Async XLA Ops:
  0.6 24.8 %copy-start.3 = (f32[16,16,128]{2,1,0:T(8,128)S(1)}, f32[16,16,128]{2,1,0:T(8,128)}, u32[]{:S(2)}) copy-start(f32[16,16,128]{2,1,0:T(8,128)} %f0.2) | copy-start | bytes 393220
  0.6 24.8 %copy-start.10 = (f32[16,16,128]{2,1,0:T(8,128)S(1)}, f32[16,16,128]{2,1,0:T(8,128)}, u32[]{:S(2)}) copy-start(f32[16,16,128]{2,1,0:T(8,128)} %f1.1) | copy-start | bytes 393220
  0.7 30.0 %copy-start.33 = (s32[1,1,1,64]{3,2,1,0:T(1,128)S(1)}, s32[1,1,1,64]{3,2,1,0:T(1,128)}, u32[]{:S(2)}) copy-start(s32[1,1,1,64]{3,2,1,0:T(1,128)} %param.21) | copy-start | bytes 772
  0.7 30.0 %copy-start.30 = (s32[1,1,1,64,512]{4,3,2,1,0:T(8,128)S(1)}, s32[1,1,1,64,512]{4,3,2,1,0:T(8,128)}, u32[]{:S(2)}) copy-start(s32[1,1,1,64,512]{4,3,2,1,0:T(8,128)} %param.20) | copy-start | bytes 393220
  2.9 8.3 %collective-permute-start = (f32[8,768]{1,0:T(8,128)}, f32[8,768]{1,0:T(8,128)S(1)}, u32[]{:S(2)}, u32[]{:S(2)}) collective-permute-start(f32[8,768]{1,0:T(8,128)} %get-tuple-element.33), channel_id=1, source_target_pairs={{0,64},{64,128},{128,192},{192,0},{1,65},{65,129},{129,193},{193,1... | collective-permute-start | bytes 73736 | tf_op jit(solution)/shard_map/ppermute | solution.py:175
  6.7 5.6 %collective-permute-start.1 = (f32[8,768]{1,0:T(8,128)}, f32[8,768]{1,0:T(8,128)S(1)}, u32[]{:S(2)}, u32[]{:S(2)}) collective-permute-start(f32[8,768]{1,0:T(8,128)} %get-tuple-element.34), channel_id=1, source_target_pairs={{64,0},{128,64},{192,128},{0,192},{65,1},{129,65},{193,129},{1,193... | collective-permute-start | bytes 73736 | tf_op jit(solution)/shard_map/ppermute | solution.py:170
  9.8 68.0 %copy-start.26 = (s32[5]{0:T(128)}, s32[5]{0:T(128)S(1)}, u32[]{:S(2)}) copy-start(s32[5]{0:T(128)S(1)} %stack.11.place) | copy-start | bytes 64
  12.3 1.0 copy-start
  13.3 0.9 copy-start.2
  14.2 0.9 copy-start.9
  15.1 0.9 copy-start.11
  16.0 0.9 copy-start.12
  17.0 0.7 copy-start.29
  17.6 28.8 %copy-start.1 = (f32[16,32,128]{2,1,0:T(8,128)S(1)}, f32[16,32,128]{2,1,0:T(8,128)}, u32[]{:S(2)}) copy-start(f32[16,32,128]{2,1,0:T(8,128)} %f0.3) | copy-start | bytes 786436
  18.9 0.7 copy-start.15
  19.6 0.7 copy-start.17
  20.3 5.1 %collective-permute-start.2 = (f32[34,8,128]{2,1,0:T(8,128)S(1)}, f32[34,8,128]{2,1,0:T(8,128)S(1)}, u32[]{:S(2)}, u32[]{:S(2)}) collective-permute-start(f32[34,8,128]{2,1,0:T(8,128)S(1)} %get-tuple-element.37), channel_id=1, source_target_pairs={{0,1},{1,2},{2,3},{3,0},{4,5},{5,6},{6,7},{7,4},{8,9},{9,10},{10,1... | collective-permute-start | bytes 417800 | tf_op jit(solution)/shard_map/ppermute | solution.py:175
  21.5 3.9 %collective-permute-start.3 = (f32[34,8,128]{2,1,0:T(8,128)S(1)}, f32[34,8,128]{2,1,0:T(8,128)S(1)}, u32[]{:S(2)}, u32[]{:S(2)}) collective-permute-start(f32[34,8,128]{2,1,0:T(8,128)S(1)} %get-tuple-element.38), channel_id=1, source_target_pairs={{1,0},{2,1},{3,2},{0,3},{5,4},{6,5},{7,6},{4,7},{9,8},{10,9},{11,1... | collective-permute-start | bytes 417800 | tf_op jit(solution)/shard_map/ppermute | solution.py:170
  26.2 6.4 %collective-permute-start.4 = (f32[10,24,128]{2,1,0:T(8,128)S(1)}, f32[10,24,128]{2,1,0:T(8,128)S(1)}, u32[]{:S(2)}, u32[]{:S(2)}) collective-permute-start(f32[10,24,128]{2,1,0:T(8,128)S(1)} %get-tuple-element.40), channel_id=1, source_target_pairs={{0,4},{4,8},{8,12},{12,16},{16,20},{20,24},{24,28},{28,32},{32,36}... | collective-permute-start | bytes 368648 | tf_op jit(solution)/shard_map/ppermute | solution.py:175
  32.5 18.1 %copy-start.31 = (s32[1,1,1,64,512]{4,3,2,1,0:T(8,128)S(1)}, s32[1,1,1,64,512]{4,3,2,1,0:T(8,128)}, u32[]{:S(2)}) copy-start(s32[1,1,1,64,512]{4,3,2,1,0:T(8,128)} %param.22) | copy-start | bytes 393220
  32.5 18.1 %copy-start.34 = (s32[1,1,1,64]{3,2,1,0:T(1,128)S(1)}, s32[1,1,1,64]{3,2,1,0:T(1,128)}, u32[]{:S(2)}) copy-start(s32[1,1,1,64]{3,2,1,0:T(1,128)} %param.23) | copy-start | bytes 772
  36.6 0.6 copy-start.13
  37.2 17.7 %all-to-all-start = ((f32[64,1,512]{2,1,0:T(1,128)}), f32[64,1,512]{2,1,0:T(1,128)S(1)}, u32[]{:S(2)}, u32[]{:S(2)}) async-start(f32[64,1,512]{2,1,0:T(1,128)} %shard_map.144.sent), calls=%async_computation | async-start | bytes 262144 | tf_op jit(solution)/shard_map/all_to_all | solution.py:179
  46.4 24.1 %copy-start.32 = (f32[5,12]{1,0:T(8,128)S(1)}, f32[5,12]{1,0:T(8,128)}, u32[]{:S(2)}) copy-start(f32[5,12]{1,0:T(8,128)} %param.15) | copy-start | bytes 724
  46.4 1.0 copy-start.16
  47.4 0.9 copy-start.18
  49.1 1.1 %copy-start.7 = (f32[4,16,40,128]{3,2,1,0:T(8,128)}, f32[4,16,40,128]{3,2,1,0:T(8,128)S(1)}, u32[]{:S(2)}) copy-start(f32[4,16,40,128]{3,2,1,0:T(8,128)S(1)} %get-tuple-element.54.E) | copy-start | bytes 3932164
  50.2 20.9 %collective-permute-start.5 = (f32[10,64,128]{2,1,0:T(8,128)S(1)}, f32[10,64,128]{2,1,0:T(8,128)S(1)}, u32[]{:S(2)}, u32[]{:S(2)}) collective-permute-start(f32[10,64,128]{2,1,0:T(8,128)S(1)} %get-tuple-element.44), channel_id=1, source_target_pairs={{4,0},{8,4},{12,8},{16,12},{20,16},{24,20},{28,24},{32,28},{36,32}... | collective-permute-start | bytes 983048 | tf_op jit(solution)/shard_map/ppermute | solution.py:170
  59.5 4.9 %collective-permute-start.6 = (f32[8,128]{1,0:T(8,128)S(1)}, f32[8,128]{1,0:T(8,128)S(1)}, u32[]{:S(2)}, u32[]{:S(2)}) collective-permute-start(f32[8,128]{1,0:T(8,128)S(1)} %get-tuple-element.47), channel_id=1, source_target_pairs={{0,64},{64,128},{128,192},{192,0},{1,65},{65,129},{129,193},{193,1... | collective-permute-start | bytes 12296 | tf_op jit(solution)/shard_map/ppermute | solution.py:175
  63.4 3.5 %collective-permute-start.7 = (f32[8,128]{1,0:T(8,128)S(1)}, f32[8,128]{1,0:T(8,128)S(1)}, u32[]{:S(2)}, u32[]{:S(2)}) collective-permute-start(f32[8,128]{1,0:T(8,128)S(1)} %get-tuple-element.48), channel_id=1, source_target_pairs={{64,0},{128,64},{192,128},{0,192},{65,1},{129,65},{193,129},{1,193... | collective-permute-start | bytes 12296 | tf_op jit(solution)/shard_map/ppermute | solution.py:170
  63.4 7.7 %collective-permute-start.10 = (f32[10,40,128]{2,1,0:T(8,128)S(1)}, f32[10,40,128]{2,1,0:T(8,128)S(1)}, u32[]{:S(2)}, u32[]{:S(2)}) collective-permute-start(f32[10,40,128]{2,1,0:T(8,128)S(1)} %get-tuple-element.55), channel_id=1, source_target_pairs={{0,4},{4,8},{8,12},{12,16},{16,20},{20,24},{24,28},{28,32},{32,36}... | collective-permute-start | bytes 614408 | tf_op jit(solution)/shard_map/ppermute | solution.py:175
  67.8 9.9 %collective-permute-start.8 = (f32[5,8,128]{2,1,0:T(8,128)S(1)}, f32[5,8,128]{2,1,0:T(8,128)S(1)}, u32[]{:S(2)}, u32[]{:S(2)}) collective-permute-start(f32[5,8,128]{2,1,0:T(8,128)S(1)} %get-tuple-element.51), channel_id=1, source_target_pairs={{0,1},{1,2},{2,3},{3,0},{4,5},{5,6},{6,7},{7,4},{8,9},{9,10},{10,1... | collective-permute-start | bytes 61448 | tf_op jit(solution)/shard_map/ppermute | solution.py:175
  67.9 9.8 %collective-permute-start.9 = (f32[5,8,128]{2,1,0:T(8,128)S(1)}, f32[5,8,128]{2,1,0:T(8,128)S(1)}, u32[]{:S(2)}, u32[]{:S(2)}) collective-permute-start(f32[5,8,128]{2,1,0:T(8,128)S(1)} %get-tuple-element.52), channel_id=1, source_target_pairs={{1,0},{2,1},{3,2},{0,3},{5,4},{6,5},{7,6},{4,7},{9,8},{10,9},{11,1... | collective-permute-start | bytes 61448 | tf_op jit(solution)/shard_map/ppermute | solution.py:170
  71.1 0.7 copy-start.4
  71.8 1.0 copy-start.5
  72.8 1.3 %copy-start.8 = (f32[4,16,40,128]{3,2,1,0:T(8,128)S(1)}, f32[4,16,40,128]{3,2,1,0:T(8,128)}, u32[]{:S(2)}) copy-start(f32[4,16,40,128]{3,2,1,0:T(8,128)} %copy-done.7) | copy-start | bytes 3932164
  77.7 11.3 %copy-start.24 = (f32[6,32,128]{2,1,0:T(8,128)}, f32[6,32,128]{2,1,0:T(8,128)S(1)}, u32[]{:S(2)}) copy-start(f32[6,32,128]{2,1,0:T(8,128)S(1)} %get-tuple-element.60.middle) | copy-start | bytes 294916
  79.1 23.4 %collective-permute-start.11 = (f32[10,40,128]{2,1,0:T(8,128)}, f32[10,40,128]{2,1,0:T(8,128)}, u32[]{:S(2)}, u32[]{:S(2)}) collective-permute-start(f32[10,40,128]{2,1,0:T(8,128)} %get-tuple-element.61), channel_id=1, source_target_pairs={{4,0},{8,4},{12,8},{16,12},{20,16},{24,20},{28,24},{32,28},{36,32}... | collective-permute-start | bytes 614408 | tf_op jit(solution)/shard_map/ppermute | solution.py:170
  83.0 13.7 %copy-start.14 = (f32[10,24,128]{2,1,0:T(8,128)S(1)}, f32[10,24,128]{2,1,0:T(8,128)}, u32[]{:S(2)}) copy-start(f32[10,24,128]{2,1,0:T(8,128)} %copy-done.13) | copy-start | bytes 368644
  89.0 0.7 copy-start.19
  90.3 14.6 %all-to-all-start.1 = ((f32[64,1,512]{2,1,0:T(1,128)}), f32[64,1,512]{2,1,0:T(1,128)S(1)}, u32[]{:S(2)}, u32[]{:S(2)}) async-start(f32[64,1,512]{2,1,0:T(1,128)} %copy-done.19), calls=%async_computation.1 | async-start | bytes 262144 | tf_op jit(solution)/shard_map/all_to_all | solution.py:179
  94.5 8.0 %copy-start.23 = (f32[7,32,128]{2,1,0:T(8,128)S(1)}, f32[7,32,128]{2,1,0:T(8,128)}, u32[]{:S(2)}) copy-start(f32[7,32,128]{2,1,0:T(8,128)} %copy-done.22) | copy-start | bytes 344068
  94.5 8.0 %copy-start.25 = (f32[6,32,128]{2,1,0:T(8,128)S(1)}, f32[6,32,128]{2,1,0:T(8,128)}, u32[]{:S(2)}) copy-start(f32[6,32,128]{2,1,0:T(8,128)} %copy-done.24) | copy-start | bytes 294916
  96.8 1.0 copy-start.6
  97.7 0.7 copy-start.27
  101.8 0.7 copy-start.20
  102.5 2.4 %copy-start.28 = (s32[5]{0:T(128)S(1)}, s32[5]{0:T(128)}, u32[]{:S(2)}) copy-start(s32[5]{0:T(128)} %copy-done.26) | copy-start | bytes 64
  102.5 2.4 %copy-start.21 = (f32[16,16,128]{2,1,0:T(8,128)S(1)}, f32[16,16,128]{2,1,0:T(8,128)}, u32[]{:S(2)}) copy-start(f32[16,16,128]{2,1,0:T(8,128)} %copy-done.20) | copy-start | bytes 393220
  (1 other events, 0.6 us)
